TPU v7x, 32 devices: a whole 2x2x4 slice. The times are simulated.
32 devices in a mesh: dp: 8 (over y, x, core), mp: 4 (over z).
Axes of the slice: x: 2, y: 2, z: 4, core: 2. Of those that a mesh axis runs over, the one named last changes fastest.
Arguments:
- activations: bfloat16 [16384, 1024], P('dp'), may hold values from -6 to 6
- cotangent: bfloat16 [16384, 1024], P('dp'), may hold values from -6 to 6
- level_table: bfloat16 [1024, 1024], P('dp'), may hold values from -6 to 6
- true_frames: int32 [16], P('dp'), may hold values from 4 to 16
- group_pattern: int32 [16], P('dp'), may hold values from 0 to 3
- noise_levels: int32 [4, 16], replicated, may hold values from 1 to 1023
- context_flags: int32 [16, 16], P('dp'), may hold values 0 or 1
- owner_list: int32 [288], replicated, may hold values from 0 to 287, as said below
- masters: float32 [4, 288, 128, 128], P('mp', 'dp')
- moment_one: float32 [4, 288, 128, 128], P('mp', 'dp')
- moment_two: float32 [4, 288, 128, 128], P('mp', 'dp')
- basis_left: float32 [4, 288, 128, 128], P('mp', 'dp'), as said below
- basis_right: float32 [4, 288, 128, 128], P('mp', 'dp'), as said below
Outputs:
- block_output: bfloat16 [16384, 1024], P('dp')
- input_grad: float32 [16384, 1024], P('dp')
- table_grad: float32 [1024, 1024], P(('dp', 'mp'))
- new_masters: float32 [4, 288, 128, 128], P('mp', 'dp')
- new_moment_one: float32 [4, 288, 128, 128], P('mp', 'dp')
- new_moment_two: float32 [4, 288, 128, 128], P('mp', 'dp')
- new_weights: bfloat16 [4, 288, 128, 128], P('mp', 'dp')
Inputs may be any that keep to these rules, and one draw needn't show every extreme that they name: `owner_list`: each tile number appears once; position p belongs to the dp index p // 36. `basis_left`: every tile is an orthogonal matrix. `basis_right`: every tile is an orthogonal matrix.
All inputs are finite; a program needn't handle non-finite values. No bound on the sum of `context_flags` on one device may be relied on, other than what follows from the above.
Results may differ from a plain program's by a relative error of at most 0.02.
Values may be sent and summed in bfloat16 or wider, within the bound.
A program may use at most 256 MiB of HBM per device.

v0:
```python
import jax
import jax.numpy as jnp
from jax import lax
from jax.sharding import PartitionSpec as P

D = 1024
H = 16
HD = 64
FF = 4096
FRAMES = 16
FRAME_TOK = 64
LEVELS = 1024
PATTERNS = 4
TILE = 128


HIGHEST = lax.Precision.HIGHEST
EPS_NORM = 1e-06
BETA_ONE = 0.5
BETA_TWO = 0.75
EPS_ADAM = 1e-08
DECAY = 0.01


def tile_layout(model_width, heads, head_dim, hidden, groups, tile_size):
    local_width = heads // groups * head_dim
    shapes = [
        (model_width, 3 * local_width),
        (local_width, model_width),
        (model_width, hidden // groups),
        (hidden // groups, model_width),
        (model_width, 6 * model_width // groups),
    ]
    counts = [height // tile_size * (breadth // tile_size) for height, breadth in shapes]
    return (shapes, counts)


def unpack(tile_stack, shapes, counts, tile_size):
    matrices = []
    offset = 0
    for (height, breadth), amount in zip(shapes, counts):
        stacked = tile_stack[offset : offset + amount].reshape(
            height // tile_size, breadth // tile_size, tile_size, tile_size
        )
        matrices.append(stacked.transpose(0, 2, 1, 3).reshape(height, breadth))
        offset = offset + amount
    return matrices


def pack(matrices, tile_size):
    stacked = []
    for matrix in matrices:
        height, breadth = matrix.shape
        stacked.append(
            matrix.reshape(height // tile_size, tile_size, breadth // tile_size, tile_size)
            .transpose(0, 2, 1, 3)
            .reshape(-1, tile_size, tile_size)
        )
    return jnp.concatenate(stacked, axis=0)


def kind_rates(tile_ids, counts):
    scales = [
        0.35 * D ** (-0.5),
        1.5 * (H * HD) ** (-0.5),
        0.5 * D ** (-0.5),
        0.5 * FF ** (-0.5),
        0.5 * D ** (-0.5),
    ]
    tile_rates = jnp.full(tile_ids.shape, scales[0], jnp.float32)
    boundary = 0
    for category in range(1, 5):
        boundary = boundary + counts[category - 1]
        tile_rates = jnp.where(tile_ids >= boundary, jnp.float32(scales[category]), tile_rates)
    return tile_rates


def layer_norm(stream):
    centered = stream - jnp.mean(stream, axis=-1, keepdims=True)
    inverse_std = lax.rsqrt(jnp.mean(centered * centered, axis=-1, keepdims=True) + EPS_NORM)
    return (centered * inverse_std, inverse_std)


def norm_back(grad_normed, normed, inverse_std):
    centered_grad = grad_normed - jnp.mean(grad_normed, axis=-1, keepdims=True)
    return inverse_std * (
        centered_grad - normed * jnp.mean(grad_normed * normed, axis=-1, keepdims=True)
    )


def gelu_tanh(values):
    return jax.nn.gelu(values, approximate=True)


def gelu_back(values, incoming):
    _, pullback = jax.vjp(gelu_tanh, values)
    return pullback(incoming)[0]


def contract_rows(left_side, right_side):
    return lax.dot_general(
        left_side, right_side, (((0,), (0,)), ((), ())), preferred_element_type=jnp.float32
    )


def contract_cols(left_side, right_side):
    return lax.dot_general(
        left_side, right_side, (((1,), (1,)), ((), ())), preferred_element_type=jnp.float32
    )


def block_scores(queries, key_all, mask_rows, score_scale):
    scores = (
        jnp.einsum("cqhd,ckhd->chqk", queries, key_all, preferred_element_type=jnp.float32)
        * score_scale
    )
    return jnp.where(mask_rows[:, None], scores, -1e30)


def attend_block(queries, key_all, value_all, mask_rows, score_scale):
    scores = block_scores(queries, key_all, mask_rows, score_scale)
    row_peak = jnp.max(scores, axis=-1, keepdims=True)
    exp_scores = jnp.exp(scores - row_peak)
    row_total = jnp.sum(exp_scores, axis=-1, keepdims=True)
    soft_rows = (exp_scores / row_total).astype(jnp.bfloat16)
    attended = jnp.einsum(
        "chqk,ckhd->cqhd", soft_rows, value_all, preferred_element_type=jnp.float32
    )
    return (attended, row_peak + jnp.log(row_total))


def attend_back(queries, key_all, value_all, mask_rows, log_total, grad_rows, score_scale):
    scores = block_scores(queries, key_all, mask_rows, score_scale)
    soft_rows = jnp.exp(scores - log_total)
    grad_soft = jnp.einsum(
        "cqhd,ckhd->chqk", grad_rows, value_all, preferred_element_type=jnp.float32
    )
    row_delta = jnp.sum(soft_rows * grad_soft, axis=-1, keepdims=True)
    grad_scores = (soft_rows * (grad_soft - row_delta)).astype(jnp.bfloat16)
    grad_query = (
        jnp.einsum("chqk,ckhd->cqhd", grad_scores, key_all, preferred_element_type=jnp.float32)
        * score_scale
    )
    grad_key = (
        jnp.einsum("chqk,cqhd->ckhd", grad_scores, queries, preferred_element_type=jnp.float32)
        * score_scale
    )
    grad_value = jnp.einsum(
        "chqk,cqhd->ckhd",
        soft_rows.astype(jnp.bfloat16),
        grad_rows,
        preferred_element_type=jnp.float32,
    )
    return (grad_query, grad_key, grad_value)


def body(
    activations,
    cotangent,
    level_table,
    true_frames,
    group_pattern,
    noise_levels,
    context_flags,
    owner_list,
    masters,
    moment_one,
    moment_two,
    basis_left,
    basis_right,
):
    groups = lax.axis_size("mp")
    member = lax.axis_index("mp")
    owner_rank = lax.axis_index("dp")
    shapes, counts = tile_layout(D, H, HD, FF, groups, TILE)
    slot_count = masters.shape[1]
    clip_count = true_frames.shape[0]
    frame_rows = clip_count * FRAMES
    tok_rows = activations.shape[0]
    clip_len = FRAMES * FRAME_TOK
    score_scale = HD ** (-0.5)
    inverse = jnp.argsort(owner_list)
    gathered, level_rows = (
        lax.all_gather(masters.astype(jnp.bfloat16), "dp", axis=1, tiled=True),
        lax.all_gather(level_table, "dp", axis=0, tiled=True),
    )
    w_qkv, w_out, w_up, w_down, w_mod = unpack(
        jnp.take(gathered[0], inverse, axis=0), shapes, counts, TILE
    )
    local_width = w_out.shape[0]
    heads_here = local_width // HD
    frame_index = jnp.arange(FRAMES, dtype=jnp.int32)
    valid_frame = frame_index[None, :] < true_frames[:, None]
    flagged = context_flags == 1
    in_context = flagged & valid_frame
    visible = valid_frame[:, None, :] & (
        jnp.logical_not(in_context)[:, :, None] | in_context[:, None, :]
    )
    pattern_hot = (group_pattern[:, None] == jnp.arange(PATTERNS, dtype=jnp.int32)[None, :]).astype(
        jnp.int32
    )
    pattern_levels = jnp.sum(pattern_hot[:, :, None] * noise_levels[None, :, :], axis=1)
    levels = jnp.where(flagged, 0, pattern_levels)
    level_hot = (
        levels.reshape(-1)[:, None] == jnp.arange(LEVELS, dtype=jnp.int32)[None, :]
    ).astype(jnp.bfloat16)
    embedded = jnp.dot(level_hot, level_rows, preferred_element_type=jnp.float32).astype(
        jnp.bfloat16
    )
    mod_part = jnp.dot(embedded, w_mod, preferred_element_type=jnp.float32)
    mod_all = lax.all_gather(mod_part, "mp", axis=1, tiled=True)
    modulation = (
        mod_all.reshape(frame_rows, groups, 6, D // groups)
        .transpose(0, 2, 1, 3)
        .reshape(frame_rows, 6, D)
    )
    token_mask = jnp.repeat(jnp.repeat(visible, FRAME_TOK, axis=1), FRAME_TOK, axis=2)
    stream = activations.astype(jnp.float32).reshape(frame_rows, FRAME_TOK, D)
    normed_one, inverse_one = layer_norm(stream)
    hidden_one = (
        (normed_one * (1.0 + modulation[:, 1, None, :]) + modulation[:, 0, None, :])
        .astype(jnp.bfloat16)
        .reshape(tok_rows, D)
    )
    qkv_rows = jnp.dot(hidden_one, w_qkv, preferred_element_type=jnp.float32).astype(jnp.bfloat16)
    queries = qkv_rows[:, :local_width].reshape(clip_count, clip_len, heads_here, HD)
    key_rows = qkv_rows[:, local_width : 2 * local_width].reshape(
        clip_count, clip_len, heads_here, HD
    )
    value_rows = qkv_rows[:, 2 * local_width :].reshape(clip_count, clip_len, heads_here, HD)
    block_rows = min(512, clip_len)
    block_total = clip_len // block_rows
    attended_parts = []
    log_parts = []
    for block_id in range(block_total):
        first_row = block_id * block_rows
        attended_blk, log_blk = attend_block(
            queries[:, first_row : first_row + block_rows],
            key_rows,
            value_rows,
            token_mask[:, first_row : first_row + block_rows],
            score_scale,
        )
        attended_parts.append(attended_blk)
        log_parts.append(log_blk)
    attended = (
        jnp.concatenate(attended_parts, axis=1).astype(jnp.bfloat16).reshape(tok_rows, local_width)
    )
    branch = (
        lax.psum(
            jnp.dot(attended, w_out, preferred_element_type=jnp.float32).astype(jnp.bfloat16), "mp"
        )
        .astype(jnp.float32)
        .reshape(frame_rows, FRAME_TOK, D)
    )
    middle = stream + modulation[:, 2, None, :] * branch
    normed_two, inverse_two = layer_norm(middle)
    hidden_two = (
        (normed_two * (1.0 + modulation[:, 4, None, :]) + modulation[:, 3, None, :])
        .astype(jnp.bfloat16)
        .reshape(tok_rows, D)
    )
    pre_act = jnp.dot(hidden_two, w_up, preferred_element_type=jnp.float32)
    activated = gelu_tanh(pre_act).astype(jnp.bfloat16)
    feed_out = (
        lax.psum(
            jnp.dot(activated, w_down, preferred_element_type=jnp.float32).astype(jnp.bfloat16),
            "mp",
        )
        .astype(jnp.float32)
        .reshape(frame_rows, FRAME_TOK, D)
    )
    result = middle + modulation[:, 5, None, :] * feed_out
    block_output = result.reshape(tok_rows, D).astype(jnp.bfloat16)
    regathered = lax.all_gather(masters.astype(jnp.bfloat16), "dp", axis=1, tiled=True)
    back_qkv, back_out, back_up, back_down, back_mod = unpack(
        jnp.take(regathered[0], inverse, axis=0), shapes, counts, TILE
    )
    grad_out = cotangent.astype(jnp.float32).reshape(frame_rows, FRAME_TOK, D)
    grad_feed = (modulation[:, 5, None, :] * grad_out).astype(jnp.bfloat16).reshape(tok_rows, D)
    grad_down = contract_rows(activated, grad_feed)
    grad_act = contract_cols(grad_feed, back_down).astype(jnp.bfloat16)
    grad_pre = gelu_back(pre_act, grad_act.astype(jnp.float32)).astype(jnp.bfloat16)
    grad_up = contract_rows(hidden_two, grad_pre)
    grad_gate_two = jnp.sum(grad_out * feed_out, axis=1)
    grad_hidden_two = (
        lax.psum(contract_cols(grad_pre, back_up).astype(jnp.bfloat16), "mp")
        .astype(jnp.float32)
        .reshape(frame_rows, FRAME_TOK, D)
    )
    grad_shift_two = jnp.sum(grad_hidden_two, axis=1)
    grad_scale_two = jnp.sum(grad_hidden_two * normed_two, axis=1)
    grad_middle = grad_out + norm_back(
        grad_hidden_two * (1.0 + modulation[:, 4, None, :]), normed_two, inverse_two
    )
    grad_gate_one = jnp.sum(grad_middle * branch, axis=1)
    grad_branch = (
        (modulation[:, 2, None, :] * grad_middle).astype(jnp.bfloat16).reshape(tok_rows, D)
    )
    grad_out_proj = contract_rows(attended, grad_branch)
    grad_attended = (
        contract_cols(grad_branch, back_out)
        .astype(jnp.bfloat16)
        .reshape(clip_count, clip_len, heads_here, HD)
    )
    query_parts = []
    grad_key = jnp.zeros((clip_count, clip_len, heads_here, HD), jnp.float32)
    grad_value = jnp.zeros((clip_count, clip_len, heads_here, HD), jnp.float32)
    for block_id in range(block_total):
        first_row = block_id * block_rows
        grad_query_blk, grad_key_blk, grad_value_blk = attend_back(
            queries[:, first_row : first_row + block_rows],
            key_rows,
            value_rows,
            token_mask[:, first_row : first_row + block_rows],
            log_parts[block_id],
            grad_attended[:, first_row : first_row + block_rows],
            score_scale,
        )
        query_parts.append(grad_query_blk)
        grad_key = grad_key + grad_key_blk
        grad_value = grad_value + grad_value_blk
    grad_query = jnp.concatenate(query_parts, axis=1)
    grad_qkv = jnp.concatenate(
        [
            grad_query.astype(jnp.bfloat16).reshape(tok_rows, local_width),
            grad_key.astype(jnp.bfloat16).reshape(tok_rows, local_width),
            grad_value.astype(jnp.bfloat16).reshape(tok_rows, local_width),
        ],
        axis=1,
    )
    grad_w_qkv = contract_rows(hidden_one, grad_qkv)
    grad_hidden_one = (
        lax.psum(contract_cols(grad_qkv, back_qkv).astype(jnp.bfloat16), "mp")
        .astype(jnp.float32)
        .reshape(frame_rows, FRAME_TOK, D)
    )
    grad_shift_one = jnp.sum(grad_hidden_one, axis=1)
    grad_scale_one = jnp.sum(grad_hidden_one * normed_one, axis=1)
    input_grad = (
        grad_middle
        + norm_back(grad_hidden_one * (1.0 + modulation[:, 1, None, :]), normed_one, inverse_one)
    ).reshape(tok_rows, D)
    grad_mod = jnp.stack(
        [
            grad_shift_one,
            grad_scale_one,
            grad_gate_one,
            grad_shift_two,
            grad_scale_two,
            grad_gate_two,
        ],
        axis=1,
    )
    grad_mod_own = lax.dynamic_index_in_dim(
        grad_mod.reshape(frame_rows, 6, groups, D // groups), member, axis=2, keepdims=False
    )
    grad_mod_own = grad_mod_own.reshape(frame_rows, 6 * D // groups).astype(jnp.bfloat16)
    grad_w_mod = contract_rows(embedded, grad_mod_own)
    grad_embedded = contract_cols(grad_mod_own, back_mod)
    table_term = lax.dot_general(
        level_hot.astype(jnp.float32),
        grad_embedded,
        (((0,), (0,)), ((), ())),
        precision=HIGHEST,
        preferred_element_type=jnp.float32,
    )
    table_grad = lax.psum_scatter(table_term, ("dp", "mp"), scatter_dimension=0, tiled=True)
    packed = pack([grad_w_qkv, grad_out_proj, grad_up, grad_down, grad_w_mod], TILE)
    owned = jnp.take(packed, owner_list, axis=0)
    reduced = lax.psum_scatter(
        owned[None].astype(jnp.bfloat16), "dp", scatter_dimension=1, tiled=True
    ).astype(jnp.float32)[0]
    tile_ids = lax.dynamic_slice_in_dim(owner_list, owner_rank * slot_count, slot_count)
    rotated = jnp.einsum("pji,pjk->pik", basis_left[0], reduced, precision=HIGHEST)
    rotated = jnp.einsum("pik,pkl->pil", rotated, basis_right[0], precision=HIGHEST)
    new_one = BETA_ONE * moment_one[0] + (1.0 - BETA_ONE) * rotated
    new_two = BETA_TWO * moment_two[0] + (1.0 - BETA_TWO) * rotated * rotated
    direction = new_one / (jnp.sqrt(new_two) + EPS_ADAM)
    turned = jnp.einsum("pij,pjk->pik", basis_left[0], direction, precision=HIGHEST)
    turned = jnp.einsum("pik,plk->pil", turned, basis_right[0], precision=HIGHEST)
    tile_rates = kind_rates(tile_ids, counts)
    new_masters = masters[0] - tile_rates[:, None, None] * (turned + DECAY * masters[0])
    return (
        block_output,
        input_grad,
        table_grad,
        new_masters[None],
        new_one[None],
        new_two[None],
        new_masters[None].astype(jnp.bfloat16),
    )


def solution(mesh):
    in_specs = (
        P("dp", None),
        P("dp", None),
        P("dp", None),
        P("dp"),
        P("dp"),
        P(),
        P("dp", None),
        P(),
        P("mp", "dp", None, None),
        P("mp", "dp", None, None),
        P("mp", "dp", None, None),
        P("mp", "dp", None, None),
        P("mp", "dp", None, None),
    )
    out_specs = (
        P("dp", None),
        P("dp", None),
        P(("dp", "mp"), None),
        P("mp", "dp", None, None),
        P("mp", "dp", None, None),
        P("mp", "dp", None, None),
        P("mp", "dp", None, None),
    )
    return jax.shard_map(body, mesh=mesh, in_specs=in_specs, out_specs=out_specs, check_vma=False)
```

profile of v0, /device:TPU:1, one launch (start us, length us, event | category | flops | bytes accessed | tf_op | source)
XLA Modules:
  0.0 1281.1 jit_solution(2902918120802603525)
XLA Ops:
  32.7 8.6 all-gather.3.cloned.1.call-done
  43.5 59.1 %all-gather.5.cloned.1.call-done = bf16[1,288,128,128]{3,2,0,1:T(8,128)(2,1)} async-done(((bf16[1,36,128,128]{3,2,0,1:T(8,128)(2,1)}), bf16[1,288,128,128]{3,2,0,1:T(8,128)(2,1)}) %all-gather.5.cloned.1.call-update) | async-done | bytes 9437200 | tf_op jit(solution)/shard_map/all_gather | solution.py:184
  102.6 14.0 %gather_fusion.1 = bf16[288,128,128]{2,1,0:T(8,128)(2,1)} fusion(bf16[288,128,128]{2,1,0:T(8,128)(2,1)} %bitcast.414, s32[1024]{0:T(1024)S(1)} %pad_clamp_fusion.1), kind=kCustom, calls=%fused_computation.clone | custom fusion | bytes 18875520 | tf_op jit(solution)/shard_map/jit(_take)/gather | solution.py:188
  116.6 8.2 broadcast_select_fusion
  143.3 18.1 %all_gather.12 = f32[32,6144]{1,0:T(8,128)} all-gather(f32[32,1536]{1,0:T(8,128)S(1)} %fusion.68), channel_id=1, replica_groups=mesh['dp'=8,'mp'=4] {'mp'}, dimensions={1}, use_global_device_ids=true | all-gather | bytes 983040 | tf_op jit(solution)/shard_map/all_gather | solution.py:211
  251.6 138.8 %all-reduce.5.cloned.1.call-done = bf16[2048,1024]{1,0:T(8,128)(2,1)} async-done(((bf16[2048,1024]{1,0:T(8,128)(2,1)}), bf16[2048,1024]{1,0:T(8,128)(2,1)}) %all-reduce.5.cloned.1.call-update) | async-done | bytes 4194320 | tf_op jit(solution)/shard_map/psum | solution.py:250
  401.0 14.3 %fusion.40 = (bf16[1024,2048]{1,0:T(8,128)(2,1)}, bf16[1024,2048]{1,0:T(8,128)(2,1)}, f32[2048,1024]{0,1:T(8,128)S(1)}) fusion(bf16[2048,1024]{0,1:T(8,128)(2,1)} %convolution_convert_fusion.2, bf16[2048,1024]{1,0:T(8,128)(2,1)S(1)} %fusion.35, bf16[128,8,8,128]{3,2,1,0:T(8,128)(2,1)S(1)} %bitcast.439), kind=kOutput, calls=%fused_computation.70 | convolution fusion | flops 4343201792 | bytes 27262976 | tf_op jit(solution)/shard_map/dot_general | solution.py:263
  418.7 12.9 %fusion.63 = bf16[2048,1024]{1,0:T(8,128)(2,1)} fusion(f32[2048,1024]{0,1:T(8,128)S(1)} %get-tuple-element.58, bf16[2048,1024]{0,1:T(8,128)(2,1)} %convolution_convert_fusion.2, bf16[128,8,8,128]{3,2,1,0:T(8,128)(2,1)S(1)} %bitcast.440), kind=kOutput, calls=%fused_computation.107 | convolution fusion | flops 4341104640 | bytes 18874368 | tf_op jit(solution)/shard_map/dot_general | solution.py:107
  432.9 12.1 fusion.62
  445.1 140.7 %all-reduce.7.cloned.1.call-done = bf16[2048,1024]{1,0:T(8,128)(2,1)} async-done(((bf16[2048,1024]{1,0:T(8,128)(2,1)}), bf16[2048,1024]{1,0:T(8,128)(2,1)}) %all-reduce.7.cloned.1.call-update) | async-done | bytes 4194320 | tf_op jit(solution)/shard_map/psum | solution.py:287
  594.1 8.3 fusion.28
  615.7 14.2 %multiply_reduce_fusion.1 = (f32[2,4,512]{2,1,0:T(4,128)S(1)}, f32[2,4,512,1024]{3,2,1,0:T(8,128)}) fusion(f32[2,4,512,1024]{3,2,1,0:T(8,128)} %copy-done.5, f32[2,4,512]{2,1,0:T(4,128)} %bitcast.454, bf16[2,512,4,64]{1,3,2,0:T(8,128)(2,1)} %copy.253, bf16[2,1024,4,64]{1,3,2,0:T(8,128)(2,1)} %copy.198), kind=kOutput, calls=%fused_computation.8 | convolution fusion | flops 549449728 | bytes 35160064 | tf_op jit(solution)/shard_map/cqhd,ckhd->chqk/dot_general | solution.py:135
  632.6 10.3 multiply_convert_fusion.1
  662.1 13.7 %multiply_reduce_fusion = (f32[2,4,512]{2,1,0:T(4,128)S(1)}, f32[2,4,512,1024]{3,2,1,0:T(8,128)}) fusion(f32[2,4,512,1024]{3,2,1,0:T(8,128)} %copy-done.4, f32[2,4,512]{2,1,0:T(4,128)S(1)} %bitcast.452, bf16[2,512,4,64]{1,3,2,0:T(8,128)(2,1)S(1)} %copy-done.30, bf16[2,1024,4,64]{1,3,2,0:T(8,128)(2,1)S(1)} %copy-done.21), kind=kOutput, calls=%fused_computation.5 | convolution fusion | flops 549449728 | bytes 35160064 | tf_op jit(solution)/shard_map/cqhd,ckhd->chqk/dot_general | solution.py:135
  675.8 9.2 fusion.106
  687.4 10.7 multiply_convert_fusion
  740.0 8.8 fusion.161
  775.2 230.7 %all-reduce.9.cloned.1.call-done = (bf16[2048,1024]{1,0:T(8,128)(2,1)}, bf16[2048,1024]{1,0:T(8,128)(2,1)}) async-done(((bf16[2048,1024]{1,0:T(8,128)(2,1)}, bf16[2048,1024]{1,0:T(8,128)(2,1)}), (bf16[2048,1024]{1,0:T(8,128)(2,1)}, bf16[2048,1024]{1,0:T(8,128)(2,1)})) %all-reduce.9.cloned.1.call-update) | async-done | bytes 8388624 | tf_op jit(solution)/shard_map/psum | solution.py:266
  1006.0 17.0 %fusion.49 = (bf16[32,1024]{1,0:T(8,128)(2,1)S(1)}, bf16[32,1024]{1,0:T(8,128)(2,1)S(1)}, bf16[32,1024]{1,0:T(8,128)(2,1)S(1)}, bf16[32,1024]{1,0:T(8,128)(2,1)S...) fusion(bf16[2048,1024]{1,0:T(8,128)(2,1)} %all-reduce.7.cloned.1.call-done, ...), kind=kLoop, calls=%fused_computation.83 | loop fusion | flops 58523648 | bytes 25870336 | tf_op jit(solution)/shard_map/reduce_sum | solution.py:292
  1027.0 14.0 %gather_fusion = bf16[288,128,128]{2,1,0:T(8,128)(2,1)} fusion(bf16[288,128,128]{2,1,0:T(8,128)(2,1)} %constant_dynamic-update-slice_fusion.9, s32[1024]{0:T(1024)S(1)} %copy-done.78), kind=kCustom, calls=%fused_computation.1 | custom fusion | bytes 18875520 | tf_op jit(solution)/shard_map/jit(_take)/gather | solution.py:370
  1041.0 9.3 fusion
  1066.1 12.4 fusion.46
  1078.5 47.8 %reduce-scatter.5.cloned.1.call-done = bf16[1,36,128,128]{3,2,1,0:T(8,128)(2,1)} async-done(((bf16[1,288,128,128]{3,2,1,0:T(8,128)(2,1)}), bf16[1,36,128,128]{3,2,1,0:T(8,128)(2,1)}) %reduce-scatter.5.cloned.1.call-update) | async-done | bytes 1179664 | tf_op jit(solution)/shard_map/reduce_scatter | solution.py:371
  1148.6 125.3 %reduce-scatter.3.cloned.1.call-done = f32[32,1024]{1,0:T(8,128)} async-done(((f32[1024,1024]{1,0:T(8,128)}), f32[32,1024]{1,0:T(8,128)}) %reduce-scatter.3.cloned.1.call-update) | async-done | bytes 131088 | tf_op jit(solution)/shard_map/reduce_scatter | solution.py:368
  (341 shorter events, 306.7 us)
Async XLA Ops:
  7.2 1119.1 %copy-start = (f32[1,36,128,128]{3,2,1,0:T(8,128)S(1)}, f32[1,36,128,128]{3,2,1,0:T(8,128)}, u32[]{:S(2)}) copy-start(f32[1,36,128,128]{3,2,1,0:T(8,128)} %param.26) | copy-start | bytes 7077892
  7.2 15.9 %copy-start.76 = (s32[288]{0:T(512)S(1)}, s32[288]{0:T(512)}, u32[]{:S(2)}) copy-start(s32[288]{0:T(512)} %param.22) | copy-start | bytes 3460
  7.2 34.2 %all-gather.3.cloned.1.call-start = ((), (), s32[]{:S(2)}) async-start(), calls=%async_computation.2 | async-start | bytes 2359296 | tf_op jit(solution)/shard_map/all_gather | solution.py:185
  7.9 94.7 %all-gather.5.cloned.1.call-start = ((), (), s32[]{:S(2)}) async-start(), calls=%async_computation.3 | async-start | bytes 10616832 | tf_op jit(solution)/shard_map/all_gather | solution.py:184
  10.9 379.6 %all-reduce.5.cloned.1.call-start = ((), (), s32[]{:S(2)}) async-start(), calls=%async_computation.4 | async-start | bytes 8388608 | tf_op jit(solution)/shard_map/psum | solution.py:250
  13.2 28.2 %copy-start.79 = (s32[32]{0:T(128)}, s32[32]{0:T(128)S(1)}, u32[]{:S(2)}) copy-start(s32[32]{0:T(128)S(1)} %eq.43) | copy-start | bytes 388
  29.7 136.8 %copy-start.56 = (f32[2048]{0:T(1024)}, f32[2048]{0:T(1024)S(1)}, u32[]{:S(2)}) copy-start(f32[2048]{0:T(1024)S(1)} %broadcast_multiply_fusion.5) | copy-start | bytes 24580
  32.7 133.8 %copy-start.62 = (f32[2048]{0:T(1024)}, f32[2048]{0:T(1024)S(1)}, u32[]{:S(2)}) copy-start(f32[2048]{0:T(1024)S(1)} %add_rsqrt_fusion.1) | copy-start | bytes 24580
  43.5 96.9 %copy-start.52 = (bf16[32,1024]{1,0:T(8,128)(2,1)}, bf16[32,1024]{1,0:T(8,128)(2,1)S(1)}, u32[]{:S(2)}) copy-start(bf16[32,1024]{1,0:T(8,128)(2,1)S(1)} %convolution_convert_fusion.5) | copy-start | bytes 196612
  179.8 35.7 %copy-start.13 = (bf16[2,1024,4,64]{1,3,2,0:T(8,128)(2,1)}, bf16[2,1024,4,64]{1,3,2,0:T(8,128)(2,1)S(1)}, u32[]{:S(2)}) copy-start(bf16[2,1024,4,64]{1,3,2,0:T(8,128)(2,1)S(1)} %copy.197) | copy-start | bytes 3145732
  235.0 350.8 %all-reduce.7.cloned.1.call-start = ((), (), s32[]{:S(2)}) async-start(), calls=%async_computation.5 | async-start | bytes 8388608 | tf_op jit(solution)/shard_map/psum | solution.py:287
  431.6 574.3 %all-reduce.9.cloned.1.call-start = ((), (), s32[]{:S(2)}) async-start(), calls=%async_computation.8 | async-start | bytes 16777216 | tf_op jit(solution)/shard_map/psum | solution.py:266
  615.7 16.9 %slice-start.7 = ((s8[16777216]{0:T(1024)(128)(4,1)}), s8[4194304]{0:T(1024)(128)(4,1)S(1)}, s32[]{:S(2)}) async-start(s8[16777216]{0:T(1024)(128)(4,1)} %bitcast.403), calls=%async_computation.16 | async-start | bytes 8388608
  615.7 16.9 %copy-start.59 = (f32[1,8,512]{2,1,0:T(8,128)S(1)}, f32[1,8,512]{2,1,0:T(8,128)}, u32[]{:S(2)}) copy-start(f32[1,8,512]{2,1,0:T(8,128)} %log_add_fusion.1) | copy-start | bytes 49156
  662.1 25.3 %slice-start = ((s8[16777216]{0:T(1024)(128)(4,1)}), s8[4194304]{0:T(1024)(128)(4,1)S(1)}, s32[]{:S(2)}) async-start(s8[16777216]{0:T(1024)(128)(4,1)} %bitcast.401), calls=%async_computation.9 | async-start | bytes 8388608
  662.1 25.3 %slice-start.1 = ((s8[16777216]{0:T(1024)(128)(4,1)}), s8[4194304]{0:T(1024)(128)(4,1)S(1)}, s32[]{:S(2)}) async-start(s8[16777216]{0:T(1024)(128)(4,1)} %bitcast.401), calls=%async_computation.10 | async-start | bytes 8388608
  662.1 25.3 %slice-start.2 = ((s8[16777216]{0:T(1024)(128)(4,1)}), s8[4194304]{0:T(1024)(128)(4,1)S(1)}, s32[]{:S(2)}) async-start(s8[16777216]{0:T(1024)(128)(4,1)} %bitcast.401), calls=%async_computation.11 | async-start | bytes 8388608
  687.4 16.9 %copy-start.15 = (f32[2,4,64,1024]{3,2,1,0:T(8,128)S(1)}, f32[2,4,64,1024]{3,2,1,0:T(8,128)}, u32[]{:S(2)}) copy-start(f32[2,4,64,1024]{3,2,1,0:T(8,128)} %fusion.157) | copy-start | bytes 6291460
  716.0 410.2 %reduce-scatter.5.cloned.1.call-start = ((), (), s32[]{:S(2)}) async-start(), calls=%async_computation.7 | async-start | bytes 10616832 | tf_op jit(solution)/shard_map/reduce_scatter | solution.py:371
  770.1 235.9 %copy-start.37 = (f32[32,1024]{1,0:T(8,128)S(1)}, f32[32,1024]{1,0:T(8,128)}, u32[]{:S(2)}) copy-start(f32[32,1024]{1,0:T(8,128)} %get-tuple-element.43) | copy-start | bytes 393220
  770.1 235.9 %copy-start.72 = (f32[32,64]{1,0:T(8,128)S(1)}, f32[32,64]{1,0:T(8,128)}, u32[]{:S(2)}) copy-start(f32[32,64]{1,0:T(8,128)} %rsqrt.27) | copy-start | bytes 24580
  770.1 235.9 %copy-start.73 = (f32[32,64]{1,0:T(8,128)S(1)}, f32[32,64]{1,0:T(8,128)}, u32[]{:S(2)}) copy-start(f32[32,64]{1,0:T(8,128)} %div.65) | copy-start | bytes 24580
  1006.0 17.8 %copy-start.61 = (bf16[4,8,8,128]{3,2,1,0:T(8,128)(2,1)S(1)}, bf16[4,8,8,128]{3,2,1,0:T(8,128)(2,1)}, u32[]{:S(2)}) copy-start(bf16[4,8,8,128]{3,2,1,0:T(8,128)(2,1)} %copy.266) | copy-start | bytes 196612
  1050.3 223.6 %reduce-scatter.3.cloned.1.call-start = ((), (), s32[]{:S(2)}) async-start(), calls=%async_computation.6 | async-start | bytes 4325376 | tf_op jit(solution)/shard_map/reduce_scatter | solution.py:368
  (76 other events, 510.7 us)
Sparse Core Ops, SparseCore 0:
  9.9 31.4 all-gather.2
  43.8 58.6 all-gather.4
  235.1 155.3 all-reduce.4
  431.8 153.9 all-reduce.6
  716.1 289.8 all-reduce.8
  1050.4 75.7 reduce-scatter.4
  1129.1 144.7 reduce-scatter.2
where the time goes:
time: 1300 us; the launch traced here: 1280 us
  waiting for transfers between devices  752 us (58%)
  matrix products  190 us (15%)
  local copies, waits for them, and re-layouts  168 us (13%)
  other arithmetic  137 us (11%)
  blocking collectives  18.1 us (1%)
  between operations  15.8 us (1%)
    psum x1, waiting for transfers between devices, body(): lax.psum(jnp.dot(activated, w_down, preferred_element_type=jnp.float32).a...  231 us
    psum x1, waiting for transfers between devices, body(): lax.psum(contract_cols(grad_pre, back_up).astype(jnp.bfloat16), 'mp')  141 us
    psum x1, waiting for transfers between devices, body(): lax.psum(jnp.dot(attended, w_out, preferred_element_type=jnp.float32).ast...  139 us
    reduce_scatter x1, waiting for transfers between devices, body(): lax.psum_scatter(table_term, ('dp', 'mp'), scatter_dimension=0, tiled=True)  125 us
    all_gather x1, waiting for transfers between devices, body(): lax.all_gather(masters.astype(jnp.bfloat16), 'dp', axis=1, tiled=True)  59.1 us
    reduce_scatter x1, waiting for transfers between devices, body(): lax.psum_scatter(owned[None].astype(jnp.bfloat16), 'dp', scatter_dimensio...  47.8 us
    unnamed x205, local copies, waits for them, and re-layouts  36.8 us
    dot_general x5, matrix products, contract_cols(): lax.dot_general(left_side, right_side, (((1,), (1,)), ((), ())), preferre...  29.2 us
  transfers between devices with their start and end apart: 7, of which 7 were waited for; matrix products, arithmetic and copies ran while one was open for 13% of the time, Pallas kernels for 0%

commit v1 on v0

v1 whole, which is shorter than its diff:
```python
import functools

import jax
import jax.numpy as jnp
from jax import lax
from jax.experimental import pallas as pl
from jax.experimental.pallas import tpu as pltpu
from jax.sharding import PartitionSpec as P

D = 1024
H = 16
HD = 64
FF = 4096
FRAMES = 16
FRAME_TOK = 64
LEVELS = 1024
PATTERNS = 4
TILE = 128
CLIP = FRAMES * FRAME_TOK

EPS_NORM = 1e-06
BETA_ONE = 0.5
BETA_TWO = 0.75
EPS_ADAM = 1e-08
DECAY = 0.01
LOG2E = 1.4426950408889634
GELU_A = 0.7978845608028654
GELU_B = 0.044715

BF = jnp.bfloat16
F32 = jnp.float32
VMEM_BYTES = 60 * 1024 * 1024


def params(**kw):
    return pltpu.CompilerParams(vmem_limit_bytes=VMEM_BYTES, **kw)


def cost(flops, nbytes, trans=0):
    return pl.CostEstimate(flops=int(flops), bytes_accessed=int(nbytes), transcendentals=int(trans))


def dot(left, right, dims):
    return lax.dot_general(left, right, (dims, ((), ())), preferred_element_type=F32)


NN = ((1,), (0,))
NT = ((1,), (1,))
TN = ((0,), (0,))


def tile_layout(groups):
    local_width = H // groups * HD
    shapes = [
        (D, 3 * local_width),
        (local_width, D),
        (D, FF // groups),
        (FF // groups, D),
        (D, 6 * D // groups),
    ]
    counts = [height // TILE * (breadth // TILE) for height, breadth in shapes]
    return (shapes, counts)


def kind_rates(tile_ids, counts):
    scales = [
        0.35 * D ** (-0.5),
        1.5 * (H * HD) ** (-0.5),
        0.5 * D ** (-0.5),
        0.5 * FF ** (-0.5),
        0.5 * D ** (-0.5),
    ]
    tile_rates = jnp.full(tile_ids.shape, scales[0], F32)
    boundary = 0
    for category in range(1, 5):
        boundary = boundary + counts[category - 1]
        tile_rates = jnp.where(tile_ids >= boundary, jnp.float32(scales[category]), tile_rates)
    return tile_rates


def unpack(tile_stack, shapes, counts):
    matrices = []
    offset = 0
    for (height, breadth), amount in zip(shapes, counts):
        stacked = tile_stack[offset : offset + amount].reshape(
            height // TILE, breadth // TILE, TILE, TILE
        )
        matrices.append(stacked.transpose(0, 2, 1, 3).reshape(height, breadth))
        offset = offset + amount
    return matrices


def pack(matrices):
    stacked = []
    for matrix in matrices:
        height, breadth = matrix.shape
        stacked.append(
            matrix.reshape(height // TILE, TILE, breadth // TILE, TILE)
            .transpose(0, 2, 1, 3)
            .reshape(-1, TILE, TILE)
        )
    return jnp.concatenate(stacked, axis=0)


def pick_kernel(inv_ref, q_ref, k_ref, v_ref, o_ref, up_ref, down_ref, *rest):
    mod_refs, (attn_out, up_out, down_out, mod_out) = rest[:-4], rest[-4:]
    part = inv_ref[inv_ref.shape[0] - 1]
    del part
    for role, ref in enumerate((q_ref, k_ref, v_ref)):
        attn_out[role] = ref[0].T
    attn_out[3] = o_ref[0]
    up_out[...] = up_ref[0].T
    down_out[...] = down_ref[0]
    for col, ref in enumerate(mod_refs):
        mod_out[:, col * TILE : (col + 1) * TILE] = ref[0]


def pick_chunk(gathered, inverse, chip, core):
    table = jnp.concatenate([inverse, jnp.stack([chip, core]).astype(jnp.int32)])
    base = inverse.shape[0]

    def at(fn):
        def index_map(j, tab):
            return (tab[fn(j, tab[base], tab[base + 1])], 0, 0)

        return pl.BlockSpec((1, TILE, TILE), index_map)

    specs = [
        at(lambda j, c, k: j * 6 + k),
        at(lambda j, c, k: j * 6 + 2 + k),
        at(lambda j, c, k: j * 6 + 4 + k),
        at(lambda j, c, k: 48 + k * 8 + j),
        at(lambda j, c, k: 64 + j * 8 + 4 * k + c),
        at(lambda j, c, k: 128 + (4 * k + c) * 8 + j),
    ] + [at(lambda j, c, k, col=col: 192 + j * 12 + col) for col in range(12)]
    attn, up, down, mod = pl.pallas_call(
        pick_kernel,
        grid_spec=pltpu.PrefetchScalarGridSpec(
            num_scalar_prefetch=1,
            grid=(8,),
            in_specs=specs,
            out_specs=[
                pl.BlockSpec((4, TILE, TILE), lambda j, tab: (0, 0, j)),
                pl.BlockSpec((TILE, TILE), lambda j, tab: (0, j)),
                pl.BlockSpec((TILE, TILE), lambda j, tab: (0, j)),
                pl.BlockSpec((TILE, 12 * TILE), lambda j, tab: (j, 0)),
            ],
        ),
        out_shape=[
            jax.ShapeDtypeStruct((4, TILE, D), BF),
            jax.ShapeDtypeStruct((TILE, D), BF),
            jax.ShapeDtypeStruct((TILE, D), BF),
            jax.ShapeDtypeStruct((D, 12 * TILE), BF),
        ],
        compiler_params=params(),
        cost_estimate=cost(0, 2 * 144 * 32768),
        name="pick",
    )(table, *([gathered] * len(specs)))
    rows = TILE // 4
    attn = lax.dynamic_slice_in_dim(attn, chip * rows, rows, axis=1)
    return attn.reshape(4 * rows, D), up, down, mod


def pick_chunk_plain(gathered, inverse, chip, core, chips, shapes, counts):
    w_qkv, w_out, w_up, w_down, w_mod = unpack(jnp.take(gathered, inverse, axis=0), shapes, counts)
    width = w_out.shape[0]
    half = width // 2
    ffn = w_up.shape[1] // 2
    rows, ffn_rows = half // chips, ffn // chips
    parts = []
    for role in range(3):
        parts.append(w_qkv[:, role * width : (role + 1) * width].T)
    parts.append(w_out)
    start = core * half + chip * rows
    attn = jnp.concatenate([lax.dynamic_slice_in_dim(p, start, rows, axis=0) for p in parts], axis=0)
    ffn_start = core * ffn + chip * ffn_rows
    up = lax.dynamic_slice_in_dim(w_up.T, ffn_start, ffn_rows, axis=0)
    down = lax.dynamic_slice_in_dim(w_down, ffn_start, ffn_rows, axis=0)
    return attn, up, down, w_mod


def norm_rows(values):
    centered = values - jnp.mean(values, axis=-1, keepdims=True)
    inverse_std = lax.rsqrt(jnp.mean(centered * centered, axis=-1, keepdims=True) + EPS_NORM)
    return centered * inverse_std, inverse_std


def norm_back(grad_normed, normed, inverse_std):
    centered = grad_normed - jnp.mean(grad_normed, axis=-1, keepdims=True)
    return inverse_std * (centered - normed * jnp.mean(grad_normed * normed, axis=-1, keepdims=True))


def frames_of(rows):
    return rows.reshape(-1, FRAME_TOK, D)


def flat(framed):
    return framed.reshape(-1, D)


BLK = 256
FBLK = BLK // FRAME_TOK


def row_spec():
    return pl.BlockSpec((BLK, D), lambda i: (i, 0))


def mod_spec(parts):
    return pl.BlockSpec((FBLK, parts, D), lambda i: (i, 0, 0))


def row_call(kernel, name, row_ins, mods, row_outs, mod_outs, nbytes):
    outs = [jax.ShapeDtypeStruct((CLIP, D), t) for t in row_outs]
    outs += [jax.ShapeDtypeStruct((FRAMES, n, D), F32) for n in mod_outs]
    return pl.pallas_call(
        kernel,
        grid=(CLIP // BLK,),
        in_specs=[row_spec() for _ in row_ins] + [mod_spec(6)],
        out_specs=[row_spec() for _ in row_outs] + [mod_spec(n) for n in mod_outs],
        out_shape=outs,
        compiler_params=params(),
        cost_estimate=cost(30 * CLIP * D, nbytes),
        name=name,
    )(*row_ins, mods)


def first_norm_kernel(x_ref, mod_ref, h_ref):
    normed, _ = norm_rows(x_ref[...].astype(F32))
    mods = mod_ref[...]
    h_ref[...] = flat(
        frames_of(normed) * (1.0 + mods[:, 1:2]) + mods[:, 0:1]
    ).astype(BF)


def middle_kernel(x_ref, a_ref, b_ref, dy_ref, mod_ref, y_ref, s_ref, h_ref, de_ref):
    mods = mod_ref[...]
    branch = (a_ref[...].astype(F32) + b_ref[...].astype(F32)).astype(BF)
    s_ref[...] = branch
    mid = frames_of(x_ref[...].astype(F32)) + mods[:, 2:3] * frames_of(branch.astype(F32))
    y_ref[...] = flat(mid)
    normed, _ = norm_rows(flat(mid))
    h_ref[...] = flat(
        frames_of(normed) * (1.0 + mods[:, 4:5]) + mods[:, 3:4]
    ).astype(BF)
    de_ref[...] = flat(mods[:, 5:6] * frames_of(dy_ref[...].astype(F32))).astype(BF)


def back_kernel(y_ref, g_ref, gp_ref, dy_ref, s_ref, e_ref, ep_ref, mod_ref, out_ref, dy1_ref, da_ref, dm_ref):
    mods = mod_ref[...]
    mid = y_ref[...]
    feed = e_ref[...].astype(F32) + ep_ref[...].astype(F32)
    dy = dy_ref[...].astype(F32)
    out_ref[...] = (mid + flat(mods[:, 5:6] * frames_of(feed))).astype(BF)
    normed, inverse_std = norm_rows(mid)
    grad = g_ref[...].astype(F32) + gp_ref[...].astype(F32)
    dm_ref[:, 0] = jnp.sum(frames_of(grad), axis=1)
    dm_ref[:, 1] = jnp.sum(frames_of(grad * normed), axis=1)
    scaled = flat(frames_of(grad) * (1.0 + mods[:, 4:5]))
    dy1 = dy + norm_back(scaled, normed, inverse_std)
    dy1_ref[...] = dy1
    dm_ref[:, 2] = jnp.sum(frames_of(dy1 * s_ref[...].astype(F32)), axis=1)
    dm_ref[:, 3] = jnp.sum(frames_of(dy * feed), axis=1)
    da_ref[...] = flat(mods[:, 2:3] * frames_of(dy1)).astype(BF)


def last_kernel(x_ref, g_ref, gp_ref, dy1_ref, mod_ref, out_ref, dm_ref):
    mods = mod_ref[...]
    normed, inverse_std = norm_rows(x_ref[...].astype(F32))
    grad = g_ref[...].astype(F32) + gp_ref[...].astype(F32)
    dm_ref[:, 0] = jnp.sum(frames_of(grad), axis=1)
    dm_ref[:, 1] = jnp.sum(frames_of(grad * normed), axis=1)
    scaled = flat(frames_of(grad) * (1.0 + mods[:, 1:2]))
    out_ref[...] = (dy1_ref[...] + norm_back(scaled, normed, inverse_std)).astype(BF)


QBLK = 256
SCALE2 = HD ** (-0.5) * LOG2E


def attend_kernel(qkv_ref, bias_ref, o_ref, lse_ref):
    for head in range(2):
        lanes = slice(head * HD, (head + 1) * HD)
        keys = qkv_ref[:, TILE + head * HD : TILE + (head + 1) * HD]
        values = qkv_ref[:, 2 * TILE + head * HD : 2 * TILE + (head + 1) * HD]

        def step(i, _, lanes=lanes, keys=keys, values=values, head=head):
            start = pl.multiple_of(i * QBLK, QBLK)
            queries = qkv_ref[pl.ds(start, QBLK), lanes]
            scores = dot(keys, queries, NT).reshape(FRAMES, FRAME_TOK, QBLK)
            scores = scores * SCALE2 + bias_ref[:, pl.ds(start, QBLK)][:, None, :]
            peak = jnp.max(jnp.max(scores, axis=0), axis=0, keepdims=True)
            weights = jnp.exp2(scores - peak[None])
            total = jnp.sum(jnp.sum(weights, axis=0), axis=0, keepdims=True)
            mixed = dot(values, weights.reshape(CLIP, QBLK).astype(BF), TN)
            o_ref[lanes, pl.ds(start, QBLK)] = (mixed / total).astype(BF)
            lse_ref[0, head : head + 1, pl.ds(start, QBLK)] = peak + jnp.log2(total)
            return 0

        lax.fori_loop(0, CLIP // QBLK, step, 0)


def attend(qkv, bias):
    groups = qkv.shape[1] // (3 * TILE)
    return pl.pallas_call(
        attend_kernel,
        grid=(groups,),
        in_specs=[
            pl.BlockSpec((CLIP, 3 * TILE), lambda m: (0, m)),
            pl.BlockSpec((FRAMES, CLIP), lambda m: (0, 0)),
        ],
        out_specs=[
            pl.BlockSpec((TILE, CLIP), lambda m: (m, 0)),
            pl.BlockSpec((1, 2, CLIP), lambda m: (m, 0, 0)),
        ],
        out_shape=[
            jax.ShapeDtypeStruct((groups * TILE, CLIP), BF),
            jax.ShapeDtypeStruct((groups, 2, CLIP), F32),
        ],
        compiler_params=params(),
        cost_estimate=cost(groups * 2 * 4 * CLIP * CLIP * HD * 3, 2 * qkv.size, groups * 2 * CLIP * CLIP),
        name="attend",
    )(qkv, bias)


def attend_back_kernel(qkv_ref, o_ref, do_ref, lse_ref, bias_ref, out_ref, dk_ref, dv_ref):
    for head in range(2):
        lanes = slice(head * HD, (head + 1) * HD)
        keys = qkv_ref[:, TILE + head * HD : TILE + (head + 1) * HD]
        values = qkv_ref[:, 2 * TILE + head * HD : 2 * TILE + (head + 1) * HD]
        dk_ref[...] = jnp.zeros_like(dk_ref)
        dv_ref[...] = jnp.zeros_like(dv_ref)

        def step(i, _, lanes=lanes, keys=keys, values=values, head=head):
            start = pl.multiple_of(i * QBLK, QBLK)
            across = pl.ds(start, QBLK)
            queries = qkv_ref[across, lanes]
            grad = do_ref[lanes, across]
            shift = bias_ref[:, across] - lse_ref[0, head : head + 1, across]
            scores = dot(keys, queries, NT).reshape(FRAMES, FRAME_TOK, QBLK)
            soft = jnp.exp2(scores * SCALE2 + shift[:, None, :]).reshape(CLIP, QBLK)
            delta = jnp.sum(
                grad.astype(F32) * o_ref[lanes, across].astype(F32), axis=0, keepdims=True
            )
            grad_soft = dot(values, grad, NN)
            grad_scores = (soft * (grad_soft - delta)).astype(BF)
            dv_ref[...] += dot(soft.astype(BF), grad, NT)
            dk_ref[...] += dot(grad_scores, queries, NN)
            grad_query = dot(keys, grad_scores, TN) * HD ** (-0.5)
            out_ref[across, lanes] = grad_query.T.astype(BF)
            return 0

        lax.fori_loop(0, CLIP // QBLK, step, 0)
        out_ref[:, TILE + head * HD : TILE + (head + 1) * HD] = (dk_ref[...] * HD ** (-0.5)).astype(BF)
        out_ref[:, 2 * TILE + head * HD : 2 * TILE + (head + 1) * HD] = dv_ref[...].astype(BF)


def attend_back(qkv, o_rows, do_rows, lse, bias):
    groups = qkv.shape[1] // (3 * TILE)
    return pl.pallas_call(
        attend_back_kernel,
        grid=(groups,),
        in_specs=[
            pl.BlockSpec((CLIP, 3 * TILE), lambda m: (0, m)),
            pl.BlockSpec((TILE, CLIP), lambda m: (m, 0)),
            pl.BlockSpec((TILE, CLIP), lambda m: (m, 0)),
            pl.BlockSpec((1, 2, CLIP), lambda m: (m, 0, 0)),
            pl.BlockSpec((FRAMES, CLIP), lambda m: (0, 0)),
        ],
        out_specs=pl.BlockSpec((CLIP, 3 * TILE), lambda m: (0, m)),
        out_shape=jax.ShapeDtypeStruct(qkv.shape, BF),
        scratch_shapes=[pltpu.VMEM((CLIP, HD), F32), pltpu.VMEM((CLIP, HD), F32)],
        compiler_params=params(),
        cost_estimate=cost(groups * 2 * 10 * CLIP * CLIP * HD * 3, 4 * qkv.size, groups * 2 * CLIP * CLIP),
        name="attend_back",
    )(qkv, o_rows, do_rows, lse, bias)


UNITS = 256
ROWS = 512


def feed_kernel(h_ref, de_ref, up_ref, down_ref, e_ref, dh_ref, dup_ref, ddown_ref, e_acc, dh_acc, up_acc, down_acc):
    block = pl.program_id(0)
    last = pl.num_programs(0) - 1
    up = up_ref[...]
    down = down_ref[...]
    for part in range(CLIP // ROWS):
        rows = slice(part * ROWS, (part + 1) * ROWS)
        hidden = h_ref[rows]
        grad = de_ref[rows]
        pre = dot(hidden, up, NT)
        square = pre * pre
        tanh = jnp.tanh(GELU_A * pre * (1.0 + GELU_B * square))
        act = (0.5 * pre * (1.0 + tanh)).astype(BF)
        slope = 0.5 * (1.0 + tanh) + 0.5 * pre * (1.0 - tanh * tanh) * (
            GELU_A * (1.0 + 3.0 * GELU_B * square)
        )
        grad_act = dot(grad, down, NT).astype(BF).astype(F32)
        grad_pre = (grad_act * slope).astype(BF)
        feed = dot(act, down, NN)
        back = dot(grad_pre, up, NN)

        @pl.when(block == 0)
        def _():
            e_acc[rows] = feed
            dh_acc[rows] = back

        @pl.when(block > 0)
        def _():
            e_acc[rows] += feed
            dh_acc[rows] += back

        if part == 0:
            down_acc[...] = dot(act, grad, TN)
            up_acc[...] = dot(grad_pre, hidden, TN)
        else:
            ddown_ref[...] = (down_acc[...] + dot(act, grad, TN)).astype(BF)
            dup_ref[...] = (up_acc[...] + dot(grad_pre, hidden, TN)).astype(BF)

    @pl.when(block == last)
    def _():
        e_ref[...] = e_acc[...].astype(BF)
        dh_ref[...] = dh_acc[...].astype(BF)


def feed_both(hidden, grad, up, down):
    units = up.shape[0]
    whole = pl.BlockSpec((CLIP, D), lambda i: (0, 0))
    strip = pl.BlockSpec((UNITS, D), lambda i: (i, 0))
    return pl.pallas_call(
        feed_kernel,
        grid=(units // UNITS,),
        in_specs=[whole, whole, strip, strip],
        out_specs=[whole, whole, strip, strip],
        out_shape=[jax.ShapeDtypeStruct((CLIP, D), BF)] * 2 + [jax.ShapeDtypeStruct((units, D), BF)] * 2,
        scratch_shapes=[
            pltpu.VMEM((CLIP, D), F32),
            pltpu.VMEM((CLIP, D), F32),
            pltpu.VMEM((UNITS, D), F32),
            pltpu.VMEM((UNITS, D), F32),
        ],
        compiler_params=params(),
        cost_estimate=cost(12 * CLIP * D * units, 8 * CLIP * D + 8 * units * D, CLIP * units),
        name="feed_both",
    )(hidden, grad, up, down)


def adam_step(grad, left, right, one, two, master, rate):
    low_left, low_right = left.astype(BF), right.astype(BF)
    turned = dot(low_left, grad.astype(BF), TN)
    rotated = dot(turned.astype(BF), low_right, NN)
    new_one = BETA_ONE * one + (1.0 - BETA_ONE) * rotated
    new_two = BETA_TWO * two + (1.0 - BETA_TWO) * rotated * rotated
    direction = new_one / (jnp.sqrt(new_two) + EPS_ADAM)
    back = dot(low_left, direction.astype(BF), NN)
    back = dot(back.astype(BF), low_right, NT)
    return master - rate * (back + DECAY * master), new_one, new_two


def adam_kernel(tab_ref, rate_ref, *refs, picked, batch):
    if picked:
        red_ref, mod_ref = refs[:2]
        refs = refs[2:]
    else:
        grad_ref = refs[0]
        refs = refs[1:]
    master_ref, one_ref, two_ref, left_ref, right_ref, nm_ref, n1_ref, n2_ref, nw_ref = refs
    for slot in range(batch):
        tile = pl.program_id(0) * batch + slot
        if picked:
            col = pl.multiple_of(tab_ref[tile, 8] * TILE, TILE)
            pieces = [
                red_ref[
                    tab_ref[tile, i],
                    pl.ds(pl.multiple_of(tab_ref[tile, 4 + i] * 32, 32), 32),
                    pl.ds(col, TILE),
                ]
                for i in range(4)
            ]
            grad = jnp.concatenate(pieces, axis=0).astype(F32)
            mod_row = pl.multiple_of(tab_ref[tile, 9] * TILE, TILE)
            mod_col = pl.multiple_of(tab_ref[tile, 10] * TILE, TILE)
            mod_grad = mod_ref[pl.ds(mod_row, TILE), pl.ds(mod_col, TILE)].astype(F32)
            kind = tab_ref[tile, 11]
            grad = jnp.where(kind == 1, grad.T, jnp.where(kind == 2, mod_grad, grad))
        else:
            grad = grad_ref[slot].astype(F32)
        master, one, two = adam_step(
            grad, left_ref[slot], right_ref[slot], one_ref[slot], two_ref[slot], master_ref[slot], rate_ref[tile]
        )
        nm_ref[slot] = master
        n1_ref[slot] = one
        n2_ref[slot] = two
        nw_ref[slot] = master.astype(BF)


def pick_table(tiles, device):
    table = []
    piece = jnp.arange(4, dtype=jnp.int32)[None, :]
    t = tiles[:, None]
    is_in = t < 48
    is_out = (t >= 48) & (t < 64)
    is_up = (t >= 64) & (t < 128)
    is_down = (t >= 128) & (t < 192)
    is_mod = t >= 192
    q0, q1, q2, q3, q4 = t, t - 48, t - 64, t - 128, t - 192
    core = jnp.where(is_in, (q0 % 6) % 2, jnp.where(is_out, q1 // 8, jnp.where(is_up, (q2 % 8) // 4, (q3 // 8) // 4)))
    chip = jnp.where(is_up, q2 % 4, (q3 // 8) % 4)
    chip = jnp.where(is_in | is_out, piece, chip)
    source = jnp.where(is_mod, 0, jnp.bitwise_xor(2 * chip + core, device))
    row = jnp.where(is_in, (q0 % 6) // 2, jnp.where(is_out, 3, jnp.where(is_up, 4 + piece, 8 + piece)))
    row = jnp.where(is_mod, 0, row + jnp.zeros_like(piece))
    col = jnp.where(is_in, q0 // 6, jnp.where(is_out, q1 % 8, jnp.where(is_up, q2 // 8, q3 % 8)))
    col = jnp.where(is_mod, 0, col)
    mod_row = jnp.where(is_mod, q4 // 12, 0)
    mod_col = jnp.where(is_mod, q4 % 12, 0)
    kind = jnp.where(is_mod, 2, jnp.where(is_in | is_up, 1, 0))
    return jnp.concatenate([source, row, col, mod_row, mod_col, kind], axis=1).astype(jnp.int32)


def adam(table, rates, sources, master, one, two, left, right):
    slots = master.shape[0]
    batch = max(b for b in (4, 3, 2, 1) if slots % b == 0)
    picked = len(sources) == 2
    tiles = pl.BlockSpec((batch, TILE, TILE), lambda i, *_: (i, 0, 0))
    if picked:
        source_specs = [
            pl.BlockSpec(sources[0].shape, lambda i, *_: (0, 0, 0)),
            pl.BlockSpec(sources[1].shape, lambda i, *_: (0, 0)),
        ]
    else:
        source_specs = [tiles]
    return pl.pallas_call(
        functools.partial(adam_kernel, picked=picked, batch=batch),
        grid_spec=pltpu.PrefetchScalarGridSpec(
            num_scalar_prefetch=2,
            grid=(slots // batch,),
            in_specs=source_specs + [tiles] * 5,
            out_specs=[tiles] * 4,
        ),
        out_shape=[jax.ShapeDtypeStruct(master.shape, F32)] * 3 + [jax.ShapeDtypeStruct(master.shape, BF)],
        compiler_params=params(),
        cost_estimate=cost(slots * 8 * TILE**3, slots * TILE * TILE * 36),
        name="adam",
    )(table, rates, *sources, master, one, two, left, right)


def body(
    activations,
    cotangent,
    level_table,
    true_frames,
    group_pattern,
    noise_levels,
    context_flags,
    owner_list,
    masters,
    moment_one,
    moment_two,
    basis_left,
    basis_right,
):
    groups = lax.axis_size("mp")
    owners = lax.axis_size("dp")
    chips = owners // 2
    bits = chips.bit_length() - 1
    z = lax.axis_index("mp")
    device = lax.axis_index("dp")
    core = device % 2
    chip = device // 2
    local_clips = true_frames.shape[0]
    column_clips = 2 * local_clips
    assert column_clips == groups and chips == 1 << bits
    shapes, counts = tile_layout(groups)
    slots = masters.shape[1]
    fast = chips == 4 and groups == 4

    def swap(v, step):
        return lax.ppermute(v, "dp", [(i, i ^ step) for i in range(owners)])

    def across(v):
        return swap(v, 1)

    def plane(v, bit):
        return swap(v, 2 << bit)

    def z_get(v, s):
        return lax.ppermute(v, "mp", [((i + s) % groups, i) for i in range(groups)])

    def z_put(v, s):
        return lax.ppermute(v, "mp", [(i, (i + s) % groups) for i in range(groups)])

    def plane_double(v):
        held = v[None]
        for bit in range(bits):
            held = jnp.concatenate([held, plane(held, bit)], axis=0)
        return held

    def plane_gather(v):
        if chips != 4:
            return plane_double(v)
        half = v.shape[0] // 2
        by_x, by_y = plane(v, 0), plane(v, 1)
        low, high = plane(by_x[:half], 1), plane(by_y[half:], 0)
        return jnp.stack([v, by_x, by_y, jnp.concatenate([low, high], axis=0)])

    def add(a, b):
        return (a.astype(F32) + b.astype(F32)).astype(BF)

    def plane_reduce(v):
        if chips != 4:
            held = v
            for bit in reversed(range(bits)):
                half = 1 << bit
                held = add(held[:half], plane(held[half:], bit))
            return held[0]
        half = v.shape[1] // 2
        got_low = [plane(v[1, :half], 0), plane(v[3, :half], 0)]
        got_high = [plane(v[2, half:], 1), plane(v[3, half:], 1)]
        pass_low = plane(add(v[2, :half], got_low[1]), 1)
        pass_high = plane(add(v[1, half:], got_high[1]), 0)
        low = v[0, :half].astype(F32) + got_low[0].astype(F32) + pass_low.astype(F32)
        high = v[0, half:].astype(F32) + got_high[0].astype(F32) + pass_high.astype(F32)
        return jnp.concatenate([low, high], axis=0).astype(BF)

    def z_gather(v):
        return jnp.stack([v] + [z_get(v, s) for s in range(1, groups)])

    def z_reduce(v):
        total = v[0].astype(F32)
        for s in range(1, groups):
            total = total + z_put(v[s], s).astype(F32)
        return total

    with jax.named_scope("entry"):
        holds = (z // local_clips) == core
        local = (z % local_clips) * CLIP
        pair = jnp.stack(
            [
                lax.dynamic_slice_in_dim(activations, local, CLIP, axis=0),
                lax.dynamic_slice_in_dim(cotangent, local, CLIP, axis=0),
            ]
        )
        pair = jnp.where(holds, pair, across(pair))
        x, dy = pair[0], pair[1]
        facts = jnp.concatenate(
            [context_flags, true_frames[:, None], group_pattern[:, None]], axis=1
        ).astype(jnp.int32)
        other = across(facts)
        facts = jnp.where(
            core == 0, jnp.concatenate([facts, other]), jnp.concatenate([other, facts])
        )
        flagged = facts[:, :FRAMES] == 1
        frame_index = jnp.arange(FRAMES, dtype=jnp.int32)
        valid = frame_index[None, :] < facts[:, FRAMES][:, None]
        pattern_hot = (
            facts[:, FRAMES + 1][:, None] == jnp.arange(PATTERNS, dtype=jnp.int32)[None, :]
        ).astype(jnp.int32)
        levels = jnp.where(
            flagged, 0, jnp.sum(pattern_hot[:, :, None] * noise_levels[None, :, :], axis=1)
        )
        in_context = flagged & valid
        visible = valid[:, :, None] & (
            jnp.logical_not(in_context)[:, None, :] | in_context[:, :, None]
        )
        visible = lax.dynamic_index_in_dim(visible, z, axis=0, keepdims=False)
        bias = jnp.repeat(jnp.where(visible, 0.0, -1e30).astype(F32), FRAME_TOK, axis=1)
        all_levels = plane_double(levels)

    with jax.named_scope("owner_gather"):
        gathered = lax.all_gather(masters[0].astype(BF), "dp", axis=0, tiled=True)
        table = lax.all_gather(level_table, "dp", axis=0, tiled=True)
        position = jnp.arange(owner_list.shape[0], dtype=jnp.int32)
        inverse = jnp.sum(
            jnp.where(owner_list[None, :] == position[:, None], position[None, :], 0), axis=1
        ).astype(jnp.int32)
        if fast:
            chunk_attn, chunk_up, chunk_down, w_mod = pick_chunk(gathered, inverse, chip, core)
        else:
            chunk_attn, chunk_up, chunk_down, w_mod = pick_chunk_plain(
                gathered, inverse, chip, core, chips, shapes, counts
            )

    with jax.named_scope("weights"):
        rows = chunk_attn.shape[0] // 4
        got = plane_gather(z_gather(chunk_attn)).reshape(chips, groups, 4, rows, D)
        w_in = got[:, :, :3].transpose(1, 2, 0, 3, 4).reshape(-1, D)
        w_out = got[:, :, 3].transpose(1, 0, 2, 3).reshape(-1, D)
        w_up = plane_gather(z_gather(chunk_up)).reshape(-1, D)
        w_down = plane_gather(z_gather(chunk_down)).reshape(-1, D)

    with jax.named_scope("modulation"):
        level_ids = jnp.arange(LEVELS, dtype=jnp.int32)[None, :]
        hot = (levels.reshape(-1)[:, None] == level_ids).astype(BF)
        embedded = dot(hot, table, NN).astype(BF)
        mod_part = dot(embedded, w_mod, NN).reshape(column_clips, FRAMES, -1)
        pieces = [lax.dynamic_index_in_dim(mod_part, z, axis=0, keepdims=False)]
        for s in range(1, groups):
            piece = lax.dynamic_index_in_dim(mod_part, (z + groups - s) % groups, axis=0, keepdims=False)
            pieces.append(z_get(piece, s))
        mods = lax.dynamic_slice_in_dim(jnp.stack(pieces + pieces), (groups - z) % groups, groups, axis=0)
        mods = mods.reshape(groups, FRAMES, 6, D // groups).transpose(1, 2, 0, 3).reshape(FRAMES, 6, D)

    mb = CLIP * D
    with jax.named_scope("attention"):
        (h1,) = row_call(first_norm_kernel, "first_norm", [x], mods, [BF], [], 4 * mb)
        qkv = dot(h1, w_in, NT).astype(BF)
        o_rows, lse = attend(qkv, bias)
        part = dot(o_rows, w_out, TN).astype(BF)
        y1, branch, h2, de = row_call(
            middle_kernel, "middle", [x, part, across(part), dy], mods, [F32, BF, BF, BF], [], 18 * mb
        )

    with jax.named_scope("feed"):
        e_part, dh2_part, d_up, d_down = feed_both(h2, de, w_up, w_down)
        out, dy1, da, dm_mid = row_call(
            back_kernel,
            "back",
            [y1, dh2_part, across(dh2_part), dy, branch, e_part, across(e_part)],
            mods,
            [BF, F32, BF],
            [4],
            24 * mb,
        )
        shape = (chips, groups, -1, D)
        red_up = z_reduce(plane_reduce(d_up.reshape(shape))).astype(BF)
        red_down = z_reduce(plane_reduce(d_down.reshape(shape))).astype(BF)

    def to_column(rows_here):
        half = CLIP // 2
        mine = lax.dynamic_slice_in_dim(rows_here, core * half, half, axis=0)
        by_clip = [mine] + [z_get(mine, s) for s in range(1, groups)]
        by_clip = lax.dynamic_slice_in_dim(jnp.stack(by_clip + by_clip), (groups - z) % groups, groups, axis=0)
        keep = lax.dynamic_slice_in_dim(by_clip, core * local_clips, local_clips, axis=0)
        send = lax.dynamic_slice_in_dim(by_clip, (1 - core) * local_clips, local_clips, axis=0)
        got_half = across(send)
        both = jnp.where(
            core == 0, jnp.stack([keep, got_half], axis=1), jnp.stack([got_half, keep], axis=1)
        )
        return both.reshape(local_clips * CLIP, D)

    with jax.named_scope("block_output"):
        block_output = to_column(out)

    with jax.named_scope("attention_back"):
        do_rows = dot(w_out, da, NT).astype(BF)
        d_out = dot(o_rows, da, NN).astype(BF)
        d_qkv = attend_back(qkv, o_rows, do_rows, lse, bias)
        dh1_part = dot(d_qkv, w_in, NN).astype(BF)
        d_in = dot(d_qkv, h1, TN).astype(BF)
        in_grad, dm_last = row_call(
            last_kernel, "last", [x, dh1_part, across(dh1_part), dy1], mods, [BF], [2], 12 * mb
        )
        d_in = d_in.reshape(groups, 3, chips, rows, D).transpose(2, 0, 1, 3, 4)
        d_out = d_out.reshape(groups, 1, chips, rows, D).transpose(2, 0, 1, 3, 4)
        d_attn = jnp.concatenate([d_in, d_out], axis=2).reshape(chips, groups, 4 * rows, D)
        red_attn = z_reduce(plane_reduce(d_attn)).astype(BF)

    with jax.named_scope("input_grad"):
        input_grad = to_column(in_grad).astype(F32)

    with jax.named_scope("modulation_back"):
        d_mod = jnp.stack(
            [dm_last[:, 0], dm_last[:, 1], dm_mid[:, 2], dm_mid[:, 0], dm_mid[:, 1], dm_mid[:, 3]], axis=1
        ).astype(BF)
        d_mod = (
            d_mod.reshape(FRAMES, 6, groups, D // groups).transpose(2, 0, 1, 3).reshape(groups, FRAMES, -1)
        )
        pieces = [lax.dynamic_index_in_dim(d_mod, z, axis=0, keepdims=False)]
        for s in range(1, groups):
            pieces.append(z_put(lax.dynamic_index_in_dim(d_mod, (z + s) % groups, axis=0, keepdims=False), s))
        d_mod = plane_double(jnp.stack(pieces)).reshape(chips * groups * FRAMES, -1)
        back_clip = (z + groups - jnp.arange(groups, dtype=jnp.int32)) % groups
        clip_hot = (back_clip[:, None] == jnp.arange(groups, dtype=jnp.int32)[None, :]).astype(jnp.int32)
        order = jnp.sum(clip_hot[None, :, :, None] * all_levels[:, None, :, :], axis=2).reshape(-1)
        all_embedded = dot((order[:, None] == level_ids).astype(BF), table, NN).astype(BF)
        d_w_mod = dot(all_embedded, d_mod, TN).astype(BF)
        own_levels = level_table.shape[0]
        own_hot = (
            order[:, None] == device * own_levels + jnp.arange(own_levels, dtype=jnp.int32)[None, :]
        ).astype(BF)
        own_rows = dot(dot(own_hot, d_mod, TN).astype(BF), w_mod, NT)
        own_rows = own_rows.reshape(groups, own_levels // groups, D)
        table_grad = lax.dynamic_index_in_dim(own_rows, z, axis=0, keepdims=False)
        for s in range(1, groups):
            table_grad = table_grad + z_put(
                lax.dynamic_index_in_dim(own_rows, (z + s) % groups, axis=0, keepdims=False), s
            )

    with jax.named_scope("owners"):
        reduced = jnp.concatenate([red_attn, red_up, red_down], axis=0)
        if chips == 4:
            height = reduced.shape[0]
            plane_parts = plane_gather(reduced.reshape(2, height // 2, D)).reshape(chips, height, D)
        else:
            plane_parts = plane_double(reduced)
        everyone = jnp.stack([plane_parts, across(plane_parts)], axis=1).reshape(owners, -1, D)
        tile_ids = lax.dynamic_slice_in_dim(owner_list, device * slots, slots)
        rates = kind_rates(tile_ids, counts)
        if fast:
            picks = pick_table(tile_ids, device)
            sources = [everyone, d_w_mod]
        else:
            picks = jnp.zeros((slots, 12), jnp.int32)
            absolute = jnp.take(
                everyone, jnp.bitwise_xor(jnp.arange(owners, dtype=jnp.int32), device), axis=0
            ).reshape(chips, 2, -1, D)
            attn = absolute[:, :, : 4 * rows].reshape(chips, 2, 4, rows, D)
            attn = attn.transpose(2, 1, 0, 3, 4).reshape(4, -1, D)
            ffn_rows = (absolute.shape[2] - 4 * rows) // 2
            up = absolute[:, :, 4 * rows : 4 * rows + ffn_rows].transpose(1, 0, 2, 3).reshape(-1, D)
            down = absolute[:, :, 4 * rows + ffn_rows :].transpose(1, 0, 2, 3).reshape(-1, D)
            g_in = jnp.concatenate([attn[0].T, attn[1].T, attn[2].T], axis=1)
            packed = pack([g_in, attn[3], up.T, down, d_w_mod])
            sources = [jnp.take(packed, tile_ids, axis=0)]
        new_masters, new_one, new_two, new_weights = adam(
            picks, rates, sources, masters[0], moment_one[0], moment_two[0], basis_left[0], basis_right[0]
        )
    return (
        block_output,
        input_grad,
        table_grad,
        new_masters[None],
        new_one[None],
        new_two[None],
        new_weights[None],
    )


def solution(mesh):
    tiles = P("mp", "dp", None, None)
    in_specs = (
        P("dp", None),
        P("dp", None),
        P("dp", None),
        P("dp"),
        P("dp"),
        P(),
        P("dp", None),
        P(),
        tiles,
        tiles,
        tiles,
        tiles,
        tiles,
    )
    out_specs = (P("dp", None), P("dp", None), P(("dp", "mp"), None), tiles, tiles, tiles, tiles)
    return jax.shard_map(body, mesh=mesh, in_specs=in_specs, out_specs=out_specs, check_vma=False)
```

time: 1300 us -> 804 us (0.62)
  waiting for transfers between devices: 752 us -> 269 us
  Pallas kernels: 0 us -> 168 us
  starting transfers between devices: 0.29 us -> 167 us
  matrix products: 190 us -> 33.5 us
  local copies, waits for them, and re-layouts: 168 us -> 71.2 us
  other arithmetic: 137 us -> 71.6 us
  blocking collectives: 18.1 us -> 0 us
    psum x3 -> x0, waiting for transfers between devices: 510 us -> none  [the longest x1 231 us: body(): lax.psum(jnp.dot(activated, w_down, preferred_element_type=jnp.float32).a...]
    ppermute x0 -> x80, waiting for transfers between devices: none -> 211 us  [the longest x47 106 us: swap(): return lax.ppermute(v, 'dp', [(i, i ^ step) for i in range(owners)])]
    reduce_scatter x2 -> x0, waiting for transfers between devices: 173 us -> none  [the longest x1 125 us: body(): lax.psum_scatter(table_term, ('dp', 'mp'), scatter_dimension=0, tiled=True)]
    pallas_call x0 -> x9, Pallas kernels: none -> 168 us  [the longest x1 47 us: feed_both(): pl.pallas_call(feed_kernel, grid=(units // UNITS,), in_specs=[whole, whol...]
    ppermute x0 -> x80, starting transfers between devices: none -> 167 us  [the longest x15 84.9 us: z_put(): return lax.ppermute(v, 'mp', [(i, (i + s) % groups) for i in range(groups)])]
    dot_general x33 -> x9, matrix products: 190 us -> 33.5 us  [dot(): lax.dot_general(left, right, (dims, ((), ())), preferred_element_type=F32)]
    reduce_sum x9 -> x2, other arithmetic: 52.6 us -> 0.25 us  [the longest x1 0.15 us: body(): jnp.sum(jnp.where(owner_list[None, :] == position[:, None], position[None...]
    another operation x0 -> x20, other arithmetic: none -> 37.3 us  [the longest x9 19 us: plane_gather(): return jnp.stack([v, by_x, by_y, jnp.concatenate([low, high], axis=0)])]
  transfers between devices with their start and end apart: 7 -> 82, of which waited for: 7 -> 29; matrix products, arithmetic and copies ran while one was open for 13% -> 20% of each run, Pallas kernels for 0% -> 12%
where the time goes in v1:
time: 804 us; the launch traced here: 796 us
  waiting for transfers between devices  269 us (33%)
  Pallas kernels  168 us (21%)
  starting transfers between devices  167 us (21%)
  other arithmetic  71.6 us (9%)
  local copies, waits for them, and re-layouts  71.2 us (9%)
  matrix products  33.5 us (4%)
  between operations  15.6 us (2%)
    ppermute x47, waiting for transfers between devices, swap(): return lax.ppermute(v, 'dp', [(i, i ^ step) for i in range(owners)])  106 us
    ppermute x18, waiting for transfers between devices, z_get(): return lax.ppermute(v, 'mp', [((i + s) % groups, i) for i in range(groups)])  90 us
    ppermute x15, starting transfers between devices, z_put(): return lax.ppermute(v, 'mp', [(i, (i + s) % groups) for i in range(groups)])  84.9 us
    ppermute x47, starting transfers between devices, swap(): return lax.ppermute(v, 'dp', [(i, i ^ step) for i in range(owners)])  53.3 us
    pallas_call x1, Pallas kernels, feed_both(): pl.pallas_call(feed_kernel, grid=(units // UNITS,), in_specs=[whole, whol...  47 us
    all_gather x1, waiting for transfers between devices, body(): gathered = lax.all_gather(masters[0].astype(BF), 'dp', axis=0, tiled=True)  41.5 us
    pallas_call x1, Pallas kernels, attend_back(): pl.pallas_call(attend_back_kernel, grid=(groups,), in_specs=[pl.BlockSpec...  35.4 us
    dot_general x9, matrix products, dot(): lax.dot_general(left, right, (dims, ((), ())), preferred_element_type=F32)  33.5 us
  transfers between devices with their start and end apart: 82, of which 29 were waited for; matrix products, arithmetic and copies ran while one was open for 20% of the time, Pallas kernels for 12%

profile of v1, /device:TPU:1, one launch (start us, length us, event | category | flops | bytes accessed | tf_op | source)
XLA Modules:
  0.0 795.7 jit_solution(11050641013277125995)
XLA Ops:
  17.2 5.9 collective-permute-done.1
  30.2 41.5 %all-gather.5.cloned.1.call-done.q_ref.k_ref.v_ref.o_ref.up_ref.down_ref.rest_0_.rest_1_.rest_2_.rest_3_.rest_4_.rest_5_.rest_6_.rest_7_.rest_8_.rest_9_.rest_10_.rest_11_ = bf16[288,128,128]{2,1,0:T(8,128)(2,1)} async-done(((bf16[36,128,128]{2,1,0:T(8,128)(2,1)}), bf16[288,128,128]{2,1,0:T(8,128)(2,1)}) %all-gather.5.cloned.1.call-update) | async-done | bytes 9437200 | tf_op jit(solution)/shard_map/owner_gather/all_gather | solution.py:672
  71.6 7.4 pick.1
  84.9 16.4 %all-gather.3.cloned.1.call-done = bf16[1024,1024]{1,0:T(8,128)(2,1)} async-done(((bf16[128,1024]{1,0:T(8,128)(2,1)}), bf16[1024,1024]{1,0:T(8,128)(2,1)}) %all-gather.3.cloned.1.call-update) | async-done | bytes 2097168 | tf_op jit(solution)/shard_map/owner_gather/all_gather | solution.py:673
  128.3 20.6 %collective-permute-done.9 = bf16[4,128,1024]{2,1,0:T(8,128)(2,1)S(1)} collective-permute-done((bf16[4,128,1024]{2,1,0:T(8,128)(2,1)S(1)}, bf16[4,128,1024]{2,1,0:T(8,128)(2,1)S(1)}, u32[]{:S(2)}, u32[]{:S(2)}) %collective-permute-start.9) | collective-permute-done | bytes 1048608 | tf_op jit(solution)/shard_map/weights/ppermute | solution.py:580
  166.2 7.8 collective-permute-done.21
  188.0 26.6 %attend.1 = (bf16[512,1024]{1,0:T(8,128)(2,1)}, f32[4,2,1024]{2,1,0:T(2,128)}) custom-call(bf16[1024,1536]{1,0:T(8,128)(2,1)} %convolution_convert_fusion.2.qkv_ref, f32[16,1024]{1,0:T(8,128)} %reshape.484.bias_ref), custom_call_target="tpu_custom_call" | custom-call | flops 6442450944 | bytes 3145728 | tf_op jit(solution)/shard_map/attention/attend/pallas_call | solution.py:305
  237.6 7.7 collective-permute-done.25
  256.0 8.0 %middle.1 = (f32[1024,1024]{1,0:T(8,128)}, bf16[1024,1024]{1,0:T(8,128)(2,1)}, bf16[1024,1024]{1,0:T(8,128)(2,1)}, bf16[1024,1024]{1,0:T(8,128)(2,1)}) custom-call(bf16[1024,1024]{1,0:T(8,128)(2,1)} %get-tuple-element.93.x_ref, bf16[1024,1024]{1,0:T(8,128)(2,1)} %copy-done.25, bf16[1024,1024]{1,0:T(8,128)(2,1)} %collective-permute-done.12.b_ref, ...), custom_call_target="tpu_custom_call" | custom-call | flops 31457280 | bytes 18874368 | tf_op jit(solution)/shard_map/attention/middle/pallas_call | solution.py:216
  264.0 47.0 %feed_both.1 = (bf16[1024,1024]{1,0:T(8,128)(2,1)}, bf16[1024,1024]{1,0:T(8,128)(2,1)}, bf16[2048,1024]{1,0:T(8,128)(2,1)}, bf16[2048,1024]{1,0:T(8,128)(2,1)}) custom-call(bf16[1024,1024]{1,0:T(8,128)(2,1)} %get-tuple-element.35.h_ref, bf16[1024,1024]{1,0:T(8,128)(2,1)} %get-tuple-element.36.de_ref, bf16[2048,1024]{1,0:T(8,128)(2,1)} %bitcast.347, ...), custom_call_target="tpu_custom_call" | custom-call | flops 25769803776 | bytes 25165824 | tf_op jit(solution)/shard_map/feed/feed_both/pallas_call | solution.py:431
  321.0 5.1 collective-permute-done.67
  330.9 17.7 %collective-permute-done.38 = s32[1,4,16]{2,1,0:T(4,128)S(1)} collective-permute-done((s32[1,4,16]{2,1,0:T(4,128)S(1)}, s32[1,4,16]{2,1,0:T(4,128)S(1)}, u32[]{:S(2)}, u32[]{:S(2)}) %collective-permute-start.38) | collective-permute-done | bytes 288 | tf_op jit(solution)/shard_map/entry/ppermute | solution.py:580
  362.1 10.0 %collective-permute-done.59 = bf16[2,128,1024]{2,1,0:T(8,128)(2,1)S(1)} collective-permute-done((bf16[2,128,1024]{2,1,0:T(8,128)(2,1)S(1)}, bf16[2,128,1024]{2,1,0:T(8,128)(2,1)S(1)}, u32[]{:S(2)}, u32[]{:S(2)}) %collective-permute-start.59) | collective-permute-done | bytes 524320 | tf_op jit(solution)/shard_map/feed/ppermute | solution.py:580
  374.1 9.3 %collective-permute-done.70 = bf16[2,128,1024]{2,1,0:T(8,128)(2,1)S(1)} collective-permute-done((bf16[2,128,1024]{2,1,0:T(8,128)(2,1)S(1)}, bf16[2,128,1024]{2,1,0:T(8,128)(2,1)S(1)}, u32[]{:S(2)}, u32[]{:S(2)}) %collective-permute-start.70) | collective-permute-done | bytes 524320 | tf_op jit(solution)/shard_map/feed/ppermute | solution.py:580
  406.2 11.4 %back.1 = (bf16[1024,1024]{1,0:T(8,128)(2,1)}, f32[1024,1024]{1,0:T(8,128)}, bf16[1024,1024]{1,0:T(8,128)(2,1)}, f32[16,4,1024]{2,1,0:T(4,128)}) custom-call(f32[1024,1024]{1,0:T(8,128)} %get-tuple-element.34.y_ref, bf16[1024,1024]{1,0:T(8,128)(2,1)} %get-tuple-element.39.g_ref, bf16[1024,1024]{1,0:T(8,128)(2,1)} %copy-done.23, ...), custom_call_target="tpu_custom_call" | custom-call | flops 31457280 | bytes 25165824 | tf_op jit(solution)/shard_map/feed/back/pallas_call | solution.py:216
  421.5 35.4 %attend_back.1 = bf16[1024,1536]{1,0:T(8,128)(2,1)} custom-call(bf16[1024,1536]{1,0:T(8,128)(2,1)} %convolution_convert_fusion.2.qkv_ref, bf16[512,1024]{1,0:T(8,128)(2,1)} %get-tuple-element.33.o_ref, bf16[512,1024]{1,0:T(8,128)(2,1)} %convolution_convert_fusion.7.do_ref, f32[4,2,1024]{2,1,0:T(2,128)} %get-tuple-element.44.lse_ref, ...), custom_call_target="tpu_custom_call" | custom-call | flops 16106127360 | bytes 6291456 | tf_op jit(solution)/shard_map/attention_back/attend_back/pallas_call | solution.py:360
  456.9 5.7 convolution_convert_fusion.1
  489.5 6.8 collective-permute-done.50
  496.3 13.3 %collective-permute-start.33 = (bf16[1024,1024]{1,0:T(8,128)(2,1)}, bf16[1024,1024]{1,0:T(8,128)(2,1)}, u32[]{:S(2)}, u32[]{:S(2)}) collective-permute-start(bf16[1024,1024]{1,0:T(8,128)(2,1)} %convolution_convert_fusion.4.g_ref), channel_id=1, source_target_pairs={{0,4},{4,0},{8,12},{12,8},{16,20},{20,16},{24,28},{28,24},{1,5},{5... | collective-permute-start | bytes 6291464 | tf_op jit(solution)/shard_map/attention_back/ppermute | solution.py:580
  516.0 56.7 %collective-permute-start.51 = (bf16[128,1024]{1,0:T(8,128)(2,1)S(1)}, bf16[128,1024]{1,0:T(8,128)(2,1)S(1)}, u32[]{:S(2)}, u32[]{:S(2)}) collective-permute-start(bf16[128,1024]{1,0:T(8,128)(2,1)S(1)} %slice_bitcast_fusion.36), channel_id=1, source_target_pairs={{0,1},{1,2},{2,3},{3,0},{4,5},{5,6},{6,7},{7,4},{8,9},{9,10},{10,1... | collective-permute-start | bytes 786440 | tf_op jit(solution)/shard_map/attention_back/ppermute | solution.py:592
  593.6 11.3 %collective-permute-done.55 = bf16[128,1024]{1,0:T(8,128)(2,1)S(1)} collective-permute-done((bf16[128,1024]{1,0:T(8,128)(2,1)S(1)}, bf16[128,1024]{1,0:T(8,128)(2,1)S(1)}, u32[]{:S(2)}, u32[]{:S(2)}) %collective-permute-start.55) | collective-permute-done | bytes 262176 | tf_op jit(solution)/shard_map/attention_back/ppermute | solution.py:592
  608.1 7.4 last.1
  656.8 64.4 %collective-permute-done.35 = bf16[512,1024]{1,0:T(8,128)(2,1)S(1)} collective-permute-done((bf16[512,1024]{1,0:T(8,128)(2,1)S(1)}, bf16[512,1024]{1,0:T(8,128)(2,1)S(1)}, u32[]{:S(2)}, u32[]{:S(2)}) %collective-permute-start.35) | collective-permute-done | bytes 1048608 | tf_op jit(solution)/shard_map/input_grad/ppermute | solution.py:589
  768.2 20.2 %adam.1 = (f32[36,128,128]{2,1,0:T(8,128)}, f32[36,128,128]{2,1,0:T(8,128)}, f32[36,128,128]{2,1,0:T(8,128)}, bf16[36,128,128]{2,1,0:T(8,128)(2,1)}) custom-call(s32[36,12]{1,0:T(8,128)} %copy.80.tab_ref, f32[36]{0:T(128)} %get-tuple-element.59.rate_ref, bf16[8,384,1024]{2,1,0:T(8,128)(2,1)} %bitcast.319, ...), custom_call_target="tpu_custom_call" | custom-call | flops 603979776 | bytes 21233664 | tf_op jit(solution)/shard_map/owners/adam/pallas_call | solution.py:534
  (408 shorter events, 316.4 us)
Async XLA Ops:
  7.2 64.5 %all-gather.5.cloned.1.call-start = ((), (), s32[]{:S(2)}) async-start(), calls=%async_computation.1 | async-start | bytes 10616832 | tf_op jit(solution)/shard_map/owner_gather/all_gather | solution.py:672
  10.1 91.2 %all-gather.3.cloned.1.call-start = ((), (), s32[]{:S(2)}) async-start(), calls=%async_computation | async-start | bytes 2359296 | tf_op jit(solution)/shard_map/owner_gather/all_gather | solution.py:673
  84.6 67.6 %collective-permute-start.15 = (bf16[128,1024]{1,0:T(8,128)(2,1)}, bf16[128,1024]{1,0:T(8,128)(2,1)}, u32[]{:S(2)}, u32[]{:S(2)}) collective-permute-start(bf16[128,1024]{1,0:T(8,128)(2,1)} %get-tuple-element.37), channel_id=1, source_target_pairs={{3,0},{0,1},{1,2},{2,3},{7,4},{4,5},{5,6},{6,7},{11,8},{8,9},{9,10... | collective-permute-start | bytes 786440 | tf_op jit(solution)/shard_map/weights/ppermute | solution.py:589
  165.4 53.3 %collective-permute-start.16 = (bf16[4,128,1024]{2,1,0:T(8,128)(2,1)}, bf16[4,128,1024]{2,1,0:T(8,128)(2,1)}, u32[]{:S(2)}, u32[]{:S(2)}) collective-permute-start(bf16[4,128,1024]{2,1,0:T(8,128)(2,1)} %get-tuple-element.97), channel_id=1, source_target_pairs={{0,8},{4,12},{8,0},{12,4},{16,24},{20,28},{24,16},{28,20},{1,9},{5... | collective-permute-start | bytes 3145736 | tf_op jit(solution)/shard_map/weights/ppermute | solution.py:580
  174.0 47.4 %collective-permute-start.17 = (bf16[4,128,1024]{2,1,0:T(8,128)(2,1)}, bf16[4,128,1024]{2,1,0:T(8,128)(2,1)}, u32[]{:S(2)}, u32[]{:S(2)}) collective-permute-start(bf16[4,128,1024]{2,1,0:T(8,128)(2,1)} %get-tuple-element.97), channel_id=1, source_target_pairs={{0,16},{4,20},{8,24},{12,28},{16,0},{20,4},{24,8},{28,12},{1,17},{... | collective-permute-start | bytes 3145736 | tf_op jit(solution)/shard_map/weights/ppermute | solution.py:580
  177.9 46.6 %collective-permute-start.23 = (bf16[4,128,1024]{2,1,0:T(8,128)(2,1)}, bf16[4,128,1024]{2,1,0:T(8,128)(2,1)}, u32[]{:S(2)}, u32[]{:S(2)}) collective-permute-start(bf16[4,128,1024]{2,1,0:T(8,128)(2,1)} %get-tuple-element.95), channel_id=1, source_target_pairs={{0,8},{4,12},{8,0},{12,4},{16,24},{20,28},{24,16},{28,20},{1,9},{5... | collective-permute-start | bytes 3145736 | tf_op jit(solution)/shard_map/weights/ppermute | solution.py:580
  178.2 48.4 %collective-permute-start.24 = (bf16[4,128,1024]{2,1,0:T(8,128)(2,1)}, bf16[4,128,1024]{2,1,0:T(8,128)(2,1)}, u32[]{:S(2)}, u32[]{:S(2)}) collective-permute-start(bf16[4,128,1024]{2,1,0:T(8,128)(2,1)} %get-tuple-element.95), channel_id=1, source_target_pairs={{0,16},{4,20},{8,24},{12,28},{16,0},{20,4},{24,8},{28,12},{1,17},{... | collective-permute-start | bytes 3145736 | tf_op jit(solution)/shard_map/weights/ppermute | solution.py:580
  351.5 51.6 %collective-permute-start.27 = (bf16[1024,1024]{1,0:T(8,128)(2,1)}, bf16[1024,1024]{1,0:T(8,128)(2,1)S(1)}, u32[]{:S(2)}, u32[]{:S(2)}) collective-permute-start(bf16[1024,1024]{1,0:T(8,128)(2,1)} %get-tuple-element.39.g_ref), channel_id=1, source_target_pairs={{0,4},{4,0},{8,12},{12,8},{16,20},{20,16},{24,28},{28,24},{1,5},{5... | collective-permute-start | bytes 6291464 | tf_op jit(solution)/shard_map/feed/ppermute | solution.py:580
  354.6 48.6 %collective-permute-start.28 = (bf16[1024,1024]{1,0:T(8,128)(2,1)S(1)}, bf16[1024,1024]{1,0:T(8,128)(2,1)S(1)}, u32[]{:S(2)}, u32[]{:S(2)}) collective-permute-start(bf16[1024,1024]{1,0:T(8,128)(2,1)S(1)} %copy-done.22), channel_id=1, source_target_pairs={{0,4},{4,0},{8,12},{12,8},{16,20},{20,16},{24,28},{28,24},{1,5},{5... | collective-permute-start | bytes 6291464 | tf_op jit(solution)/shard_map/feed/ppermute | solution.py:580
  384.3 80.8 %collective-permute-start.69 = (bf16[128,1024]{1,0:T(8,128)(2,1)}, bf16[128,1024]{1,0:T(8,128)(2,1)S(1)}, u32[]{:S(2)}, u32[]{:S(2)}) collective-permute-start(bf16[128,1024]{1,0:T(8,128)(2,1)} %slice_bitcast_fusion.28), channel_id=1, source_target_pairs={{0,1},{1,2},{2,3},{3,0},{4,5},{5,6},{6,7},{7,4},{8,9},{9,10},{10,1... | collective-permute-start | bytes 786440 | tf_op jit(solution)/shard_map/feed/ppermute | solution.py:592
  394.6 76.1 %collective-permute-start.60 = (bf16[128,1024]{1,0:T(8,128)(2,1)}, bf16[128,1024]{1,0:T(8,128)(2,1)S(1)}, u32[]{:S(2)}, u32[]{:S(2)}) collective-permute-start(bf16[128,1024]{1,0:T(8,128)(2,1)} %slice_bitcast_fusion.32), channel_id=1, source_target_pairs={{0,1},{1,2},{2,3},{3,0},{4,5},{5,6},{6,7},{7,4},{8,9},{9,10},{10,1... | collective-permute-start | bytes 786440 | tf_op jit(solution)/shard_map/feed/ppermute | solution.py:592
  398.9 69.5 %collective-permute-start.73 = (bf16[128,1024]{1,0:T(8,128)(2,1)}, bf16[128,1024]{1,0:T(8,128)(2,1)S(1)}, u32[]{:S(2)}, u32[]{:S(2)}) collective-permute-start(bf16[128,1024]{1,0:T(8,128)(2,1)} %get-tuple-element.105), channel_id=1, source_target_pairs={{0,2},{1,3},{2,0},{3,1},{4,6},{5,7},{6,4},{7,5},{8,10},{9,11},{10,... | collective-permute-start | bytes 786440 | tf_op jit(solution)/shard_map/feed/ppermute | solution.py:592
  403.2 65.5 %collective-permute-start.74 = (bf16[128,1024]{1,0:T(8,128)(2,1)}, bf16[128,1024]{1,0:T(8,128)(2,1)}, u32[]{:S(2)}, u32[]{:S(2)}) collective-permute-start(bf16[128,1024]{1,0:T(8,128)(2,1)} %get-tuple-element.106), channel_id=1, source_target_pairs={{0,3},{1,0},{2,1},{3,2},{4,7},{5,4},{6,5},{7,6},{8,11},{9,8},{10,9... | collective-permute-start | bytes 786440 | tf_op jit(solution)/shard_map/feed/ppermute | solution.py:592
  405.9 64.8 %collective-permute-start.64 = (bf16[128,1024]{1,0:T(8,128)(2,1)}, bf16[128,1024]{1,0:T(8,128)(2,1)}, u32[]{:S(2)}, u32[]{:S(2)}) collective-permute-start(bf16[128,1024]{1,0:T(8,128)(2,1)} %get-tuple-element.103), channel_id=1, source_target_pairs={{0,2},{1,3},{2,0},{3,1},{4,6},{5,7},{6,4},{7,5},{8,10},{9,11},{10,... | collective-permute-start | bytes 786440 | tf_op jit(solution)/shard_map/feed/ppermute | solution.py:592
  474.2 100.7 %collective-permute-start.30 = (bf16[512,1024]{1,0:T(8,128)(2,1)}, bf16[512,1024]{1,0:T(8,128)(2,1)S(1)}, u32[]{:S(2)}, u32[]{:S(2)}) collective-permute-start(bf16[512,1024]{1,0:T(8,128)(2,1)} %get-tuple-element.66), channel_id=1, source_target_pairs={{2,0},{3,1},{0,2},{1,3},{6,4},{7,5},{4,6},{5,7},{10,8},{11,9},{8,1... | collective-permute-start | bytes 3145736 | tf_op jit(solution)/shard_map/block_output/ppermute | solution.py:589
  488.9 89.7 %collective-permute-start.31 = (bf16[512,1024]{1,0:T(8,128)(2,1)}, bf16[512,1024]{1,0:T(8,128)(2,1)S(1)}, u32[]{:S(2)}, u32[]{:S(2)}) collective-permute-start(bf16[512,1024]{1,0:T(8,128)(2,1)} %get-tuple-element.66), channel_id=1, source_target_pairs={{3,0},{0,1},{1,2},{2,3},{7,4},{4,5},{5,6},{6,7},{11,8},{8,9},{9,10... | collective-permute-start | bytes 3145736 | tf_op jit(solution)/shard_map/block_output/ppermute | solution.py:589
  489.2 95.1 %collective-permute-start.52 = (bf16[2,128,1024]{2,1,0:T(8,128)(2,1)}, bf16[2,128,1024]{2,1,0:T(8,128)(2,1)S(1)}, u32[]{:S(2)}, u32[]{:S(2)}) collective-permute-start(bf16[2,128,1024]{2,1,0:T(8,128)(2,1)} %get-tuple-element.78), channel_id=1, source_target_pairs={{0,16},{4,20},{8,24},{12,28},{16,0},{20,4},{24,8},{28,12},{1,17},{... | collective-permute-start | bytes 1572872 | tf_op jit(solution)/shard_map/attention_back/ppermute | solution.py:580
  496.3 111.9 %collective-permute-start.33 = (bf16[1024,1024]{1,0:T(8,128)(2,1)}, bf16[1024,1024]{1,0:T(8,128)(2,1)}, u32[]{:S(2)}, u32[]{:S(2)}) collective-permute-start(bf16[1024,1024]{1,0:T(8,128)(2,1)} %convolution_convert_fusion.4.g_ref), channel_id=1, source_target_pairs={{0,4},{4,0},{8,12},{12,8},{16,20},{20,16},{24,28},{28,24},{1,5},{5... | collective-permute-start | bytes 6291464 | tf_op jit(solution)/shard_map/attention_back/ppermute | solution.py:580
  516.0 77.7 %collective-permute-start.51 = (bf16[128,1024]{1,0:T(8,128)(2,1)S(1)}, bf16[128,1024]{1,0:T(8,128)(2,1)S(1)}, u32[]{:S(2)}, u32[]{:S(2)}) collective-permute-start(bf16[128,1024]{1,0:T(8,128)(2,1)S(1)} %slice_bitcast_fusion.36), channel_id=1, source_target_pairs={{0,1},{1,2},{2,3},{3,0},{4,5},{5,6},{6,7},{7,4},{8,9},{9,10},{10,1... | collective-permute-start | bytes 786440 | tf_op jit(solution)/shard_map/attention_back/ppermute | solution.py:592
  634.7 86.5 %collective-permute-start.35 = (bf16[512,1024]{1,0:T(8,128)(2,1)S(1)}, bf16[512,1024]{1,0:T(8,128)(2,1)S(1)}, u32[]{:S(2)}, u32[]{:S(2)}) collective-permute-start(bf16[512,1024]{1,0:T(8,128)(2,1)S(1)} %get-tuple-element.64), channel_id=1, source_target_pairs={{2,0},{3,1},{0,2},{1,3},{6,4},{7,5},{4,6},{5,7},{10,8},{11,9},{8,1... | collective-permute-start | bytes 3145736 | tf_op jit(solution)/shard_map/input_grad/ppermute | solution.py:589
  641.3 85.2 %collective-permute-start.39 = (s32[2,4,16]{2,1,0:T(4,128)S(1)}, s32[2,4,16]{2,1,0:T(4,128)S(1)}, u32[]{:S(2)}, u32[]{:S(2)}) collective-permute-start(s32[2,4,16]{2,1,0:T(4,128)S(1)} %pad_add_fusion.1), channel_id=1, source_target_pairs={{0,16},{4,20},{8,24},{12,28},{16,0},{20,4},{24,8},{28,12},{1,17},{... | collective-permute-start | bytes 1544 | tf_op jit(solution)/shard_map/entry/ppermute | solution.py:580
  642.3 81.1 %collective-permute-start.36 = (bf16[512,1024]{1,0:T(8,128)(2,1)S(1)}, bf16[512,1024]{1,0:T(8,128)(2,1)S(1)}, u32[]{:S(2)}, u32[]{:S(2)}) collective-permute-start(bf16[512,1024]{1,0:T(8,128)(2,1)S(1)} %get-tuple-element.64), channel_id=1, source_target_pairs={{3,0},{0,1},{1,2},{2,3},{7,4},{4,5},{5,6},{6,7},{11,8},{8,9},{9,10... | collective-permute-start | bytes 3145736 | tf_op jit(solution)/shard_map/input_grad/ppermute | solution.py:589
  645.0 105.5 %collective-permute-start.32 = (bf16[2,512,1024]{2,1,0:T(8,128)(2,1)}, bf16[2,512,1024]{2,1,0:T(8,128)(2,1)}, u32[]{:S(2)}, u32[]{:S(2)}) collective-permute-start(bf16[2,512,1024]{2,1,0:T(8,128)(2,1)} %get-tuple-element.73), channel_id=1, source_target_pairs={{0,4},{4,0},{8,12},{12,8},{16,20},{20,16},{24,28},{28,24},{1,5},{5... | collective-permute-start | bytes 6291464 | tf_op jit(solution)/shard_map/block_output/ppermute | solution.py:580
  655.2 71.4 %collective-permute-start.44 = (bf16[2,4,16,1536]{3,2,1,0:T(8,128)(2,1)}, bf16[2,4,16,1536]{3,2,1,0:T(8,128)(2,1)}, u32[]{:S(2)}, u32[]{:S(2)}) collective-permute-start(bf16[2,4,16,1536]{3,2,1,0:T(8,128)(2,1)} %pad_maximum_fusion.14), channel_id=1, source_target_pairs={{0,16},{4,20},{8,24},{12,28},{16,0},{20,4},{24,8},{28,12},{1,17},{... | collective-permute-start | bytes 1179656 | tf_op jit(solution)/shard_map/modulation_back/ppermute | solution.py:580
  (113 other events, 1668.6 us)
Sparse Core Ops, SparseCore 0:
  10.4 61.1 all-gather.4
  73.5 27.7 all-gather.2

commit v2 on v1

--- a/solution.py
+++ b/solution.py
@@ -100,65 +100,6 @@
             .reshape(-1, TILE, TILE)
         )
     return jnp.concatenate(stacked, axis=0)
-
-
-def pick_kernel(inv_ref, q_ref, k_ref, v_ref, o_ref, up_ref, down_ref, *rest):
-    mod_refs, (attn_out, up_out, down_out, mod_out) = rest[:-4], rest[-4:]
-    part = inv_ref[inv_ref.shape[0] - 1]
-    del part
-    for role, ref in enumerate((q_ref, k_ref, v_ref)):
-        attn_out[role] = ref[0].T
-    attn_out[3] = o_ref[0]
-    up_out[...] = up_ref[0].T
-    down_out[...] = down_ref[0]
-    for col, ref in enumerate(mod_refs):
-        mod_out[:, col * TILE : (col + 1) * TILE] = ref[0]
-
-
-def pick_chunk(gathered, inverse, chip, core):
-    table = jnp.concatenate([inverse, jnp.stack([chip, core]).astype(jnp.int32)])
-    base = inverse.shape[0]
-
-    def at(fn):
-        def index_map(j, tab):
-            return (tab[fn(j, tab[base], tab[base + 1])], 0, 0)
-
-        return pl.BlockSpec((1, TILE, TILE), index_map)
-
-    specs = [
-        at(lambda j, c, k: j * 6 + k),
-        at(lambda j, c, k: j * 6 + 2 + k),
-        at(lambda j, c, k: j * 6 + 4 + k),
-        at(lambda j, c, k: 48 + k * 8 + j),
-        at(lambda j, c, k: 64 + j * 8 + 4 * k + c),
-        at(lambda j, c, k: 128 + (4 * k + c) * 8 + j),
-    ] + [at(lambda j, c, k, col=col: 192 + j * 12 + col) for col in range(12)]
-    attn, up, down, mod = pl.pallas_call(
-        pick_kernel,
-        grid_spec=pltpu.PrefetchScalarGridSpec(
-            num_scalar_prefetch=1,
-            grid=(8,),
-            in_specs=specs,
-            out_specs=[
-                pl.BlockSpec((4, TILE, TILE), lambda j, tab: (0, 0, j)),
-                pl.BlockSpec((TILE, TILE), lambda j, tab: (0, j)),
-                pl.BlockSpec((TILE, TILE), lambda j, tab: (0, j)),
-                pl.BlockSpec((TILE, 12 * TILE), lambda j, tab: (j, 0)),
-            ],
-        ),
-        out_shape=[
-            jax.ShapeDtypeStruct((4, TILE, D), BF),
-            jax.ShapeDtypeStruct((TILE, D), BF),
-            jax.ShapeDtypeStruct((TILE, D), BF),
-            jax.ShapeDtypeStruct((D, 12 * TILE), BF),
-        ],
-        compiler_params=params(),
-        cost_estimate=cost(0, 2 * 144 * 32768),
-        name="pick",
-    )(table, *([gathered] * len(specs)))
-    rows = TILE // 4
-    attn = lax.dynamic_slice_in_dim(attn, chip * rows, rows, axis=1)
-    return attn.reshape(4 * rows, D), up, down, mod
 
 
 def pick_chunk_plain(gathered, inverse, chip, core, chips, shapes, counts):
@@ -272,6 +213,335 @@
     dm_ref[:, 1] = jnp.sum(frames_of(grad * normed), axis=1)
     scaled = flat(frames_of(grad) * (1.0 + mods[:, 1:2]))
     out_ref[...] = (dy1_ref[...] + norm_back(scaled, normed, inverse_std)).astype(BF)
+
+
+MESH = pl.DeviceIdType.MESH
+HEAD_TILES = 36
+TABLE_TILES = 8
+PAYLOAD = 46
+LEVEL_TILE = HEAD_TILES + TABLE_TILES
+
+
+class Link:
+    def __init__(self, sends, recvs):
+        self.sends, self.recvs, self.used, self.pending = sends, recvs, 0, []
+
+    def make(self, src, dst, dp, mp):
+        copy = pltpu.make_async_remote_copy(
+            src_ref=src,
+            dst_ref=dst,
+            send_sem=self.sends.at[self.used],
+            recv_sem=self.recvs.at[self.used],
+            device_id=(dp, mp),
+            device_id_type=MESH,
+        )
+        self.used += 1
+        return copy
+
+    def send(self, src, dst, dp, mp):
+        copy = self.make(src, dst, dp, mp)
+        copy.start()
+        self.pending.append(copy)
+        return copy
+
+    def drain(self):
+        for copy in self.pending:
+            copy.wait_send()
+        self.pending = []
+
+
+def greet(d, z):
+    barrier = pltpu.get_barrier_semaphore()
+    for step in (1, 2, 4):
+        pl.semaphore_signal(barrier, inc=1, device_id=(jnp.bitwise_xor(d, step), z), device_id_type=MESH)
+    for s in (1, 2, 3):
+        pl.semaphore_signal(barrier, inc=1, device_id=(d, lax.rem(z + s, 4)), device_id_type=MESH)
+    pl.semaphore_wait(barrier, 6)
+
+
+ENTRY_COPIES = 8 + 45 + 3
+
+
+def entry_kernel(
+    idx_ref,
+    pay_ref,
+    act_ref,
+    cot_ref,
+    bias_ref,
+    w_ref,
+    wmod_ref,
+    x_ref,
+    dy_ref,
+    h_ref,
+    mods_ref,
+    bias_out,
+    emb_ref,
+    own_hot_ref,
+    gath,
+    own,
+    turn,
+    xs,
+    dys,
+    bs,
+    part,
+    modbuf,
+    hots,
+    sends,
+    recvs,
+    swap_sends,
+    swap_recvs,
+    local_sems,
+):
+    d, z = lax.axis_index("dp"), lax.axis_index("mp")
+    core, chip = lax.rem(d, 2), d // 2
+    dk, dx, dy = jnp.bitwise_xor(d, 1), jnp.bitwise_xor(d, 2), jnp.bitwise_xor(d, 4)
+    dxy = jnp.bitwise_xor(d, 6)
+    link = Link(sends, recvs)
+    greet(d, z)
+
+    def slot(owner, first=0, count=PAYLOAD):
+        return gath.at[pl.ds(owner * PAYLOAD + first, count)]
+
+    half = PAYLOAD // 2
+    home = pltpu.make_async_copy(pay_ref, slot(d), local_sems.at[0])
+    home.start()
+    to_x = link.send(pay_ref, slot(d), dx, z)
+    to_y = link.send(pay_ref, slot(d), dy, z)
+    to_k = link.send(pay_ref, slot(d), dk, z)
+
+    holds = (z // 2) == core
+    rows = pl.ds(lax.rem(z, 2) * CLIP, CLIP)
+    picks = [
+        (act_ref.at[rows], xs),
+        (cot_ref.at[rows], dys),
+        (bias_ref.at[lax.rem(z, 2)], bs),
+    ]
+
+    def swaps():
+        return [
+            pltpu.make_async_remote_copy(
+                src_ref=src,
+                dst_ref=dst,
+                send_sem=swap_sends.at[i],
+                recv_sem=swap_recvs.at[i],
+                device_id=(dk, z),
+                device_id_type=MESH,
+            )
+            for i, (src, dst) in enumerate(picks)
+        ]
+
+    def keeps():
+        return [pltpu.make_async_copy(src, dst, local_sems.at[1 + i]) for i, (src, dst) in enumerate(picks)]
+
+    @pl.when(holds)
+    def _():
+        for copy in swaps() + keeps():
+            copy.start()
+
+    to_x.wait_recv()
+    x_to_y = link.send(slot(dx, 0, half), slot(dx, 0, half), dy, z)
+    x_to_k = link.send(slot(dx), slot(dx), dk, z)
+    to_y.wait_recv()
+    y_to_x = link.send(slot(dy, half, half), slot(dy, half, half), dx, z)
+    y_to_k = link.send(slot(dy), slot(dy), dk, z)
+
+    @pl.when(holds)
+    def _():
+        for copy in swaps():
+            copy.wait_send()
+        for copy in keeps():
+            copy.wait()
+
+    @pl.when(jnp.logical_not(holds))
+    def _():
+        for copy in swaps():
+            copy.wait_recv()
+
+    x_ref[...] = xs[...]
+    dy_ref[...] = dys[...]
+    bias_out[...] = bs[...]
+
+    x_to_y.wait_recv()
+    y_to_x.wait_recv()
+    xy_to_k = link.send(slot(dxy), slot(dxy), dk, z)
+    home.wait()
+    to_k.wait_recv()
+    x_to_k.wait_recv()
+    y_to_k.wait_recv()
+    xy_to_k.wait_recv()
+
+    def tile(number):
+        return gath[idx_ref[number]]
+
+    def pick_attn(j, _):
+        lanes = pl.ds(pl.multiple_of(j * TILE, TILE), TILE)
+        for role in range(3):
+            turn[role] = tile(j * 6 + 2 * role + core).T
+        turn[3] = tile(48 + core * 8 + j)
+        for role in range(4):
+            own[0, role * 32 : (role + 1) * 32, lanes] = turn[role, pl.ds(pl.multiple_of(chip * 32, 32), 32), :]
+        return 0
+
+    def pick_feed(j, _):
+        lanes = pl.ds(pl.multiple_of(j * TILE, TILE), TILE)
+        own[1, :, lanes] = tile(64 + j * 8 + 4 * core + chip).T
+        own[2, :, lanes] = tile(128 + (4 * core + chip) * 8 + j)
+        return 0
+
+    def pick_mod(j, _):
+        strip = pl.ds(pl.multiple_of(j * TILE, TILE), TILE)
+        for col in range(12):
+            wmod_ref[strip, col * TILE : (col + 1) * TILE] = tile(192 + j * 12 + col)
+        return 0
+
+    along, by_x, by_y, diag, homes = {}, {}, {}, {}, []
+
+    def send_along(g):
+        for s in (1, 3, 2):
+            along[g, s] = link.send(own.at[g], w_ref.at[g, 0, z], d, lax.rem(z + s, 4))
+
+    def send_plane(g, s):
+        m = lax.rem(z + 4 - s, 4)
+        src = own.at[g] if s == 0 else w_ref.at[g, 0, m]
+        by_x[g, s] = link.send(src, w_ref.at[g, 1, m], dx, z)
+        by_y[g, s] = link.send(src, w_ref.at[g, 2, m], dy, z)
+
+    def send_diag(g, s):
+        m = lax.rem(z + 4 - s, 4)
+        if s < 2:
+            by_x[g, s].wait_recv()
+            diag[g, s] = link.send(w_ref.at[g, 1, m], w_ref.at[g, 3, m], dy, z)
+        else:
+            by_y[g, s].wait_recv()
+            diag[g, s] = link.send(w_ref.at[g, 2, m], w_ref.at[g, 3, m], dx, z)
+
+    def keep_home(g):
+        copy = pltpu.make_async_copy(own.at[g], w_ref.at[g, 0, z], local_sems.at[4 + g])
+        copy.start()
+        homes.append(copy)
+
+    lax.fori_loop(0, 8, pick_attn, 0)
+    lax.fori_loop(0, 8, pick_feed, 0)
+    send_along(0)
+    send_plane(0, 0)
+    keep_home(0)
+    send_along(1)
+    send_along(2)
+    send_plane(1, 0)
+    keep_home(1)
+    keep_home(2)
+
+    lax.fori_loop(0, 8, pick_mod, 0)
+    places = lax.broadcasted_iota(jnp.int32, (32, LEVELS), 1).astype(F32)
+    for owner in range(8):
+        codes = gath[owner * PAYLOAD + LEVEL_TILE][:32].astype(F32)
+        level = codes[:, 0:1] * 32.0 + codes[:, 64:65]
+        hots[owner * 32 : (owner + 1) * 32] = jnp.where(level == places, 1.0, 0.0).astype(BF)
+    own_hot_ref[...] = hots[:, pl.ds(pl.multiple_of(d * TILE, TILE), TILE)]
+    for j in range(TABLE_TILES):
+        strip = jnp.concatenate([gath[owner * PAYLOAD + HEAD_TILES + j] for owner in range(8)], axis=0)
+        emb_ref[:, j * TILE : (j + 1) * TILE] = dot(hots[...], strip, NN).astype(BF)
+    embedded = emb_ref[pl.ds(pl.multiple_of(chip * 64, 64), 64), :]
+    part[...] = dot(embedded, wmod_ref[...], NN).reshape(4, FRAMES, 12 * TILE)
+    modbuf[z] = part[z]
+    shared = {}
+    for s in (1, 3, 2):
+        shared[s] = link.send(part.at[lax.rem(z + s, 4)], modbuf.at[z], d, lax.rem(z + s, 4))
+
+    for s in (1, 3, 2):
+        along[0, s].wait_recv()
+        send_plane(0, s)
+    send_plane(2, 0)
+    for s in (0, 1, 3, 2):
+        send_diag(0, s)
+
+    for s in (1, 3, 2):
+        shared[s].wait_recv()
+    for m in range(4):
+        for c in range(6):
+            mods_ref[:, c, m * 256 : (m + 1) * 256] = modbuf[m, :, c * 256 : (c + 1) * 256]
+
+    def norm_strip(i, _):
+        strip = pl.ds(pl.multiple_of(i * BLK, BLK), BLK)
+        normed, _ = norm_rows(xs[strip].astype(F32))
+        mods = mods_ref[pl.ds(i * FBLK, FBLK)]
+        h_ref[strip] = flat(frames_of(normed) * (1.0 + mods[:, 1:2]) + mods[:, 0:1]).astype(BF)
+        return 0
+
+    lax.fori_loop(0, CLIP // BLK, norm_strip, 0)
+
+    for s in (1, 3, 2):
+        along[1, s].wait_recv()
+        send_plane(1, s)
+    for s in (1, 3, 2):
+        along[2, s].wait_recv()
+        send_plane(2, s)
+    for g in (1, 2):
+        for s in (0, 1, 3, 2):
+            send_diag(g, s)
+    for g in range(3):
+        for s in range(4):
+            (by_y if s < 2 else by_x)[g, s].wait_recv()
+            diag[g, s].wait_recv()
+    for copy in homes:
+        copy.wait()
+    link.drain()
+
+
+def entry(masters, level_table, levels, bias_pair, activations, cotangent, owner_list):
+    slots = masters.shape[0]
+    codes = jnp.stack([levels.reshape(-1) // 32, levels.reshape(-1) % 32], axis=1).astype(BF)
+    codes = jnp.pad(jnp.repeat(codes, 64, axis=1), ((0, TILE - codes.shape[0]), (0, 0)))
+    payload = jnp.concatenate(
+        [
+            masters.astype(BF),
+            level_table.reshape(TILE, TABLE_TILES, TILE).transpose(1, 0, 2),
+            codes[None],
+            jnp.zeros((1, TILE, TILE), BF),
+        ]
+    )
+    position = jnp.arange(owner_list.shape[0], dtype=jnp.int32)
+    place = (position // slots) * PAYLOAD + position % slots
+    index = jnp.sum(
+        jnp.where(owner_list[None, :] == position[:, None], place[None, :], 0), axis=1
+    ).astype(jnp.int32)
+    vmem = pl.BlockSpec(memory_space=pltpu.VMEM)
+    hbm = pl.BlockSpec(memory_space=pl.ANY)
+    return pl.pallas_call(
+        entry_kernel,
+        in_specs=[pl.BlockSpec(memory_space=pltpu.SMEM), hbm, hbm, hbm, hbm],
+        out_specs=[hbm] + [vmem] * 8,
+        out_shape=[
+            jax.ShapeDtypeStruct((3, 4, 4, TILE, D), BF),
+            jax.ShapeDtypeStruct((D, 12 * TILE), BF),
+            jax.ShapeDtypeStruct((CLIP, D), BF),
+            jax.ShapeDtypeStruct((CLIP, D), BF),
+            jax.ShapeDtypeStruct((CLIP, D), BF),
+            jax.ShapeDtypeStruct((FRAMES, 6, D), F32),
+            jax.ShapeDtypeStruct((FRAMES, CLIP), F32),
+            jax.ShapeDtypeStruct((256, D), BF),
+            jax.ShapeDtypeStruct((256, TILE), BF),
+        ],
+        scratch_shapes=[
+            pltpu.VMEM((8 * PAYLOAD, TILE, TILE), BF),
+            pltpu.VMEM((3, TILE, D), BF),
+            pltpu.VMEM((4, TILE, TILE), BF),
+            pltpu.VMEM((CLIP, D), BF),
+            pltpu.VMEM((CLIP, D), BF),
+            pltpu.VMEM((FRAMES, CLIP), F32),
+            pltpu.VMEM((4, FRAMES, 12 * TILE), F32),
+            pltpu.VMEM((4, FRAMES, 12 * TILE), F32),
+            pltpu.VMEM((256, LEVELS), BF),
+            pltpu.SemaphoreType.DMA((ENTRY_COPIES,)),
+            pltpu.SemaphoreType.DMA((ENTRY_COPIES,)),
+            pltpu.SemaphoreType.DMA((3,)),
+            pltpu.SemaphoreType.DMA((3,)),
+            pltpu.SemaphoreType.DMA((7,)),
+        ],
+        compiler_params=params(collective_id=0, has_side_effects=True),
+        cost_estimate=cost(1e9, 40e6),
+        name="entry",
+    )(index, payload, activations, cotangent, bias_pair)
 
 
 QBLK = 256
@@ -628,83 +898,113 @@
         return jnp.stack([v] + [z_get(v, s) for s in range(1, groups)])
 
     def z_reduce(v):
+        if fast:
+            v = lax.dynamic_slice_in_dim(jnp.concatenate([v, v]), z, groups, axis=0)
         total = v[0].astype(F32)
         for s in range(1, groups):
             total = total + z_put(v[s], s).astype(F32)
         return total
 
-    with jax.named_scope("entry"):
-        holds = (z // local_clips) == core
-        local = (z % local_clips) * CLIP
-        pair = jnp.stack(
-            [
-                lax.dynamic_slice_in_dim(activations, local, CLIP, axis=0),
-                lax.dynamic_slice_in_dim(cotangent, local, CLIP, axis=0),
-            ]
-        )
-        pair = jnp.where(holds, pair, across(pair))
-        x, dy = pair[0], pair[1]
-        facts = jnp.concatenate(
-            [context_flags, true_frames[:, None], group_pattern[:, None]], axis=1
-        ).astype(jnp.int32)
-        other = across(facts)
-        facts = jnp.where(
-            core == 0, jnp.concatenate([facts, other]), jnp.concatenate([other, facts])
-        )
-        flagged = facts[:, :FRAMES] == 1
-        frame_index = jnp.arange(FRAMES, dtype=jnp.int32)
-        valid = frame_index[None, :] < facts[:, FRAMES][:, None]
-        pattern_hot = (
-            facts[:, FRAMES + 1][:, None] == jnp.arange(PATTERNS, dtype=jnp.int32)[None, :]
-        ).astype(jnp.int32)
-        levels = jnp.where(
-            flagged, 0, jnp.sum(pattern_hot[:, :, None] * noise_levels[None, :, :], axis=1)
-        )
+    frame_index = jnp.arange(FRAMES, dtype=jnp.int32)
+
+    def mask_rows(flagged, lengths):
+        valid = frame_index[None, :] < lengths[:, None]
         in_context = flagged & valid
         visible = valid[:, :, None] & (
             jnp.logical_not(in_context)[:, None, :] | in_context[:, :, None]
         )
-        visible = lax.dynamic_index_in_dim(visible, z, axis=0, keepdims=False)
-        bias = jnp.repeat(jnp.where(visible, 0.0, -1e30).astype(F32), FRAME_TOK, axis=1)
-        all_levels = plane_double(levels)
-
-    with jax.named_scope("owner_gather"):
-        gathered = lax.all_gather(masters[0].astype(BF), "dp", axis=0, tiled=True)
-        table = lax.all_gather(level_table, "dp", axis=0, tiled=True)
-        position = jnp.arange(owner_list.shape[0], dtype=jnp.int32)
-        inverse = jnp.sum(
-            jnp.where(owner_list[None, :] == position[:, None], position[None, :], 0), axis=1
-        ).astype(jnp.int32)
-        if fast:
-            chunk_attn, chunk_up, chunk_down, w_mod = pick_chunk(gathered, inverse, chip, core)
-        else:
+        return jnp.repeat(jnp.where(visible, 0.0, -1e30).astype(F32), FRAME_TOK, axis=2)
+
+    def level_rows(flagged, patterns):
+        pattern_hot = (patterns[:, None] == jnp.arange(PATTERNS, dtype=jnp.int32)[None, :]).astype(
+            jnp.int32
+        )
+        return jnp.where(
+            flagged, 0, jnp.sum(pattern_hot[:, :, None] * noise_levels[None, :, :], axis=1)
+        )
+
+    rows = TILE // chips
+    level_ids = jnp.arange(LEVELS, dtype=jnp.int32)[None, :]
+    if fast:
+        with jax.named_scope("entry"):
+            flagged = context_flags == 1
+            weights, w_mod, x, dy, h1, mods, bias, all_embedded, own_hot = entry(
+                masters[0],
+                level_table,
+                level_rows(flagged, group_pattern),
+                mask_rows(flagged, true_frames),
+                activations,
+                cotangent,
+                owner_list,
+            )
+            got = weights[0].reshape(chips, groups, 4, rows, D)
+            w_up = weights[1].reshape(-1, D)
+            w_down = weights[2].reshape(-1, D)
+    else:
+        with jax.named_scope("entry"):
+            holds = (z // local_clips) == core
+            local = (z % local_clips) * CLIP
+            pair = jnp.stack(
+                [
+                    lax.dynamic_slice_in_dim(activations, local, CLIP, axis=0),
+                    lax.dynamic_slice_in_dim(cotangent, local, CLIP, axis=0),
+                ]
+            )
+            pair = jnp.where(holds, pair, across(pair))
+            x, dy = pair[0], pair[1]
+            facts = jnp.concatenate(
+                [context_flags, true_frames[:, None], group_pattern[:, None]], axis=1
+            ).astype(jnp.int32)
+            other = across(facts)
+            facts = jnp.where(
+                core == 0, jnp.concatenate([facts, other]), jnp.concatenate([other, facts])
+            )
+            flagged = facts[:, :FRAMES] == 1
+            levels = level_rows(flagged, facts[:, FRAMES + 1])
+            bias = lax.dynamic_index_in_dim(
+                mask_rows(flagged, facts[:, FRAMES]), z, axis=0, keepdims=False
+            )
+            all_levels = plane_double(levels)
+
+        with jax.named_scope("owner_gather"):
+            gathered = lax.all_gather(masters[0].astype(BF), "dp", axis=0, tiled=True)
+            table = lax.all_gather(level_table, "dp", axis=0, tiled=True)
+            position = jnp.arange(owner_list.shape[0], dtype=jnp.int32)
+            inverse = jnp.sum(
+                jnp.where(owner_list[None, :] == position[:, None], position[None, :], 0), axis=1
+            ).astype(jnp.int32)
             chunk_attn, chunk_up, chunk_down, w_mod = pick_chunk_plain(
                 gathered, inverse, chip, core, chips, shapes, counts
             )
 
-    with jax.named_scope("weights"):
-        rows = chunk_attn.shape[0] // 4
-        got = plane_gather(z_gather(chunk_attn)).reshape(chips, groups, 4, rows, D)
-        w_in = got[:, :, :3].transpose(1, 2, 0, 3, 4).reshape(-1, D)
-        w_out = got[:, :, 3].transpose(1, 0, 2, 3).reshape(-1, D)
-        w_up = plane_gather(z_gather(chunk_up)).reshape(-1, D)
-        w_down = plane_gather(z_gather(chunk_down)).reshape(-1, D)
-
-    with jax.named_scope("modulation"):
-        level_ids = jnp.arange(LEVELS, dtype=jnp.int32)[None, :]
-        hot = (levels.reshape(-1)[:, None] == level_ids).astype(BF)
-        embedded = dot(hot, table, NN).astype(BF)
-        mod_part = dot(embedded, w_mod, NN).reshape(column_clips, FRAMES, -1)
-        pieces = [lax.dynamic_index_in_dim(mod_part, z, axis=0, keepdims=False)]
-        for s in range(1, groups):
-            piece = lax.dynamic_index_in_dim(mod_part, (z + groups - s) % groups, axis=0, keepdims=False)
-            pieces.append(z_get(piece, s))
-        mods = lax.dynamic_slice_in_dim(jnp.stack(pieces + pieces), (groups - z) % groups, groups, axis=0)
-        mods = mods.reshape(groups, FRAMES, 6, D // groups).transpose(1, 2, 0, 3).reshape(FRAMES, 6, D)
+        with jax.named_scope("weights"):
+            got = plane_gather(z_gather(chunk_attn)).reshape(chips, groups, 4, rows, D)
+            w_up = plane_gather(z_gather(chunk_up)).reshape(-1, D)
+            w_down = plane_gather(z_gather(chunk_down)).reshape(-1, D)
+
+        with jax.named_scope("modulation"):
+            hot = (levels.reshape(-1)[:, None] == level_ids).astype(BF)
+            embedded = dot(hot, table, NN).astype(BF)
+            mod_part = dot(embedded, w_mod, NN).reshape(column_clips, FRAMES, -1)
+            pieces = [lax.dynamic_index_in_dim(mod_part, z, axis=0, keepdims=False)]
+            for s in range(1, groups):
+                piece = lax.dynamic_index_in_dim(
+                    mod_part, (z + groups - s) % groups, axis=0, keepdims=False
+                )
+                pieces.append(z_get(piece, s))
+            mods = lax.dynamic_slice_in_dim(
+                jnp.stack(pieces + pieces), (groups - z) % groups, groups, axis=0
+            )
+            mods = (
+                mods.reshape(groups, FRAMES, 6, D // groups).transpose(1, 2, 0, 3).reshape(FRAMES, 6, D)
+            )
+            (h1,) = row_call(first_norm_kernel, "first_norm", [x], mods, [BF], [], 4 * CLIP * D)
+
+    w_in = got[:, :, :3].transpose(1, 2, 0, 3, 4).reshape(-1, D)
+    w_out = got[:, :, 3].transpose(1, 0, 2, 3).reshape(-1, D)
 
     mb = CLIP * D
     with jax.named_scope("attention"):
-        (h1,) = row_call(first_norm_kernel, "first_norm", [x], mods, [BF], [], 4 * mb)
         qkv = dot(h1, w_in, NT).astype(BF)
         o_rows, lse = attend(qkv, bias)
         part = dot(o_rows, w_out, TN).astype(BF)
@@ -770,16 +1070,26 @@
         pieces = [lax.dynamic_index_in_dim(d_mod, z, axis=0, keepdims=False)]
         for s in range(1, groups):
             pieces.append(z_put(lax.dynamic_index_in_dim(d_mod, (z + s) % groups, axis=0, keepdims=False), s))
-        d_mod = plane_double(jnp.stack(pieces)).reshape(chips * groups * FRAMES, -1)
-        back_clip = (z + groups - jnp.arange(groups, dtype=jnp.int32)) % groups
-        clip_hot = (back_clip[:, None] == jnp.arange(groups, dtype=jnp.int32)[None, :]).astype(jnp.int32)
-        order = jnp.sum(clip_hot[None, :, :, None] * all_levels[:, None, :, :], axis=2).reshape(-1)
-        all_embedded = dot((order[:, None] == level_ids).astype(BF), table, NN).astype(BF)
+        d_mod = jnp.stack(pieces)
+        if fast:
+            d_mod = lax.dynamic_slice_in_dim(
+                jnp.concatenate([d_mod, d_mod])[::-1], groups - 1 - z, groups, axis=0
+            )
+            d_mod = jnp.take(plane_double(d_mod), jnp.bitwise_xor(jnp.arange(chips), chip), axis=0)
+            d_mod = d_mod.reshape(chips * groups * FRAMES, -1)
+        else:
+            d_mod = plane_double(d_mod).reshape(chips * groups * FRAMES, -1)
+            back_clip = (z + groups - jnp.arange(groups, dtype=jnp.int32)) % groups
+            clip_hot = (back_clip[:, None] == jnp.arange(groups, dtype=jnp.int32)[None, :]).astype(
+                jnp.int32
+            )
+            order = jnp.sum(clip_hot[None, :, :, None] * all_levels[:, None, :, :], axis=2).reshape(-1)
+            all_embedded = dot((order[:, None] == level_ids).astype(BF), table, NN).astype(BF)
+            own_levels = level_table.shape[0]
+            own_ids = device * own_levels + jnp.arange(own_levels, dtype=jnp.int32)[None, :]
+            own_hot = (order[:, None] == own_ids).astype(BF)
         d_w_mod = dot(all_embedded, d_mod, TN).astype(BF)
         own_levels = level_table.shape[0]
-        own_hot = (
-            order[:, None] == device * own_levels + jnp.arange(own_levels, dtype=jnp.int32)[None, :]
-        ).astype(BF)
         own_rows = dot(dot(own_hot, d_mod, TN).astype(BF), w_mod, NT)
         own_rows = own_rows.reshape(groups, own_levels // groups, D)
         table_grad = lax.dynamic_index_in_dim(own_rows, z, axis=0, keepdims=False)

time: 804 us -> 799 us (level)
  Pallas kernels: 168 us -> 358 us
  waiting for transfers between devices: 269 us -> 187 us
  starting transfers between devices: 167 us -> 98.9 us
  other arithmetic: 71.6 us -> 46.3 us
  between operations: 15.6 us -> 1.77 us
    pallas_call x1, Pallas kernels: 7.39 us -> 202 us  [entry(): pl.pallas_call(entry_kernel, in_specs=[pl.BlockSpec(memory_space=pltpu.SM...]
    all_gather x2 -> x0, waiting for transfers between devices: 57.9 us -> none  [the longest x1 41.5 us: body(): gathered = lax.all_gather(masters[0].astype(BF), 'dp', axis=0, tiled=True)]
    ppermute x15, starting transfers between devices: 84.9 us -> 49.8 us  [z_put(): return lax.ppermute(v, 'mp', [(i, (i + s) % groups) for i in range(groups)])]
    ppermute x47 -> x31, waiting for transfers between devices: 106 us -> 76.7 us  [swap(): return lax.ppermute(v, 'dp', [(i, i ^ step) for i in range(owners)])]
    ppermute x18 -> x6, starting transfers between devices: 28.6 us -> 5.83 us  [z_get(): return lax.ppermute(v, 'mp', [((i + s) % groups, i) for i in range(groups)])]
    another operation x9 -> x2, other arithmetic: 19 us -> 3.59 us  [plane_gather(): return jnp.stack([v, by_x, by_y, jnp.concatenate([low, high], axis=0)])]
    ppermute x47 -> x31, starting transfers between devices: 53.3 us -> 43.3 us  [swap(): return lax.ppermute(v, 'dp', [(i, i ^ step) for i in range(owners)])]
    slice x8 -> x2, local copies, waits for them, and re-layouts: 9.44 us -> 0.05 us  [plane_gather(): low, high = (plane(by_x[:half], 1), plane(by_y[half:], 0))]
  transfers between devices with their start and end apart: 82 -> 52, of which waited for: 29 -> 20; matrix products, arithmetic and copies ran while one was open for 20% -> 14% of each run, Pallas kernels for 12% -> 7%
where the time goes in v2:
time: 799 us; the launch traced here: 789 us
  Pallas kernels  358 us (45%)
  waiting for transfers between devices  187 us (23%)
  starting transfers between devices  98.9 us (12%)
  local copies, waits for them, and re-layouts  66.4 us (8%)
  other arithmetic  46.3 us (6%)
  matrix products  30.4 us (4%)
    pallas_call x1, Pallas kernels, entry(): pl.pallas_call(entry_kernel, in_specs=[pl.BlockSpec(memory_space=pltpu.SM...  202 us
    ppermute x6, waiting for transfers between devices, z_get(): return lax.ppermute(v, 'mp', [((i + s) % groups, i) for i in range(groups)])  89 us
    ppermute x31, waiting for transfers between devices, swap(): return lax.ppermute(v, 'dp', [(i, i ^ step) for i in range(owners)])  76.7 us
    ppermute x15, starting transfers between devices, z_put(): return lax.ppermute(v, 'mp', [(i, (i + s) % groups) for i in range(groups)])  49.8 us
    pallas_call x1, Pallas kernels, feed_both(): pl.pallas_call(feed_kernel, grid=(units // UNITS,), in_specs=[whole, whol...  47.3 us
    ppermute x31, starting transfers between devices, swap(): return lax.ppermute(v, 'dp', [(i, i ^ step) for i in range(owners)])  43.3 us
    pallas_call x1, Pallas kernels, attend_back(): pl.pallas_call(attend_back_kernel, grid=(groups,), in_specs=[pl.BlockSpec...  35.3 us
    dot_general x8, matrix products, dot(): lax.dot_general(left, right, (dims, ((), ())), preferred_element_type=F32)  30.4 us
  transfers between devices with their start and end apart: 52, of which 20 were waited for; matrix products, arithmetic and copies ran while one was open for 14% of the time, Pallas kernels for 7%

profile of v2, /device:TPU:1, one launch (start us, length us, event | category | flops | bytes accessed | tf_op | source)
XLA Modules:
  0.0 789.3 jit_solution(11073879800719177234)
XLA Ops:
  10.4 202.2 %entry.1 = (bf16[3,4,4,128,1024]{4,3,2,1,0:T(8,128)(2,1)}, bf16[1024,1536]{1,0:T(8,128)(2,1)}, bf16[1024,1024]{1,0:T(8,128)(2,1)}, bf16[1024,1024]{1,0:T(8,128)(...) custom-call(s32[288]{0:T(512)} %select_reduce_fusion.idx_ref, ...), custom_call_target="tpu_custom_call" | custom-call | flops 1000000000 | bytes 40000000 | tf_op jit(solution)/shard_map/entry/entry/pallas_call | solution.py:510
  212.6 7.7 fusion.68
  227.6 26.7 %attend.1 = (bf16[512,1024]{1,0:T(8,128)(2,1)}, f32[4,2,1024]{2,1,0:T(2,128)}) custom-call(bf16[1024,1536]{1,0:T(8,128)(2,1)} %convolution_convert_fusion.2.qkv_ref, f32[16,1024]{1,0:T(8,128)} %get-tuple-element.39.bias_ref), custom_call_target="tpu_custom_call" | custom-call | flops 6442450944 | bytes 3145728 | tf_op jit(solution)/shard_map/attention/attend/pallas_call | solution.py:575
  261.1 8.0 %middle.1 = (f32[1024,1024]{1,0:T(8,128)}, bf16[1024,1024]{1,0:T(8,128)(2,1)}, bf16[1024,1024]{1,0:T(8,128)(2,1)}, bf16[1024,1024]{1,0:T(8,128)(2,1)}) custom-call(bf16[1024,1024]{1,0:T(8,128)(2,1)} %get-tuple-element.36.x_ref, bf16[1024,1024]{1,0:T(8,128)(2,1)} %copy-done.14, bf16[1024,1024]{1,0:T(8,128)(2,1)} %collective-permute-done.b_ref, ...), custom_call_target="tpu_custom_call" | custom-call | flops 31457280 | bytes 18874368 | tf_op jit(solution)/shard_map/attention/middle/pallas_call | solution.py:157
  269.2 47.3 %feed_both.1 = (bf16[1024,1024]{1,0:T(8,128)(2,1)}, bf16[1024,1024]{1,0:T(8,128)(2,1)}, bf16[2048,1024]{1,0:T(8,128)(2,1)}, bf16[2048,1024]{1,0:T(8,128)(2,1)}) custom-call(bf16[1024,1024]{1,0:T(8,128)(2,1)} %get-tuple-element.44.h_ref, bf16[1024,1024]{1,0:T(8,128)(2,1)} %get-tuple-element.45.de_ref, bf16[2048,1024]{1,0:T(8,128)(2,1)} %bitcast.293, ...), custom_call_target="tpu_custom_call" | custom-call | flops 25769803776 | bytes 25165824 | tf_op jit(solution)/shard_map/feed/feed_both/pallas_call | solution.py:701
  324.7 7.7 collective-permute-done.42
  336.0 19.0 %collective-permute-done.33 = bf16[2,128,1024]{2,1,0:T(8,128)(2,1)} collective-permute-done((bf16[2,128,1024]{2,1,0:T(8,128)(2,1)}, bf16[2,128,1024]{2,1,0:T(8,128)(2,1)}, u32[]{:S(2)}, u32[]{:S(2)}) %collective-permute-start.33) | collective-permute-done | bytes 524320 | tf_op jit(solution)/shard_map/feed/ppermute | solution.py:850
  368.3 9.6 %collective-permute-done.34 = bf16[2,128,1024]{2,1,0:T(8,128)(2,1)S(1)} collective-permute-done((bf16[2,128,1024]{2,1,0:T(8,128)(2,1)S(1)}, bf16[2,128,1024]{2,1,0:T(8,128)(2,1)S(1)}, u32[]{:S(2)}, u32[]{:S(2)}) %collective-permute-start.34) | collective-permute-done | bytes 524320 | tf_op jit(solution)/shard_map/feed/ppermute | solution.py:850
  380.5 8.6 %collective-permute-done.38 = bf16[2,128,1024]{2,1,0:T(8,128)(2,1)S(1)} collective-permute-done((bf16[2,128,1024]{2,1,0:T(8,128)(2,1)S(1)}, bf16[2,128,1024]{2,1,0:T(8,128)(2,1)S(1)}, u32[]{:S(2)}, u32[]{:S(2)}) %collective-permute-start.38) | collective-permute-done | bytes 524320 | tf_op jit(solution)/shard_map/feed/ppermute | solution.py:850
  393.0 7.4 collective-permute-done.29
  407.1 11.3 %back.1 = (bf16[1024,1024]{1,0:T(8,128)(2,1)}, f32[1024,1024]{1,0:T(8,128)}, bf16[1024,1024]{1,0:T(8,128)(2,1)}, f32[16,4,1024]{2,1,0:T(4,128)}) custom-call(f32[1024,1024]{1,0:T(8,128)} %get-tuple-element.43.y_ref, bf16[1024,1024]{1,0:T(8,128)(2,1)} %get-tuple-element.46.g_ref, bf16[1024,1024]{1,0:T(8,128)(2,1)} %collective-permute-done.1.gp_ref, ...), custom_call_target="tpu_custom_call" | custom-call | flops 31457280 | bytes 25165824 | tf_op jit(solution)/shard_map/feed/back/pallas_call | solution.py:157
  422.3 35.3 %attend_back.1 = bf16[1024,1536]{1,0:T(8,128)(2,1)} custom-call(bf16[1024,1536]{1,0:T(8,128)(2,1)} %convolution_convert_fusion.2.qkv_ref, bf16[512,1024]{1,0:T(8,128)(2,1)} %get-tuple-element.40.o_ref, bf16[512,1024]{1,0:T(8,128)(2,1)} %convolution_convert_fusion.7.do_ref, f32[4,2,1024]{2,1,0:T(2,128)} %get-tuple-element.51.lse_ref, ...), custom_call_target="tpu_custom_call" | custom-call | flops 16106127360 | bytes 6291456 | tf_op jit(solution)/shard_map/attention_back/attend_back/pallas_call | solution.py:630
  457.6 6.2 convolution_convert_fusion.1
  481.4 9.0 %collective-permute-done.23 = bf16[2,128,1024]{2,1,0:T(8,128)(2,1)S(1)} collective-permute-done((bf16[2,128,1024]{2,1,0:T(8,128)(2,1)S(1)}, bf16[2,128,1024]{2,1,0:T(8,128)(2,1)S(1)}, u32[]{:S(2)}, u32[]{:S(2)}) %collective-permute-start.23) | collective-permute-done | bytes 524320 | tf_op jit(solution)/shard_map/attention_back/ppermute | solution.py:850
  497.8 6.8 collective-permute-done.25
  504.6 8.2 %collective-permute-start.7 = (bf16[1024,1024]{1,0:T(8,128)(2,1)}, bf16[1024,1024]{1,0:T(8,128)(2,1)}, u32[]{:S(2)}, u32[]{:S(2)}) collective-permute-start(bf16[1024,1024]{1,0:T(8,128)(2,1)} %convolution_convert_fusion.4.g_ref), channel_id=1, source_target_pairs={{0,4},{4,0},{8,12},{12,8},{16,20},{20,16},{24,28},{28,24},{1,5},{5... | collective-permute-start | bytes 6291464 | tf_op jit(solution)/shard_map/attention_back/ppermute | solution.py:850
  514.9 24.1 %collective-permute-done.3 = bf16[512,1024]{1,0:T(8,128)(2,1)} collective-permute-done((bf16[512,1024]{1,0:T(8,128)(2,1)}, bf16[512,1024]{1,0:T(8,128)(2,1)}, u32[]{:S(2)}, u32[]{:S(2)}) %collective-permute-start.3) | collective-permute-done | bytes 1048608 | tf_op jit(solution)/shard_map/block_output/ppermute | solution.py:859
  556.0 29.3 %collective-permute-start.26 = (bf16[128,1024]{1,0:T(8,128)(2,1)S(1)}, bf16[128,1024]{1,0:T(8,128)(2,1)S(1)}, u32[]{:S(2)}, u32[]{:S(2)}) collective-permute-start(bf16[128,1024]{1,0:T(8,128)(2,1)S(1)} %get-tuple-element.102), channel_id=1, source_target_pairs={{0,1},{1,2},{2,3},{3,0},{4,5},{5,6},{6,7},{7,4},{8,9},{9,10},{10,1... | collective-permute-start | bytes 786440 | tf_op jit(solution)/shard_map/attention_back/ppermute | solution.py:862
  589.6 10.2 %collective-permute-done.27 = bf16[128,1024]{1,0:T(8,128)(2,1)S(1)} collective-permute-done((bf16[128,1024]{1,0:T(8,128)(2,1)S(1)}, bf16[128,1024]{1,0:T(8,128)(2,1)S(1)}, u32[]{:S(2)}, u32[]{:S(2)}) %collective-permute-start.27) | collective-permute-done | bytes 262176 | tf_op jit(solution)/shard_map/attention_back/ppermute | solution.py:862
  604.3 7.5 last.1
  614.1 8.7 %collective-permute-start.14 = (bf16[16,1536]{1,0:T(8,128)(2,1)S(1)}, bf16[16,1536]{1,0:T(8,128)(2,1)S(1)}, u32[]{:S(2)}, u32[]{:S(2)}) collective-permute-start(bf16[16,1536]{1,0:T(8,128)(2,1)S(1)} %get-tuple-element.117), channel_id=1, source_target_pairs={{0,3},{1,0},{2,1},{3,2},{4,7},{5,4},{6,5},{7,6},{8,11},{9,8},{10,9... | collective-permute-start | bytes 147464 | tf_op jit(solution)/shard_map/modulation_back/ppermute | solution.py:862
  657.4 60.0 %collective-permute-done.9 = bf16[512,1024]{1,0:T(8,128)(2,1)S(1)} collective-permute-done((bf16[512,1024]{1,0:T(8,128)(2,1)}, bf16[512,1024]{1,0:T(8,128)(2,1)S(1)}, u32[]{:S(2)}, u32[]{:S(2)}) %collective-permute-start.9) | collective-permute-done | bytes 1048608 | tf_op jit(solution)/shard_map/input_grad/ppermute | solution.py:859
  751.6 5.2 maximum_select_fusion
  768.6 20.2 %adam.1 = (f32[36,128,128]{2,1,0:T(8,128)}, f32[36,128,128]{2,1,0:T(8,128)}, f32[36,128,128]{2,1,0:T(8,128)}, bf16[36,128,128]{2,1,0:T(8,128)(2,1)}) custom-call(s32[36,12]{1,0:T(8,128)} %copy.73.tab_ref, f32[36]{0:T(128)} %get-tuple-element.67.rate_ref, bf16[8,384,1024]{2,1,0:T(8,128)(2,1)} %bitcast.268, ...), custom_call_target="tpu_custom_call" | custom-call | flops 603979776 | bytes 21233664 | tf_op jit(solution)/shard_map/owners/adam/pallas_call | solution.py:804
  (279 shorter events, 201.3 us)
Async XLA Ops:
  321.2 36.0 %collective-permute-start.41 = (bf16[2,128,1024]{2,1,0:T(8,128)(2,1)}, bf16[2,128,1024]{2,1,0:T(8,128)(2,1)S(1)}, u32[]{:S(2)}, u32[]{:S(2)}) collective-permute-start(bf16[2,128,1024]{2,1,0:T(8,128)(2,1)} %get-tuple-element.98), channel_id=1, source_target_pairs={{0,16},{4,20},{8,24},{12,28},{16,0},{20,4},{24,8},{28,12},{1,17},{... | collective-permute-start | bytes 1572872 | tf_op jit(solution)/shard_map/feed/ppermute | solution.py:850
  321.9 37.6 %collective-permute-start.39 = (bf16[2,128,1024]{2,1,0:T(8,128)(2,1)}, bf16[2,128,1024]{2,1,0:T(8,128)(2,1)S(1)}, u32[]{:S(2)}, u32[]{:S(2)}) collective-permute-start(bf16[2,128,1024]{2,1,0:T(8,128)(2,1)} %get-tuple-element.100), channel_id=1, source_target_pairs={{0,8},{4,12},{8,0},{12,4},{16,24},{20,28},{24,16},{28,20},{1,9},{5... | collective-permute-start | bytes 1572872 | tf_op jit(solution)/shard_map/feed/ppermute | solution.py:850
  324.0 31.0 %collective-permute-start.33 = (bf16[2,128,1024]{2,1,0:T(8,128)(2,1)}, bf16[2,128,1024]{2,1,0:T(8,128)(2,1)}, u32[]{:S(2)}, u32[]{:S(2)}) collective-permute-start(bf16[2,128,1024]{2,1,0:T(8,128)(2,1)} %get-tuple-element.93), channel_id=1, source_target_pairs={{0,16},{4,20},{8,24},{12,28},{16,0},{20,4},{24,8},{28,12},{1,17},{... | collective-permute-start | bytes 1572872 | tf_op jit(solution)/shard_map/feed/ppermute | solution.py:850
  335.3 30.8 %collective-permute-start.32 = (bf16[2,128,1024]{2,1,0:T(8,128)(2,1)}, bf16[2,128,1024]{2,1,0:T(8,128)(2,1)S(1)}, u32[]{:S(2)}, u32[]{:S(2)}) collective-permute-start(bf16[2,128,1024]{2,1,0:T(8,128)(2,1)} %get-tuple-element.92), channel_id=1, source_target_pairs={{0,16},{4,20},{8,24},{12,28},{16,0},{20,4},{24,8},{28,12},{1,17},{... | collective-permute-start | bytes 1572872 | tf_op jit(solution)/shard_map/feed/ppermute | solution.py:850
  357.2 48.2 %collective-permute-start.1 = (bf16[1024,1024]{1,0:T(8,128)(2,1)}, bf16[1024,1024]{1,0:T(8,128)(2,1)}, u32[]{:S(2)}, u32[]{:S(2)}) collective-permute-start(bf16[1024,1024]{1,0:T(8,128)(2,1)} %get-tuple-element.46.g_ref), channel_id=1, source_target_pairs={{0,4},{4,0},{8,12},{12,8},{16,20},{20,16},{24,28},{28,24},{1,5},{5... | collective-permute-start | bytes 6291464 | tf_op jit(solution)/shard_map/feed/ppermute | solution.py:850
  359.4 46.2 %collective-permute-start.2 = (bf16[1024,1024]{1,0:T(8,128)(2,1)}, bf16[1024,1024]{1,0:T(8,128)(2,1)}, u32[]{:S(2)}, u32[]{:S(2)}) collective-permute-start(bf16[1024,1024]{1,0:T(8,128)(2,1)} %get-tuple-element.48.e_ref), channel_id=1, source_target_pairs={{0,4},{4,0},{8,12},{12,8},{16,20},{20,16},{24,28},{28,24},{1,5},{5... | collective-permute-start | bytes 6291464 | tf_op jit(solution)/shard_map/feed/ppermute | solution.py:850
  393.0 73.2 %collective-permute-start.44 = (bf16[128,1024]{1,0:T(8,128)(2,1)}, bf16[128,1024]{1,0:T(8,128)(2,1)S(1)}, u32[]{:S(2)}, u32[]{:S(2)}) collective-permute-start(bf16[128,1024]{1,0:T(8,128)(2,1)} %get-tuple-element.108), channel_id=1, source_target_pairs={{0,1},{1,2},{2,3},{3,0},{4,5},{5,6},{6,7},{7,4},{8,9},{9,10},{10,1... | collective-permute-start | bytes 786440 | tf_op jit(solution)/shard_map/feed/ppermute | solution.py:862
  400.4 69.2 %collective-permute-start.45 = (bf16[128,1024]{1,0:T(8,128)(2,1)}, bf16[128,1024]{1,0:T(8,128)(2,1)S(1)}, u32[]{:S(2)}, u32[]{:S(2)}) collective-permute-start(bf16[128,1024]{1,0:T(8,128)(2,1)} %get-tuple-element.109), channel_id=1, source_target_pairs={{0,2},{1,3},{2,0},{3,1},{4,6},{5,7},{6,4},{7,5},{8,10},{9,11},{10,... | collective-permute-start | bytes 786440 | tf_op jit(solution)/shard_map/feed/ppermute | solution.py:862
  400.4 70.4 %collective-permute-start.46 = (bf16[128,1024]{1,0:T(8,128)(2,1)}, bf16[128,1024]{1,0:T(8,128)(2,1)S(1)}, u32[]{:S(2)}, u32[]{:S(2)}) collective-permute-start(bf16[128,1024]{1,0:T(8,128)(2,1)} %get-tuple-element.110), channel_id=1, source_target_pairs={{0,3},{1,0},{2,1},{3,2},{4,7},{5,4},{6,5},{7,6},{8,11},{9,8},{10,9... | collective-permute-start | bytes 786440 | tf_op jit(solution)/shard_map/feed/ppermute | solution.py:862
  405.4 65.9 %collective-permute-start.35 = (bf16[128,1024]{1,0:T(8,128)(2,1)}, bf16[128,1024]{1,0:T(8,128)(2,1)}, u32[]{:S(2)}, u32[]{:S(2)}) collective-permute-start(bf16[128,1024]{1,0:T(8,128)(2,1)} %get-tuple-element.105), channel_id=1, source_target_pairs={{0,1},{1,2},{2,3},{3,0},{4,5},{5,6},{6,7},{7,4},{8,9},{9,10},{10,1... | collective-permute-start | bytes 786440 | tf_op jit(solution)/shard_map/feed/ppermute | solution.py:862
  405.6 65.6 %collective-permute-start.36 = (bf16[128,1024]{1,0:T(8,128)(2,1)}, bf16[128,1024]{1,0:T(8,128)(2,1)}, u32[]{:S(2)}, u32[]{:S(2)}) collective-permute-start(bf16[128,1024]{1,0:T(8,128)(2,1)} %get-tuple-element.106), channel_id=1, source_target_pairs={{0,2},{1,3},{2,0},{3,1},{4,6},{5,7},{6,4},{7,5},{8,10},{9,11},{10,... | collective-permute-start | bytes 786440 | tf_op jit(solution)/shard_map/feed/ppermute | solution.py:862
  475.2 73.1 %collective-permute-start.5 = (bf16[512,1024]{1,0:T(8,128)(2,1)}, bf16[512,1024]{1,0:T(8,128)(2,1)S(1)}, u32[]{:S(2)}, u32[]{:S(2)}) collective-permute-start(bf16[512,1024]{1,0:T(8,128)(2,1)} %get-tuple-element.74), channel_id=1, source_target_pairs={{3,0},{0,1},{1,2},{2,3},{7,4},{4,5},{5,6},{6,7},{11,8},{8,9},{9,10... | collective-permute-start | bytes 3145736 | tf_op jit(solution)/shard_map/block_output/ppermute | solution.py:859
  476.2 71.1 %collective-permute-start.4 = (bf16[512,1024]{1,0:T(8,128)(2,1)}, bf16[512,1024]{1,0:T(8,128)(2,1)S(1)}, u32[]{:S(2)}, u32[]{:S(2)}) collective-permute-start(bf16[512,1024]{1,0:T(8,128)(2,1)} %get-tuple-element.74), channel_id=1, source_target_pairs={{2,0},{3,1},{0,2},{1,3},{6,4},{7,5},{4,6},{5,7},{10,8},{11,9},{8,1... | collective-permute-start | bytes 3145736 | tf_op jit(solution)/shard_map/block_output/ppermute | solution.py:859
  478.6 60.4 %collective-permute-start.3 = (bf16[512,1024]{1,0:T(8,128)(2,1)}, bf16[512,1024]{1,0:T(8,128)(2,1)}, u32[]{:S(2)}, u32[]{:S(2)}) collective-permute-start(bf16[512,1024]{1,0:T(8,128)(2,1)} %get-tuple-element.74), channel_id=1, source_target_pairs={{1,0},{2,1},{3,2},{0,3},{5,4},{6,5},{7,6},{4,7},{9,8},{10,9},{11,1... | collective-permute-start | bytes 3145736 | tf_op jit(solution)/shard_map/block_output/ppermute | solution.py:859
  497.5 56.4 %collective-permute-start.20 = (bf16[2,128,1024]{2,1,0:T(8,128)(2,1)}, bf16[2,128,1024]{2,1,0:T(8,128)(2,1)S(1)}, u32[]{:S(2)}, u32[]{:S(2)}) collective-permute-start(bf16[2,128,1024]{2,1,0:T(8,128)(2,1)} %get-tuple-element.89), channel_id=1, source_target_pairs={{0,8},{4,12},{8,0},{12,4},{16,24},{20,28},{24,16},{28,20},{1,9},{5... | collective-permute-start | bytes 1572872 | tf_op jit(solution)/shard_map/attention_back/ppermute | solution.py:850
  504.6 99.7 %collective-permute-start.7 = (bf16[1024,1024]{1,0:T(8,128)(2,1)}, bf16[1024,1024]{1,0:T(8,128)(2,1)}, u32[]{:S(2)}, u32[]{:S(2)}) collective-permute-start(bf16[1024,1024]{1,0:T(8,128)(2,1)} %convolution_convert_fusion.4.g_ref), channel_id=1, source_target_pairs={{0,4},{4,0},{8,12},{12,8},{16,20},{20,16},{24,28},{28,24},{1,5},{5... | collective-permute-start | bytes 6291464 | tf_op jit(solution)/shard_map/attention_back/ppermute | solution.py:850
  556.0 33.6 %collective-permute-start.26 = (bf16[128,1024]{1,0:T(8,128)(2,1)S(1)}, bf16[128,1024]{1,0:T(8,128)(2,1)S(1)}, u32[]{:S(2)}, u32[]{:S(2)}) collective-permute-start(bf16[128,1024]{1,0:T(8,128)(2,1)S(1)} %get-tuple-element.102), channel_id=1, source_target_pairs={{0,1},{1,2},{2,3},{3,0},{4,5},{5,6},{6,7},{7,4},{8,9},{9,10},{10,1... | collective-permute-start | bytes 786440 | tf_op jit(solution)/shard_map/attention_back/ppermute | solution.py:862
  602.8 34.2 %collective-permute-start.48 = (bf16[2,192,1024]{2,1,0:T(8,128)(2,1)}, bf16[2,192,1024]{2,1,0:T(8,128)(2,1)S(1)}, u32[]{:S(2)}, u32[]{:S(2)}) collective-permute-start(bf16[2,192,1024]{2,1,0:T(8,128)(2,1)} %bitcast.93), channel_id=1, source_target_pairs={{0,16},{4,20},{8,24},{12,28},{16,0},{20,4},{24,8},{28,12},{1,17},{... | collective-permute-start | bytes 2359304 | tf_op jit(solution)/shard_map/owners/ppermute | solution.py:850
  603.8 33.8 %collective-permute-start.47 = (bf16[2,192,1024]{2,1,0:T(8,128)(2,1)}, bf16[2,192,1024]{2,1,0:T(8,128)(2,1)S(1)}, u32[]{:S(2)}, u32[]{:S(2)}) collective-permute-start(bf16[2,192,1024]{2,1,0:T(8,128)(2,1)} %bitcast.93), channel_id=1, source_target_pairs={{0,8},{4,12},{8,0},{12,4},{16,24},{20,28},{24,16},{28,20},{1,9},{5... | collective-permute-start | bytes 2359304 | tf_op jit(solution)/shard_map/owners/ppermute | solution.py:850
  636.4 81.1 %collective-permute-start.9 = (bf16[512,1024]{1,0:T(8,128)(2,1)}, bf16[512,1024]{1,0:T(8,128)(2,1)S(1)}, u32[]{:S(2)}, u32[]{:S(2)}) collective-permute-start(bf16[512,1024]{1,0:T(8,128)(2,1)} %get-tuple-element.72), channel_id=1, source_target_pairs={{2,0},{3,1},{0,2},{1,3},{6,4},{7,5},{4,6},{5,7},{10,8},{11,9},{8,1... | collective-permute-start | bytes 3145736 | tf_op jit(solution)/shard_map/input_grad/ppermute | solution.py:859
  643.7 107.8 %collective-permute-start.6 = (bf16[2,512,1024]{2,1,0:T(8,128)(2,1)}, bf16[2,512,1024]{2,1,0:T(8,128)(2,1)}, u32[]{:S(2)}, u32[]{:S(2)}) collective-permute-start(bf16[2,512,1024]{2,1,0:T(8,128)(2,1)} %get-tuple-element.83), channel_id=1, source_target_pairs={{0,4},{4,0},{8,12},{12,8},{16,20},{20,16},{24,28},{28,24},{1,5},{5... | collective-permute-start | bytes 6291464 | tf_op jit(solution)/shard_map/block_output/ppermute | solution.py:850
  648.5 69.0 %collective-permute-start.10 = (bf16[512,1024]{1,0:T(8,128)(2,1)}, bf16[512,1024]{1,0:T(8,128)(2,1)S(1)}, u32[]{:S(2)}, u32[]{:S(2)}) collective-permute-start(bf16[512,1024]{1,0:T(8,128)(2,1)} %get-tuple-element.72), channel_id=1, source_target_pairs={{3,0},{0,1},{1,2},{2,3},{7,4},{4,5},{5,6},{6,7},{11,8},{8,9},{9,10... | collective-permute-start | bytes 3145736 | tf_op jit(solution)/shard_map/input_grad/ppermute | solution.py:859
  649.6 77.8 %collective-permute-start.16 = (bf16[2,4,16,1536]{3,2,1,0:T(8,128)(2,1)S(1)}, bf16[2,4,16,1536]{3,2,1,0:T(8,128)(2,1)S(1)}, u32[]{:S(2)}, u32[]{:S(2)}) collective-permute-start(bf16[2,4,16,1536]{3,2,1,0:T(8,128)(2,1)S(1)} %pad_maximum_fusion.5), channel_id=1, source_target_pairs={{0,16},{4,20},{8,24},{12,28},{16,0},{20,4},{24,8},{28,12},{1,17},{... | collective-permute-start | bytes 1179656 | tf_op jit(solution)/shard_map/modulation_back/ppermute | solution.py:850
  652.1 111.4 %collective-permute-start.51 = (bf16[4,384,1024]{2,1,0:T(8,128)(2,1)}, bf16[4,384,1024]{2,1,0:T(8,128)(2,1)}, u32[]{:S(2)}, u32[]{:S(2)}) collective-permute-start(bf16[4,384,1024]{2,1,0:T(8,128)(2,1)} %pad_maximum_fusion.2), channel_id=1, source_target_pairs={{0,4},{4,0},{8,12},{12,8},{16,20},{20,16},{24,28},{28,24},{1,5},{5... | collective-permute-start | bytes 9437192 | tf_op jit(solution)/shard_map/owners/ppermute | solution.py:850
  (61 other events, 768.0 us)

commit v3 on v2

--- a/solution.py
+++ b/solution.py
@@ -716,6 +716,574 @@
     )(hidden, grad, up, down)
 
 
+HALF = CLIP // 2
+EXIT_COPIES = 8 + 1 + 18 + 9 + 24 + 12 + 6 + 14
+EXIT_LOCAL = 32
+
+
+class Relay:
+    def __init__(self, sends, recvs, local, src, full, d, z):
+        self.sends, self.recvs, self.local = sends, recvs, local
+        self.src, self.full, self.d, self.z = src, full, d, z
+        self.core = lax.rem(d, 2)
+
+    def place(self, clip, first, count):
+        start = pl.multiple_of(lax.rem(clip, 2) * CLIP + first * HALF, HALF)
+        return self.full.at[pl.ds(start, count)]
+
+    def copy(self, src, clip, half, way, hop):
+        index = way * 6 + (hop - 1) * 2 + half
+        return pltpu.make_async_remote_copy(
+            src_ref=src,
+            dst_ref=self.place(clip, half, HALF),
+            send_sem=self.sends.at[index],
+            recv_sem=self.recvs.at[index],
+            device_id=(self.d - self.core + clip // 2, lax.rem(self.z + (1 if way == 0 else 3), 4)),
+            device_id_type=MESH,
+        )
+
+    def more(self, way):
+        return self.z < 3 if way == 0 else self.z > 0
+
+    def own(self, way):
+        part = self.src.at[pl.ds(pl.multiple_of(self.core * HALF, HALF), HALF)]
+        return self.copy(part, self.z, self.core, way, 1)
+
+    def home(self):
+        return pltpu.make_async_copy(self.src, self.place(self.z, 0, CLIP), self.local)
+
+    def first(self):
+        for way in range(2):
+
+            @pl.when(self.more(way))
+            def _(way=way):
+                self.own(way).start()
+
+        @pl.when(self.z // 2 == self.core)
+        def _():
+            self.home().start()
+
+    def arriving(self, way, hop):
+        clip = lax.rem(self.z + (4 - hop if way == 0 else hop), 4)
+        there = self.z >= hop if way == 0 else self.z + hop <= 3
+        return clip, jnp.logical_and(there, clip // 2 == self.core)
+
+    def hop(self, hop):
+        for way in range(2):
+            clip, here = self.arriving(way, hop)
+
+            @pl.when(here)
+            def _(way=way, clip=clip):
+                for half in range(2):
+                    part = self.place(clip, half, HALF)
+                    self.copy(part, clip, half, way, hop).wait_recv()
+                    if hop < 3:
+
+                        @pl.when(self.more(way))
+                        def _(part=part, half=half):
+                            self.copy(part, clip, half, way, hop + 1).start()
+
+    def finish(self):
+        for way in range(2):
+
+            @pl.when(self.more(way))
+            def _(way=way):
+                self.own(way).wait_send()
+
+            for hop in (1, 2):
+                clip, here = self.arriving(way, hop)
+
+                @pl.when(jnp.logical_and(here, self.more(way)))
+                def _(way=way, clip=clip, hop=hop):
+                    for half in range(2):
+                        self.copy(self.place(clip, half, HALF), clip, half, way, hop + 1).wait_send()
+
+        @pl.when(self.z // 2 == self.core)
+        def _():
+            self.home().wait()
+
+
+def exit_kernel(
+    y_hbm,
+    g_hbm,
+    e_hbm,
+    dy_hbm,
+    br_hbm,
+    x_hbm,
+    h_hbm,
+    qkv_hbm,
+    o_hbm,
+    win_hbm,
+    wout_hbm,
+    wmod_hbm,
+    up_hbm,
+    down_hbm,
+    mods_ref,
+    bias_ref,
+    lse_ref,
+    emb_ref,
+    hot_ref,
+    out_all,
+    in_all,
+    everyone,
+    dwm_out,
+    table_ref,
+    ys,
+    gs,
+    es,
+    dys,
+    brs,
+    gp,
+    ep,
+    qs,
+    os_,
+    dos,
+    win,
+    wout,
+    dhp,
+    dattn,
+    got,
+    loc,
+    zbuf,
+    red,
+    dm,
+    dms,
+    dmall,
+    trow,
+    tbuf,
+    dk_ref,
+    dv_ref,
+    sends,
+    recvs,
+    strip_sends,
+    strip_recvs,
+    out_sends,
+    out_recvs,
+    in_sends,
+    in_recvs,
+    local_sems,
+):
+    d, z = lax.axis_index("dp"), lax.axis_index("mp")
+    core, chip = lax.rem(d, 2), d // 2
+    dk, dx, dyd = jnp.bitwise_xor(d, 1), jnp.bitwise_xor(d, 2), jnp.bitwise_xor(d, 4)
+    link = Link(sends, recvs)
+    locals_used = [0]
+
+    def load(src, dst):
+        copy = pltpu.make_async_copy(src, dst, local_sems.at[locals_used[0]])
+        locals_used[0] += 1
+        copy.start()
+        return copy
+
+    barrier = pltpu.get_barrier_semaphore()
+    for step in (1, 2, 4):
+        pl.semaphore_signal(barrier, inc=1, device_id=(jnp.bitwise_xor(d, step), z), device_id_type=MESH)
+    for s in (1, 2, 3):
+        pl.semaphore_signal(barrier, inc=1, device_id=(d, lax.rem(z + s, 4)), device_id_type=MESH)
+        pl.semaphore_signal(barrier, inc=1, device_id=(dk, lax.rem(z + s, 4)), device_id_type=MESH)
+
+    first_loads = [load(a, b) for a, b in ((g_hbm, gs), (e_hbm, es), (y_hbm, ys), (dy_hbm, dys), (br_hbm, brs))]
+    loads = [load(a, b) for a, b in ((o_hbm, os_), (wout_hbm, wout), (win_hbm, win))]
+    loads += [load(qkv_hbm.at[:, m * 384 : (m + 1) * 384], qs.at[m]) for m in range(4)]
+    feed_loads = []
+    for g, src in enumerate((up_hbm, down_hbm)):
+        feed_loads.append(load(src.at[0], loc.at[g, 0:4]))
+        feed_loads.append(load(src.at[2, 0:2], loc.at[g, 4:6]))
+        feed_loads.append(load(src.at[1, 2:4], loc.at[g, 6:8]))
+    pl.semaphore_wait(barrier, 9)
+
+    def strip_of(i):
+        return pl.ds(pl.multiple_of(i * BLK, BLK), BLK)
+
+    def swaps(i):
+        return [
+            pltpu.make_async_remote_copy(
+                src_ref=src.at[strip_of(i)],
+                dst_ref=dst.at[strip_of(i)],
+                send_sem=strip_sends.at[2 * i + k],
+                recv_sem=strip_recvs.at[2 * i + k],
+                device_id=(dk, z),
+                device_id_type=MESH,
+            )
+            for k, (src, dst) in enumerate(((g_hbm, gp), (e_hbm, ep)))
+        ]
+
+    def swap_start(i, _):
+        for copy in swaps(i):
+            copy.start()
+        return 0
+
+    lax.fori_loop(0, CLIP // BLK, swap_start, 0)
+
+    plane = {}
+
+    def plane_first(g, src):
+        plane[g, 0] = link.send(src.at[3, 0:2], got.at[g, 0], dx, z)
+        plane[g, 1] = link.send(src.at[3, 2:4], got.at[g, 1], dyd, z)
+        plane[g, 2] = link.send(src.at[1, 0:2], got.at[g, 2], dx, z)
+        plane[g, 3] = link.send(src.at[2, 2:4], got.at[g, 3], dyd, z)
+
+    def add_into(dst, first, count, parts):
+        def step(i, _):
+            k = i // 4
+            rows = pl.ds(pl.multiple_of(lax.rem(i, 4) * 32, 32), 32)
+            total = dst[first + k, rows].astype(F32)
+            for g, slot in parts:
+                total = total + got[g, slot, k, rows].astype(F32)
+            dst[first + k, rows] = total.astype(BF)
+            return 0
+
+        lax.fori_loop(0, count * 4, step, 0)
+
+    def places(g):
+        if g == 0:
+            return (dattn.at[0], 0), (dattn.at[2], 0), (dattn.at[1], 2)
+        return (loc.at[g - 1], 0), (loc.at[g - 1], 4), (loc.at[g - 1], 6)
+
+    def plane_pass(g):
+        _, (low, low_at), (high, high_at) = places(g)
+        plane[g, 0].wait_recv()
+        add_into(low, low_at, 2, [(g, 0)])
+        plane[g, 4] = link.send(low.at[pl.ds(low_at, 2)], got.at[g, 4], dyd, z)
+        plane[g, 1].wait_recv()
+        add_into(high, high_at, 2, [(g, 1)])
+        plane[g, 5] = link.send(high.at[pl.ds(high_at, 2)], got.at[g, 5], dx, z)
+
+    column = {}
+
+    def plane_final(g):
+        (own, _), _, _ = places(g)
+        for slot in (2, 3, 4, 5):
+            plane[g, slot].wait_recv()
+        add_into(own, 0, 2, [(g, 2), (g, 4)])
+        add_into(own, 2, 2, [(g, 3), (g, 5)])
+        for s in (1, 3, 2):
+            to = lax.rem(z + s, 4)
+            column[g, s] = link.send(own.at[to], zbuf.at[g, s - 1], d, to)
+
+    spread = {}
+    homes = []
+
+    def column_final(g):
+        (own, _), _, _ = places(g)
+        for s in (1, 3, 2):
+            column[g, s].wait_recv()
+
+        def step(i, _):
+            rows = pl.ds(pl.multiple_of(i * 32, 32), 32)
+            total = own[z, rows].astype(F32)
+            for s in range(3):
+                total = total + zbuf[g, s, rows].astype(F32)
+            red[g, rows] = total.astype(BF)
+            return 0
+
+        lax.fori_loop(0, 4, step, 0)
+        rows = pl.ds(g * TILE, TILE)
+        spread[g, 2] = link.send(red.at[g], everyone.at[2, rows], dx, z)
+        spread[g, 4] = link.send(red.at[g], everyone.at[4, rows], dyd, z)
+        spread[g, 1] = link.send(red.at[g], everyone.at[1, rows], dk, z)
+        homes.append(load(red.at[g], everyone.at[0, rows]))
+
+    def spread_on(g):
+        rows = pl.ds(g * TILE, TILE)
+        low, high = pl.ds(g * TILE, TILE // 2), pl.ds(g * TILE + TILE // 2, TILE // 2)
+        spread[g, 2].wait_recv()
+        spread[g, 6] = link.send(everyone.at[2, low], everyone.at[6, low], dyd, z)
+        spread[g, 3] = link.send(everyone.at[2, rows], everyone.at[3, rows], dk, z)
+        spread[g, 4].wait_recv()
+        spread[g, 7] = link.send(everyone.at[4, high], everyone.at[6, high], dx, z)
+        spread[g, 5] = link.send(everyone.at[4, rows], everyone.at[5, rows], dk, z)
+
+    def spread_diag(g):
+        rows = pl.ds(g * TILE, TILE)
+        spread[g, 6].wait_recv()
+        spread[g, 7].wait_recv()
+        spread[g, 8] = link.send(everyone.at[6, rows], everyone.at[7, rows], dk, z)
+
+    plane_first(1, up_hbm)
+    plane_first(2, down_hbm)
+    for copy in first_loads:
+        copy.wait()
+
+    def back_strip(i, _):
+        strip, frames = strip_of(i), pl.ds(i * FBLK, FBLK)
+        for copy in swaps(i):
+            copy.wait_recv()
+        mods = mods_ref[frames]
+        mid = ys[strip]
+        feed = es[strip].astype(F32) + ep[strip].astype(F32)
+        dy = dys[strip].astype(F32)
+        ep[strip] = (mid + flat(mods[:, 5:6] * frames_of(feed))).astype(BF)
+        normed, inverse_std = norm_rows(mid)
+        grad = gs[strip].astype(F32) + gp[strip].astype(F32)
+        dm[frames, 3] = jnp.sum(frames_of(grad), axis=1)
+        dm[frames, 4] = jnp.sum(frames_of(grad * normed), axis=1)
+        dm[frames, 5] = jnp.sum(frames_of(dy * feed), axis=1)
+        scaled = flat(frames_of(grad) * (1.0 + mods[:, 4:5]))
+        dy1 = dy + norm_back(scaled, normed, inverse_std)
+        ys[strip] = dy1
+        dm[frames, 2] = jnp.sum(frames_of(dy1 * brs[strip].astype(F32)), axis=1)
+        gp[strip] = flat(mods[:, 2:3] * frames_of(dy1)).astype(BF)
+        return 0
+
+    lax.fori_loop(0, CLIP // BLK, back_strip, 0)
+
+    def swap_done(i, _):
+        for copy in swaps(i):
+            copy.wait_send()
+        return 0
+
+    lax.fori_loop(0, CLIP // BLK, swap_done, 0)
+    x_load = load(x_hbm, gs)
+    h_load = load(h_hbm, es)
+    output = Relay(out_sends, out_recvs, local_sems.at[EXIT_LOCAL - 1], ep, out_all, d, z)
+    output.first()
+    for copy in loads:
+        copy.wait()
+
+    def project(m, _):
+        dos[m] = dot(wout[m], gp[...], NT).astype(BF)
+        grad = dot(os_[m], gp[...], NN).astype(BF)
+        for c in range(4):
+            dattn[c, m, 96:128] = grad[c * 32 : (c + 1) * 32]
+        return 0
+
+    lax.fori_loop(0, 4, project, 0)
+
+    def attend_group(m, _):
+        for head in range(2):
+            lanes = slice(head * HD, (head + 1) * HD)
+            keys = qs[m, :, TILE + head * HD : TILE + (head + 1) * HD]
+            values = qs[m, :, 2 * TILE + head * HD : 2 * TILE + (head + 1) * HD]
+            dk_ref[...] = jnp.zeros_like(dk_ref)
+            dv_ref[...] = jnp.zeros_like(dv_ref)
+
+            def step(i, _, lanes=lanes, keys=keys, values=values, head=head):
+                across = pl.ds(pl.multiple_of(i * QBLK, QBLK), QBLK)
+                queries = qs[m, across, lanes]
+                grad = dos[m, lanes, across]
+                shift = bias_ref[:, across] - lse_ref[m, head : head + 1, across]
+                scores = dot(keys, queries, NT).reshape(FRAMES, FRAME_TOK, QBLK)
+                soft = jnp.exp2(scores * SCALE2 + shift[:, None, :]).reshape(CLIP, QBLK)
+                delta = jnp.sum(
+                    grad.astype(F32) * os_[m, lanes, across].astype(F32), axis=0, keepdims=True
+                )
+                grad_soft = dot(values, grad, NN)
+                grad_scores = (soft * (grad_soft - delta)).astype(BF)
+                dv_ref[...] += dot(soft.astype(BF), grad, NT)
+                dk_ref[...] += dot(grad_scores, queries, NN)
+                grad_query = dot(keys, grad_scores, TN) * HD ** (-0.5)
+                qs[m, across, lanes] = grad_query.T.astype(BF)
+                return 0
+
+            lax.fori_loop(0, CLIP // QBLK, step, 0)
+            qs[m, :, TILE + head * HD : TILE + (head + 1) * HD] = (dk_ref[...] * HD ** (-0.5)).astype(BF)
+            qs[m, :, 2 * TILE + head * HD : 2 * TILE + (head + 1) * HD] = dv_ref[...].astype(BF)
+        return 0
+
+    lax.fori_loop(0, 2, attend_group, 0)
+    for copy in feed_loads:
+        copy.wait()
+    plane_pass(1)
+    lax.fori_loop(2, 4, attend_group, 0)
+    plane_pass(2)
+    output.hop(1)
+
+    def hidden_strip(i, _):
+        strip = strip_of(i)
+        total = dot(qs[0, strip], win[0:384], NN)
+        for m in range(1, 4):
+            total = total + dot(qs[m, strip], win[m * 384 : (m + 1) * 384], NN)
+        brs[strip] = total.astype(BF)
+        return 0
+
+    lax.fori_loop(0, CLIP // BLK, hidden_strip, 0)
+    hidden_swap = link.send(brs, dhp, dk, z)
+    h_load.wait()
+    x_load.wait()
+
+    def input_weights(m, _):
+        grad = dot(qs[m], es[...], TN).astype(BF)
+        for role in range(3):
+            for c in range(4):
+                first = role * TILE + c * 32
+                dattn[c, m, role * 32 : (role + 1) * 32] = grad[first : first + 32]
+        return 0
+
+    lax.fori_loop(0, 4, input_weights, 0)
+    plane_first(0, dattn)
+    mod_loads = [load(wmod_hbm.at[:, m * 384 : (m + 1) * 384], qs.at[m]) for m in range(4)]
+    plane_final(1)
+    plane_final(2)
+
+    hidden_swap.wait_recv()
+
+    def last_strip(i, _):
+        strip, frames = strip_of(i), pl.ds(i * FBLK, FBLK)
+        mods = mods_ref[frames]
+        normed, inverse_std = norm_rows(gs[strip].astype(F32))
+        grad = brs[strip].astype(F32) + dhp[strip].astype(F32)
+        dm[frames, 0] = jnp.sum(frames_of(grad), axis=1)
+        dm[frames, 1] = jnp.sum(frames_of(grad * normed), axis=1)
+        scaled = flat(frames_of(grad) * (1.0 + mods[:, 1:2]))
+        dys[strip] = (ys[strip] + norm_back(scaled, normed, inverse_std)).astype(BF)
+        return 0
+
+    lax.fori_loop(0, CLIP // BLK, last_strip, 0)
+    for m in range(4):
+        for c in range(6):
+            dms[m, :, c * 256 : (c + 1) * 256] = dm[:, c, m * 256 : (m + 1) * 256].astype(BF)
+    mod_column = {}
+    clip = chip * 4 + z
+    for s in (1, 3, 2):
+        to = lax.rem(z + s, 4)
+        mod_column[s] = link.send(dms.at[to], dmall.at[clip], d, to)
+    dmall[clip] = dms[z]
+    inner = Relay(in_sends, in_recvs, local_sems.at[EXIT_LOCAL - 2], dys, in_all, d, z)
+    inner.first()
+    output.hop(2)
+
+    for s in (1, 3, 2):
+        mod_column[s].wait_recv()
+
+    def clips_of(which):
+        return dmall.at[pl.ds(which * 4, 4)]
+
+    mod_x = link.send(clips_of(chip), clips_of(chip), dx, z)
+    mod_y = link.send(clips_of(chip), clips_of(chip), dyd, z)
+    plane_pass(0)
+    column_final(1)
+    column_final(2)
+    mod_x.wait_recv()
+    over_x = jnp.bitwise_xor(chip, 1)
+    mod_xy = link.send(clips_of(over_x), clips_of(over_x), dyd, z)
+    spread_on(1)
+    spread_on(2)
+    plane_final(0)
+    inner.hop(1)
+    output.hop(3)
+
+    mod_y.wait_recv()
+    mod_xy.wait_recv()
+    for copy in mod_loads:
+        copy.wait()
+    grads = dmall[...].reshape(256, 12 * TILE)
+
+    level_grads = dot(hot_ref[...], grads, TN).astype(BF)
+    rows = dot(level_grads[:, 0:384], qs[0], NT)
+    for m in range(1, 4):
+        rows = rows + dot(level_grads[:, m * 384 : (m + 1) * 384], qs[m], NT)
+    trow[...] = rows.reshape(4, 32, D)
+    table = {}
+    for s in (1, 3, 2):
+        to = lax.rem(z + s, 4)
+        table[s] = link.send(trow.at[to], tbuf.at[s - 1], d, to)
+
+    for part in range(6):
+        win[part * 256 : (part + 1) * 256] = dot(
+            grads[:, part * 256 : (part + 1) * 256], emb_ref[...], TN
+        ).astype(BF)
+    homes.append(load(win, dwm_out))
+    spread_diag(1)
+    spread_diag(2)
+    column_final(0)
+    inner.hop(2)
+    spread_on(0)
+    for s in (1, 3, 2):
+        table[s].wait_recv()
+    table_ref[...] = trow[z] + tbuf[0] + tbuf[1] + tbuf[2]
+    spread_diag(0)
+    inner.hop(3)
+    for g in range(3):
+        for slot in (1, 3, 5, 8):
+            spread[g, slot].wait_recv()
+    for copy in homes:
+        copy.wait()
+    output.finish()
+    inner.finish()
+    link.drain()
+
+
+def exit_call(y1, dh2, e, dy, branch, x, h1, qkv, o_rows, w_in, w_out, w_mod, d_up, d_down, mods, bias, lse, emb, hot):
+    vmem = pl.BlockSpec(memory_space=pltpu.VMEM)
+    hbm = pl.BlockSpec(memory_space=pl.ANY)
+    chunks = (4, 4, TILE, D)
+    heads = (4, TILE, D)
+    return pl.pallas_call(
+        exit_kernel,
+        in_specs=[hbm] * 14 + [vmem] * 5,
+        out_specs=[hbm] * 4 + [vmem],
+        out_shape=[
+            jax.ShapeDtypeStruct((2 * CLIP, D), BF),
+            jax.ShapeDtypeStruct((2 * CLIP, D), BF),
+            jax.ShapeDtypeStruct((8, 3 * TILE, D), BF),
+            jax.ShapeDtypeStruct((12 * TILE, D), BF),
+            jax.ShapeDtypeStruct((32, D), F32),
+        ],
+        scratch_shapes=[
+            pltpu.VMEM((CLIP, D), F32),
+            pltpu.VMEM((CLIP, D), BF),
+            pltpu.VMEM((CLIP, D), BF),
+            pltpu.VMEM((CLIP, D), BF),
+            pltpu.VMEM((CLIP, D), BF),
+            pltpu.VMEM((CLIP, D), BF),
+            pltpu.VMEM((CLIP, D), BF),
+            pltpu.VMEM((4, CLIP, 3 * TILE), BF),
+            pltpu.VMEM(heads, BF),
+            pltpu.VMEM(heads, BF),
+            pltpu.VMEM((12 * TILE, D), BF),
+            pltpu.VMEM(heads, BF),
+            pltpu.VMEM((CLIP, D), BF),
+            pltpu.VMEM(chunks, BF),
+            pltpu.VMEM((3, 6, 2, TILE, D), BF),
+            pltpu.VMEM((2, 8, TILE, D), BF),
+            pltpu.VMEM((3, 3, TILE, D), BF),
+            pltpu.VMEM((3, TILE, D), BF),
+            pltpu.VMEM((FRAMES, 6, D), F32),
+            pltpu.VMEM((4, FRAMES, 12 * TILE), BF),
+            pltpu.VMEM((16, FRAMES, 12 * TILE), BF),
+            pltpu.VMEM((4, 32, D), F32),
+            pltpu.VMEM((3, 32, D), F32),
+            pltpu.VMEM((CLIP, HD), F32),
+            pltpu.VMEM((CLIP, HD), F32),
+            pltpu.SemaphoreType.DMA((EXIT_COPIES,)),
+            pltpu.SemaphoreType.DMA((EXIT_COPIES,)),
+            pltpu.SemaphoreType.DMA((8,)),
+            pltpu.SemaphoreType.DMA((8,)),
+            pltpu.SemaphoreType.DMA((12,)),
+            pltpu.SemaphoreType.DMA((12,)),
+            pltpu.SemaphoreType.DMA((12,)),
+            pltpu.SemaphoreType.DMA((12,)),
+            pltpu.SemaphoreType.DMA((EXIT_LOCAL,)),
+        ],
+        compiler_params=pltpu.CompilerParams(
+            vmem_limit_bytes=63 * 1024 * 1024, collective_id=1, has_side_effects=True
+        ),
+        cost_estimate=cost(1e11, 60e6),
+        name="exit",
+    )(
+        y1,
+        dh2,
+        e,
+        dy,
+        branch,
+        x,
+        h1,
+        qkv,
+        o_rows.reshape(heads),
+        w_in,
+        w_out.reshape(heads),
+        w_mod,
+        d_up.reshape(chunks),
+        d_down.reshape(chunks),
+        mods,
+        bias,
+        lse,
+        emb,
+        hot,
+    )
+
+
 def adam_step(grad, left, right, one, two, master, rate):
     low_left, low_right = left.astype(BF), right.astype(BF)
     turned = dot(low_left, grad.astype(BF), TN)
@@ -751,9 +1319,9 @@
             grad = jnp.concatenate(pieces, axis=0).astype(F32)
             mod_row = pl.multiple_of(tab_ref[tile, 9] * TILE, TILE)
             mod_col = pl.multiple_of(tab_ref[tile, 10] * TILE, TILE)
-            mod_grad = mod_ref[pl.ds(mod_row, TILE), pl.ds(mod_col, TILE)].astype(F32)
+            mod_grad = mod_ref[pl.ds(mod_col, TILE), pl.ds(mod_row, TILE)].astype(F32)
             kind = tab_ref[tile, 11]
-            grad = jnp.where(kind == 1, grad.T, jnp.where(kind == 2, mod_grad, grad))
+            grad = jnp.where(kind == 0, grad, jnp.where(kind == 2, mod_grad, grad).T)
         else:
             grad = grad_ref[slot].astype(F32)
         master, one, two = adam_step(
@@ -898,8 +1466,6 @@
         return jnp.stack([v] + [z_get(v, s) for s in range(1, groups)])
 
     def z_reduce(v):
-        if fast:
-            v = lax.dynamic_slice_in_dim(jnp.concatenate([v, v]), z, groups, axis=0)
         total = v[0].astype(F32)
         for s in range(1, groups):
             total = total + z_put(v[s], s).astype(F32)
@@ -1014,70 +1580,72 @@
 
     with jax.named_scope("feed"):
         e_part, dh2_part, d_up, d_down = feed_both(h2, de, w_up, w_down)
-        out, dy1, da, dm_mid = row_call(
-            back_kernel,
-            "back",
-            [y1, dh2_part, across(dh2_part), dy, branch, e_part, across(e_part)],
-            mods,
-            [BF, F32, BF],
-            [4],
-            24 * mb,
-        )
-        shape = (chips, groups, -1, D)
-        red_up = z_reduce(plane_reduce(d_up.reshape(shape))).astype(BF)
-        red_down = z_reduce(plane_reduce(d_down.reshape(shape))).astype(BF)
-
-    def to_column(rows_here):
-        half = CLIP // 2
-        mine = lax.dynamic_slice_in_dim(rows_here, core * half, half, axis=0)
-        by_clip = [mine] + [z_get(mine, s) for s in range(1, groups)]
-        by_clip = lax.dynamic_slice_in_dim(jnp.stack(by_clip + by_clip), (groups - z) % groups, groups, axis=0)
-        keep = lax.dynamic_slice_in_dim(by_clip, core * local_clips, local_clips, axis=0)
-        send = lax.dynamic_slice_in_dim(by_clip, (1 - core) * local_clips, local_clips, axis=0)
-        got_half = across(send)
-        both = jnp.where(
-            core == 0, jnp.stack([keep, got_half], axis=1), jnp.stack([got_half, keep], axis=1)
-        )
-        return both.reshape(local_clips * CLIP, D)
-
-    with jax.named_scope("block_output"):
-        block_output = to_column(out)
-
-    with jax.named_scope("attention_back"):
-        do_rows = dot(w_out, da, NT).astype(BF)
-        d_out = dot(o_rows, da, NN).astype(BF)
-        d_qkv = attend_back(qkv, o_rows, do_rows, lse, bias)
-        dh1_part = dot(d_qkv, w_in, NN).astype(BF)
-        d_in = dot(d_qkv, h1, TN).astype(BF)
-        in_grad, dm_last = row_call(
-            last_kernel, "last", [x, dh1_part, across(dh1_part), dy1], mods, [BF], [2], 12 * mb
-        )
-        d_in = d_in.reshape(groups, 3, chips, rows, D).transpose(2, 0, 1, 3, 4)
-        d_out = d_out.reshape(groups, 1, chips, rows, D).transpose(2, 0, 1, 3, 4)
-        d_attn = jnp.concatenate([d_in, d_out], axis=2).reshape(chips, groups, 4 * rows, D)
-        red_attn = z_reduce(plane_reduce(d_attn)).astype(BF)
-
-    with jax.named_scope("input_grad"):
-        input_grad = to_column(in_grad).astype(F32)
-
-    with jax.named_scope("modulation_back"):
-        d_mod = jnp.stack(
-            [dm_last[:, 0], dm_last[:, 1], dm_mid[:, 2], dm_mid[:, 0], dm_mid[:, 1], dm_mid[:, 3]], axis=1
-        ).astype(BF)
-        d_mod = (
-            d_mod.reshape(FRAMES, 6, groups, D // groups).transpose(2, 0, 1, 3).reshape(groups, FRAMES, -1)
-        )
-        pieces = [lax.dynamic_index_in_dim(d_mod, z, axis=0, keepdims=False)]
-        for s in range(1, groups):
-            pieces.append(z_put(lax.dynamic_index_in_dim(d_mod, (z + s) % groups, axis=0, keepdims=False), s))
-        d_mod = jnp.stack(pieces)
-        if fast:
-            d_mod = lax.dynamic_slice_in_dim(
-                jnp.concatenate([d_mod, d_mod])[::-1], groups - 1 - z, groups, axis=0
+    if fast:
+        with jax.named_scope("exit"):
+            block_output, input_grad, everyone, d_w_mod, table_grad = exit_call(
+                y1, dh2_part, e_part, dy, branch, x, h1, qkv, o_rows, w_in, w_out, w_mod,
+                d_up, d_down, mods, bias, lse, all_embedded, own_hot,
             )
-            d_mod = jnp.take(plane_double(d_mod), jnp.bitwise_xor(jnp.arange(chips), chip), axis=0)
-            d_mod = d_mod.reshape(chips * groups * FRAMES, -1)
-        else:
+            input_grad = input_grad.astype(F32)
+    else:
+        with jax.named_scope("feed_back"):
+            out, dy1, da, dm_mid = row_call(
+                back_kernel,
+                "back",
+                [y1, dh2_part, across(dh2_part), dy, branch, e_part, across(e_part)],
+                mods,
+                [BF, F32, BF],
+                [4],
+                24 * mb,
+            )
+            shape = (chips, groups, -1, D)
+            red_up = z_reduce(plane_reduce(d_up.reshape(shape))).astype(BF)
+            red_down = z_reduce(plane_reduce(d_down.reshape(shape))).astype(BF)
+
+        def to_column(rows_here):
+            half = CLIP // 2
+            mine = lax.dynamic_slice_in_dim(rows_here, core * half, half, axis=0)
+            by_clip = [mine] + [z_get(mine, s) for s in range(1, groups)]
+            by_clip = lax.dynamic_slice_in_dim(jnp.stack(by_clip + by_clip), (groups - z) % groups, groups, axis=0)
+            keep = lax.dynamic_slice_in_dim(by_clip, core * local_clips, local_clips, axis=0)
+            send = lax.dynamic_slice_in_dim(by_clip, (1 - core) * local_clips, local_clips, axis=0)
+            got_half = across(send)
+            both = jnp.where(
+                core == 0, jnp.stack([keep, got_half], axis=1), jnp.stack([got_half, keep], axis=1)
+            )
+            return both.reshape(local_clips * CLIP, D)
+
+        with jax.named_scope("block_output"):
+            block_output = to_column(out)
+
+        with jax.named_scope("attention_back"):
+            do_rows = dot(w_out, da, NT).astype(BF)
+            d_out = dot(o_rows, da, NN).astype(BF)
+            d_qkv = attend_back(qkv, o_rows, do_rows, lse, bias)
+            dh1_part = dot(d_qkv, w_in, NN).astype(BF)
+            d_in = dot(d_qkv, h1, TN).astype(BF)
+            in_grad, dm_last = row_call(
+                last_kernel, "last", [x, dh1_part, across(dh1_part), dy1], mods, [BF], [2], 12 * mb
+            )
+            d_in = d_in.reshape(groups, 3, chips, rows, D).transpose(2, 0, 1, 3, 4)
+            d_out = d_out.reshape(groups, 1, chips, rows, D).transpose(2, 0, 1, 3, 4)
+            d_attn = jnp.concatenate([d_in, d_out], axis=2).reshape(chips, groups, 4 * rows, D)
+            red_attn = z_reduce(plane_reduce(d_attn)).astype(BF)
+
+        with jax.named_scope("input_grad"):
+            input_grad = to_column(in_grad).astype(F32)
+
+        with jax.named_scope("modulation_back"):
+            d_mod = jnp.stack(
+                [dm_last[:, 0], dm_last[:, 1], dm_mid[:, 2], dm_mid[:, 0], dm_mid[:, 1], dm_mid[:, 3]], axis=1
+            ).astype(BF)
+            d_mod = (
+                d_mod.reshape(FRAMES, 6, groups, D // groups).transpose(2, 0, 1, 3).reshape(groups, FRAMES, -1)
+            )
+            pieces = [lax.dynamic_index_in_dim(d_mod, z, axis=0, keepdims=False)]
+            for s in range(1, groups):
+                pieces.append(z_put(lax.dynamic_index_in_dim(d_mod, (z + s) % groups, axis=0, keepdims=False), s))
+            d_mod = jnp.stack(pieces)
             d_mod = plane_double(d_mod).reshape(chips * groups * FRAMES, -1)
             back_clip = (z + groups - jnp.arange(groups, dtype=jnp.int32)) % groups
             clip_hot = (back_clip[:, None] == jnp.arange(groups, dtype=jnp.int32)[None, :]).astype(
@@ -1088,24 +1656,25 @@
             own_levels = level_table.shape[0]
             own_ids = device * own_levels + jnp.arange(own_levels, dtype=jnp.int32)[None, :]
             own_hot = (order[:, None] == own_ids).astype(BF)
-        d_w_mod = dot(all_embedded, d_mod, TN).astype(BF)
-        own_levels = level_table.shape[0]
-        own_rows = dot(dot(own_hot, d_mod, TN).astype(BF), w_mod, NT)
-        own_rows = own_rows.reshape(groups, own_levels // groups, D)
-        table_grad = lax.dynamic_index_in_dim(own_rows, z, axis=0, keepdims=False)
-        for s in range(1, groups):
-            table_grad = table_grad + z_put(
-                lax.dynamic_index_in_dim(own_rows, (z + s) % groups, axis=0, keepdims=False), s
-            )
+            d_w_mod = dot(all_embedded, d_mod, TN).astype(BF)
+            own_levels = level_table.shape[0]
+            own_rows = dot(dot(own_hot, d_mod, TN).astype(BF), w_mod, NT)
+            own_rows = own_rows.reshape(groups, own_levels // groups, D)
+            table_grad = lax.dynamic_index_in_dim(own_rows, z, axis=0, keepdims=False)
+            for s in range(1, groups):
+                table_grad = table_grad + z_put(
+                    lax.dynamic_index_in_dim(own_rows, (z + s) % groups, axis=0, keepdims=False), s
+                )
 
     with jax.named_scope("owners"):
-        reduced = jnp.concatenate([red_attn, red_up, red_down], axis=0)
-        if chips == 4:
-            height = reduced.shape[0]
-            plane_parts = plane_gather(reduced.reshape(2, height // 2, D)).reshape(chips, height, D)
-        else:
-            plane_parts = plane_double(reduced)
-        everyone = jnp.stack([plane_parts, across(plane_parts)], axis=1).reshape(owners, -1, D)
+        if not fast:
+            reduced = jnp.concatenate([red_attn, red_up, red_down], axis=0)
+            if chips == 4:
+                height = reduced.shape[0]
+                plane_parts = plane_gather(reduced.reshape(2, height // 2, D)).reshape(chips, height, D)
+            else:
+                plane_parts = plane_double(reduced)
+            everyone = jnp.stack([plane_parts, across(plane_parts)], axis=1).reshape(owners, -1, D)
         tile_ids = lax.dynamic_slice_in_dim(owner_list, device * slots, slots)
         rates = kind_rates(tile_ids, counts)
         if fast:

time: 799 us -> 578 us (0.72); the launches traced: 789 us -> 577 us
  waiting for transfers between devices: 187 us -> 2.23 us
  Pallas kernels: 358 us -> 533 us
  starting transfers between devices: 98.9 us -> 0.49 us
  local copies, waits for them, and re-layouts: 66.4 us -> 18.4 us
  other arithmetic: 46.3 us -> 14.6 us
  matrix products: 30.4 us -> 7.42 us
    pallas_call x1, Pallas kernels: 35.3 us -> 229 us  [exit_call(): pl.pallas_call(exit_kernel, in_specs=[hbm] * 14 + [vmem] * 5, out_specs=[...]
    ppermute x21 -> x0, waiting for transfers between devices: 110 us -> none  [the longest x6 89 us: z_get(): return lax.ppermute(v, 'mp', [((i + s) % groups, i) for i in range(groups)])]
    ppermute x31 -> x1, waiting for transfers between devices: 76.7 us -> 2.23 us  [swap(): return lax.ppermute(v, 'dp', [(i, i ^ step) for i in range(owners)])]
    ppermute x21 -> x0, starting transfers between devices: 55.6 us -> none  [the longest x15 49.8 us: z_put(): return lax.ppermute(v, 'mp', [(i, (i + s) % groups) for i in range(groups)])]
    ppermute x31 -> x1, starting transfers between devices: 43.3 us -> 0.49 us  [swap(): return lax.ppermute(v, 'dp', [(i, i ^ step) for i in range(owners)])]
    dot_general x8 -> x2, matrix products: 30.4 us -> 7.42 us  [dot(): lax.dot_general(left, right, (dims, ((), ())), preferred_element_type=F32)]
    another operation x12 -> x1, other arithmetic: 19 us -> 0.02 us
    pallas_call x3 -> x1, Pallas kernels: 26.8 us -> 8.04 us  [row_call(): pl.pallas_call(kernel, grid=(CLIP // BLK,), in_specs=[row_spec() for _ in...]
  transfers between devices with their start and end apart: 52 -> 1, of which waited for: 20 -> 1; matrix products, arithmetic and copies ran while one was open for 14% -> 0% of each run, Pallas kernels for 7% -> 0%
where the time goes in v3:
time: 578 us; the launch traced here: 577 us
  Pallas kernels  533 us (92%)
  local copies, waits for them, and re-layouts  18.4 us (3%)
  other arithmetic  14.6 us (3%)
  matrix products  7.42 us (1%)
    pallas_call x1, Pallas kernels, exit_call(): pl.pallas_call(exit_kernel, in_specs=[hbm] * 14 + [vmem] * 5, out_specs=[...  229 us
    pallas_call x1, Pallas kernels, entry(): pl.pallas_call(entry_kernel, in_specs=[pl.BlockSpec(memory_space=pltpu.SM...  202 us
    pallas_call x1, Pallas kernels, feed_both(): pl.pallas_call(feed_kernel, grid=(units // UNITS,), in_specs=[whole, whol...  47 us
    pallas_call x1, Pallas kernels, attend(): pl.pallas_call(attend_kernel, grid=(groups,), in_specs=[pl.BlockSpec((CLI...  26.6 us
    pallas_call x1, Pallas kernels, adam(): pl.pallas_call(functools.partial(adam_kernel, picked=picked, batch=batch)...  20.2 us
  transfers between devices with their start and end apart: 1, of which 1 were waited for; matrix products, arithmetic and copies ran while one was open for 0% of the time, Pallas kernels for 0%

profile of v3, /device:TPU:1, one launch (start us, length us, event | category | flops | bytes accessed | tf_op | source)
XLA Modules:
  0.0 577.4 jit_solution(587658114932608900)
XLA Ops:
  0.7 0.8 fusion.23
  1.7 0.8 reshape.429.bias_ref
  2.5 0.7 compare_convert_fusion
  3.2 0.8 multiply_reduce_fusion
  4.0 0.7 broadcast_select_fusion
  5.1 1.9 bitcast_convert_fusion
  7.4 0.7 select_reduce_fusion.idx_ref
  8.1 1.4 maximum_maximum_fusion.pay_ref
  9.5 202.3 %entry.1 = (bf16[3,4,4,128,1024]{4,3,2,1,0:T(8,128)(2,1)}, bf16[1024,1536]{1,0:T(8,128)(2,1)}, bf16[1024,1024]{1,0:T(8,128)(2,1)}, bf16[1024,1024]{1,0:T(8,128)(...) custom-call(s32[288]{0:T(512)} %select_reduce_fusion.idx_ref, ...), custom_call_target="tpu_custom_call" | custom-call | flops 1000000000 | bytes 40000000 | tf_op jit(solution)/shard_map/entry/entry/pallas_call | solution.py:510
  211.8 7.7 %fusion.25 = (bf16[1,4,4,128,1024]{4,3,2,1,0:T(8,128)(2,1)}, bf16[1,4,4,128,1024]{4,3,2,1,0:T(8,128)(2,1)}, bf16[1,4,4,128,1024]{4,3,2,1,0:T(8,128)(2,1)S(1)}) fusion(bf16[3,4,4,128,1024]{4,3,2,1,0:T(8,128)(2,1)} %get-tuple-element.37), kind=kLoop, calls=%fused_computation.100 | loop fusion | bytes 25165824 | tf_op jit(solution)/shard_map/entry/slice | solution.py:1508
  220.6 1.8 copy-done.6
  222.4 4.9 convolution_convert_fusion.qkv_ref.qkv_hbm
  227.4 26.6 %attend.1 = (bf16[512,1024]{1,0:T(8,128)(2,1)}, f32[4,2,1024]{2,1,0:T(2,128)}) custom-call(bf16[1024,1536]{1,0:T(8,128)(2,1)} %convolution_convert_fusion.qkv_ref.qkv_hbm, f32[16,1024]{1,0:T(8,128)} %get-tuple-element.38.bias_ref), custom_call_target="tpu_custom_call" | custom-call | flops 6442450944 | bytes 3145728 | tf_op jit(solution)/shard_map/attention/attend/pallas_call | solution.py:575
  254.0 2.5 convolution_convert_fusion.1.a_ref
  257.0 0.8 fusion.14
  258.0 0.7 copy.47.tab_ref
  258.7 2.2 collective-permute-done.b_ref
  260.9 8.0 %middle.1 = (f32[1024,1024]{1,0:T(8,128)}, bf16[1024,1024]{1,0:T(8,128)(2,1)}, bf16[1024,1024]{1,0:T(8,128)(2,1)}, bf16[1024,1024]{1,0:T(8,128)(2,1)}) custom-call(bf16[1024,1024]{1,0:T(8,128)(2,1)} %get-tuple-element.35.x_ref.x_hbm, bf16[1024,1024]{1,0:T(8,128)(2,1)} %copy-done.1, bf16[1024,1024]{1,0:T(8,128)(2,1)} %collective-permute-done.b_ref, ...), custom_call_target="tpu_custom_call" | custom-call | flops 31457280 | bytes 18874368 | tf_op jit(solution)/shard_map/attention/middle/pallas_call | solution.py:157
  269.0 47.0 %feed_both.1 = (bf16[1024,1024]{1,0:T(8,128)(2,1)}, bf16[1024,1024]{1,0:T(8,128)(2,1)}, bf16[2048,1024]{1,0:T(8,128)(2,1)}, bf16[2048,1024]{1,0:T(8,128)(2,1)}) custom-call(bf16[1024,1024]{1,0:T(8,128)(2,1)} %get-tuple-element.43.h_ref, bf16[1024,1024]{1,0:T(8,128)(2,1)} %get-tuple-element.44.de_ref, bf16[2048,1024]{1,0:T(8,128)(2,1)} %bitcast.49, ...), custom_call_target="tpu_custom_call" | custom-call | flops 25769803776 | bytes 25165824 | tf_op jit(solution)/shard_map/feed/feed_both/pallas_call | solution.py:701
  316.0 229.2 %exit.1 = (bf16[2048,1024]{1,0:T(8,128)(2,1)}, bf16[2048,1024]{1,0:T(8,128)(2,1)}, bf16[8,384,1024]{2,1,0:T(8,128)(2,1)}, bf16[1536,1024]{1,0:T(8,128)(2,1)}, f32[32,1024]{1,0:T(8,128)}) custom-call(f32[1024,1024]{1,0:T(8,128)} %get-tuple-element.42.y_hbm, bf16[1024,1024]{1,0:T(8,128)(2,1)} %get-tuple-element.45.g_hbm, ...), custom_call_target="tpu_custom_call" | custom-call | flops 99999997952 | bytes 60000000 | tf_op jit(solution)/shard_map/exit/exit/pallas_call | solution.py:1212
  545.2 6.6 %convert_element_type.26 = f32[2048,1024]{1,0:T(8,128)} convert(bf16[2048,1024]{1,0:T(8,128)(2,1)} %get-tuple-element.55) | non-fusion elementwise | flops 2097152 | bytes 12582912 | tf_op jit(solution)/shard_map/exit/convert_element_type | solution.py:1589
  551.8 20.2 %adam.1 = (f32[36,128,128]{2,1,0:T(8,128)}, f32[36,128,128]{2,1,0:T(8,128)}, f32[36,128,128]{2,1,0:T(8,128)}, bf16[36,128,128]{2,1,0:T(8,128)(2,1)}) custom-call(s32[36,12]{1,0:T(8,128)} %copy.47.tab_ref, f32[36]{0:T(128)} %get-tuple-element.63.rate_ref, bf16[8,384,1024]{2,1,0:T(8,128)(2,1)} %get-tuple-element.57.refs_0_, ...), custom_call_target="tpu_custom_call" | custom-call | flops 603979776 | bytes 21233664 | tf_op jit(solution)/shard_map/owners/adam/pallas_call | solution.py:1372
  572.0 4.7 copy.52
  576.7 0.7 copy.53
  (37 shorter events, 2.8 us)
Async XLA Ops:
  0.6 6.3 %copy-start.3 = (bf16[128,1024]{1,0:T(8,128)(2,1)S(1)}, bf16[128,1024]{1,0:T(8,128)(2,1)}, u32[]{:S(2)}) copy-start(bf16[128,1024]{1,0:T(8,128)(2,1)} %param.15) | copy-start | bytes 786436
  2.5 4.9 copy-start.5
  220.2 2.3 copy-start.6
  220.5 6.8 %copy-start = (bf16[4,4,3,32,1024]{4,3,0,2,1:T(8,128)(2,1)}, bf16[4,4,3,32,1024]{4,3,0,2,1:T(8,128)(2,1)S(1)}, u32[]{:S(2)}) copy-start(bf16[4,4,3,32,1024]{4,3,0,2,1:T(8,128)(2,1)S(1)} %copy.48) | copy-start | bytes 9437188
  220.6 33.4 %copy-start.2 = (bf16[4,4,1,32,1024]{4,3,0,1,2:T(8,128)(2,1)}, bf16[4,4,1,32,1024]{4,3,0,1,2:T(8,128)(2,1)S(1)}, u32[]{:S(2)}) copy-start(bf16[4,4,1,32,1024]{4,3,0,1,2:T(8,128)(2,1)S(1)} %copy.49) | copy-start | bytes 3145732
  256.5 4.4 copy-start.1
  256.5 4.4 collective-permute-start
  572.0 4.7 copy-start.4

commit v4 on v3

--- a/solution.py
+++ b/solution.py
@@ -236,12 +236,12 @@
             device_id_type=MESH,
         )
         self.used += 1
+        self.pending.append(copy)
         return copy
 
     def send(self, src, dst, dp, mp):
         copy = self.make(src, dst, dp, mp)
         copy.start()
-        self.pending.append(copy)
         return copy
 
     def drain(self):
@@ -259,22 +259,37 @@
     pl.semaphore_wait(barrier, 6)
 
 
+QBLK = 256
+ROWS = 512
+SCALE2 = HD ** (-0.5) * LOG2E
+
+
 ENTRY_COPIES = 8 + 45 + 3
 
 
-def entry_kernel(
+def front_kernel(
     idx_ref,
     pay_ref,
     act_ref,
     cot_ref,
     bias_ref,
     w_ref,
-    wmod_ref,
-    x_ref,
-    dy_ref,
-    h_ref,
+    wmod_out,
+    x_out,
+    dy_out,
+    h_out,
+    wpack_out,
+    qkv_out,
+    o_out,
+    branch_out,
+    y_out,
+    e_out,
+    dh_out,
+    dup_out,
+    ddown_out,
     mods_ref,
     bias_out,
+    lse_ref,
     emb_ref,
     own_hot_ref,
     gath,
@@ -286,15 +301,32 @@
     part,
     modbuf,
     hots,
+    hs,
+    wpack,
+    qs,
+    os_,
+    mine,
+    peer,
+    e_acc,
+    dh_acc,
+    wfeed,
+    up_stage,
+    down_stage,
+    up_acc,
+    down_acc,
     sends,
     recvs,
     swap_sends,
     swap_recvs,
+    strip_sends,
+    strip_recvs,
     local_sems,
+    pack_sems,
+    stage_sems,
 ):
     d, z = lax.axis_index("dp"), lax.axis_index("mp")
     core, chip = lax.rem(d, 2), d // 2
-    dk, dx, dy = jnp.bitwise_xor(d, 1), jnp.bitwise_xor(d, 2), jnp.bitwise_xor(d, 4)
+    dk, dx, dyd = jnp.bitwise_xor(d, 1), jnp.bitwise_xor(d, 2), jnp.bitwise_xor(d, 4)
     dxy = jnp.bitwise_xor(d, 6)
     link = Link(sends, recvs)
     greet(d, z)
@@ -306,7 +338,7 @@
     home = pltpu.make_async_copy(pay_ref, slot(d), local_sems.at[0])
     home.start()
     to_x = link.send(pay_ref, slot(d), dx, z)
-    to_y = link.send(pay_ref, slot(d), dy, z)
+    to_y = link.send(pay_ref, slot(d), dyd, z)
     to_k = link.send(pay_ref, slot(d), dk, z)
 
     holds = (z // 2) == core
@@ -339,11 +371,11 @@
             copy.start()
 
     to_x.wait_recv()
-    x_to_y = link.send(slot(dx, 0, half), slot(dx, 0, half), dy, z)
+    x_to_y = link.send(slot(dx, 0, half), slot(dx, 0, half), dyd, z)
     x_to_k = link.send(slot(dx), slot(dx), dk, z)
     to_y.wait_recv()
-    y_to_x = link.send(slot(dy, half, half), slot(dy, half, half), dx, z)
-    y_to_k = link.send(slot(dy), slot(dy), dk, z)
+    y_to_x = link.send(slot(dyd, half, half), slot(dyd, half, half), dx, z)
+    y_to_k = link.send(slot(dyd), slot(dyd), dk, z)
 
     @pl.when(holds)
     def _():
@@ -357,9 +389,17 @@
         for copy in swaps():
             copy.wait_recv()
 
-    x_ref[...] = xs[...]
-    dy_ref[...] = dys[...]
     bias_out[...] = bs[...]
+    locals_used = [7]
+
+    def save(src, dst):
+        copy = pltpu.make_async_copy(src, dst, local_sems.at[locals_used[0]])
+        locals_used[0] += 1
+        copy.start()
+        return copy
+
+    x_saved = save(xs, x_out)
+    dy_saved = save(dys, dy_out)
 
     x_to_y.wait_recv()
     y_to_x.wait_recv()
@@ -391,47 +431,55 @@
     def pick_mod(j, _):
         strip = pl.ds(pl.multiple_of(j * TILE, TILE), TILE)
         for col in range(12):
-            wmod_ref[strip, col * TILE : (col + 1) * TILE] = tile(192 + j * 12 + col)
+            qs[col // 3, strip, (col % 3) * TILE : (col % 3 + 1) * TILE] = tile(192 + j * 12 + col)
         return 0
 
-    along, by_x, by_y, diag, homes = {}, {}, {}, {}, []
+    along, by_x, by_y, diag = {}, {}, {}, {}
+    all_groups = [(g, s) for g in range(3) for s in (0, 1, 3, 2)]
+
+    def landing(g, p, m):
+        return w_ref.at[p, m] if g == 0 else wfeed.at[g - 1, p, m]
+
+    for g, s in all_groups:
+        m = lax.rem(z + 4 - s, 4)
+        if s:
+            along[g, s] = link.make(own.at[g], landing(g, 0, z), d, lax.rem(z + s, 4))
+        src = own.at[g] if s == 0 else landing(g, 0, m)
+        by_x[g, s] = link.make(src, landing(g, 1, m), dx, z)
+        by_y[g, s] = link.make(src, landing(g, 2, m), dyd, z)
+        if s < 2:
+            diag[g, s] = link.make(landing(g, 1, m), landing(g, 3, m), dyd, z)
+        else:
+            diag[g, s] = link.make(landing(g, 2, m), landing(g, 3, m), dx, z)
+    homes = [pltpu.make_async_copy(own.at[g], landing(g, 0, z), local_sems.at[4 + g]) for g in range(3)]
 
     def send_along(g):
         for s in (1, 3, 2):
-            along[g, s] = link.send(own.at[g], w_ref.at[g, 0, z], d, lax.rem(z + s, 4))
+            along[g, s].start()
 
     def send_plane(g, s):
-        m = lax.rem(z + 4 - s, 4)
-        src = own.at[g] if s == 0 else w_ref.at[g, 0, m]
-        by_x[g, s] = link.send(src, w_ref.at[g, 1, m], dx, z)
-        by_y[g, s] = link.send(src, w_ref.at[g, 2, m], dy, z)
+        if s:
+            along[g, s].wait_recv()
+        by_x[g, s].start()
+        by_y[g, s].start()
 
     def send_diag(g, s):
-        m = lax.rem(z + 4 - s, 4)
-        if s < 2:
-            by_x[g, s].wait_recv()
-            diag[g, s] = link.send(w_ref.at[g, 1, m], w_ref.at[g, 3, m], dy, z)
-        else:
-            by_y[g, s].wait_recv()
-            diag[g, s] = link.send(w_ref.at[g, 2, m], w_ref.at[g, 3, m], dx, z)
-
-    def keep_home(g):
-        copy = pltpu.make_async_copy(own.at[g], w_ref.at[g, 0, z], local_sems.at[4 + g])
-        copy.start()
-        homes.append(copy)
+        (by_x if s < 2 else by_y)[g, s].wait_recv()
+        diag[g, s].start()
 
     lax.fori_loop(0, 8, pick_attn, 0)
-    lax.fori_loop(0, 8, pick_feed, 0)
     send_along(0)
     send_plane(0, 0)
-    keep_home(0)
+    homes[0].start()
+    lax.fori_loop(0, 8, pick_feed, 0)
     send_along(1)
     send_along(2)
     send_plane(1, 0)
-    keep_home(1)
-    keep_home(2)
+    homes[1].start()
+    homes[2].start()
 
     lax.fori_loop(0, 8, pick_mod, 0)
+    mod_saved = save(qs, wmod_out)
     places = lax.broadcasted_iota(jnp.int32, (32, LEVELS), 1).astype(F32)
     for owner in range(8):
         codes = gath[owner * PAYLOAD + LEVEL_TILE][:32].astype(F32)
@@ -442,14 +490,14 @@
         strip = jnp.concatenate([gath[owner * PAYLOAD + HEAD_TILES + j] for owner in range(8)], axis=0)
         emb_ref[:, j * TILE : (j + 1) * TILE] = dot(hots[...], strip, NN).astype(BF)
     embedded = emb_ref[pl.ds(pl.multiple_of(chip * 64, 64), 64), :]
-    part[...] = dot(embedded, wmod_ref[...], NN).reshape(4, FRAMES, 12 * TILE)
+    for k in range(4):
+        part[:, :, k * 384 : (k + 1) * 384] = dot(embedded, qs[k], NN).reshape(4, FRAMES, 384)
     modbuf[z] = part[z]
     shared = {}
     for s in (1, 3, 2):
         shared[s] = link.send(part.at[lax.rem(z + s, 4)], modbuf.at[z], d, lax.rem(z + s, 4))
 
     for s in (1, 3, 2):
-        along[0, s].wait_recv()
         send_plane(0, s)
     send_plane(2, 0)
     for s in (0, 1, 3, 2):
@@ -465,30 +513,223 @@
         strip = pl.ds(pl.multiple_of(i * BLK, BLK), BLK)
         normed, _ = norm_rows(xs[strip].astype(F32))
         mods = mods_ref[pl.ds(i * FBLK, FBLK)]
-        h_ref[strip] = flat(frames_of(normed) * (1.0 + mods[:, 1:2]) + mods[:, 0:1]).astype(BF)
+        hs[strip] = flat(frames_of(normed) * (1.0 + mods[:, 1:2]) + mods[:, 0:1]).astype(BF)
         return 0
 
     lax.fori_loop(0, CLIP // BLK, norm_strip, 0)
-
-    for s in (1, 3, 2):
-        along[1, s].wait_recv()
-        send_plane(1, s)
-    for s in (1, 3, 2):
-        along[2, s].wait_recv()
-        send_plane(2, s)
-    for g in (1, 2):
+    h_saved = save(hs, h_out)
+
+    def late(g, p):
         for s in (0, 1, 3, 2):
-            send_diag(g, s)
-    for g in range(3):
-        for s in range(4):
-            (by_y if s < 2 else by_x)[g, s].wait_recv()
-            diag[g, s].wait_recv()
-    for copy in homes:
+            if p == 3:
+                diag[g, s].wait_recv()
+            elif (p == 1) == (s >= 2):
+                (by_x if p == 1 else by_y)[g, s].wait_recv()
+
+    for p in (1, 2, 3):
+        late(0, p)
+    homes[0].wait()
+
+    def packs(m):
+        return [
+            pltpu.make_async_copy(
+                w_ref.at[p, m, pl.ds(role * 32, 32)],
+                wpack.at[m, pl.ds(role * TILE + p * 32, 32)],
+                pack_sems.at[m * 16 + p * 4 + role],
+            )
+            for p in range(4)
+            for role in range(4)
+        ]
+
+    def pack_start(m, _):
+        for copy in packs(m):
+            copy.start()
+        return 0
+
+    lax.fori_loop(0, 4, pack_start, 0)
+    mod_saved.wait()
+
+    def project_in(m, _):
+        for copy in packs(m):
+            copy.wait()
+        qs[m] = dot(hs[...], wpack[m, 0 : 3 * TILE], NT).astype(BF)
+        return 0
+
+    lax.fori_loop(0, 4, project_in, 0)
+    pack_saved = save(wpack, wpack_out)
+    qkv_saved = save(qs, qkv_out)
+
+    def attend_group(m, _):
+        @pl.when(m == 0)
+        def _():
+            for s in (1, 3, 2):
+                send_plane(1, s)
+
+        @pl.when(m == 1)
+        def _():
+            send_diag(1, 0)
+            send_diag(1, 1)
+
+        @pl.when(m == 2)
+        def _():
+            send_plane(2, 1)
+            send_plane(2, 3)
+            send_diag(1, 3)
+
+        @pl.when(m == 3)
+        def _():
+            send_plane(2, 2)
+            send_diag(1, 2)
+            send_diag(2, 0)
+
+        for head in range(2):
+            lanes = slice(head * HD, (head + 1) * HD)
+            keys = qs[m, :, TILE + head * HD : TILE + (head + 1) * HD]
+            values = qs[m, :, 2 * TILE + head * HD : 2 * TILE + (head + 1) * HD]
+
+            def step(i, _, lanes=lanes, keys=keys, values=values, head=head):
+                across = pl.ds(pl.multiple_of(i * QBLK, QBLK), QBLK)
+                queries = qs[m, across, lanes]
+                scores = dot(keys, queries, NT).reshape(FRAMES, FRAME_TOK, QBLK)
+                scores = scores * SCALE2 + bs[:, across][:, None, :]
+                peak = jnp.max(jnp.max(scores, axis=0), axis=0, keepdims=True)
+                weights = jnp.exp2(scores - peak[None])
+                total = jnp.sum(jnp.sum(weights, axis=0), axis=0, keepdims=True)
+                mixed = dot(values, weights.reshape(CLIP, QBLK).astype(BF), TN)
+                os_[m, lanes, across] = (mixed / total).astype(BF)
+                lse_ref[m, head : head + 1, across] = peak + jnp.log2(total)
+                return 0
+
+            lax.fori_loop(0, CLIP // QBLK, step, 0)
+        return 0
+
+    lax.fori_loop(0, 4, attend_group, 0)
+    o_saved = save(os_, o_out)
+    send_diag(2, 1)
+
+    def swap_strip(i):
+        strip = pl.ds(pl.multiple_of(i * BLK, BLK), BLK)
+        return pltpu.make_async_remote_copy(
+            src_ref=mine.at[strip],
+            dst_ref=peer.at[strip],
+            send_sem=strip_sends.at[i],
+            recv_sem=strip_recvs.at[i],
+            device_id=(dk, z),
+            device_id_type=MESH,
+        )
+
+    def project_out(i, _):
+        strip = pl.ds(pl.multiple_of(i * BLK, BLK), BLK)
+        total = dot(os_[0, :, strip], wpack[0, 3 * TILE : 4 * TILE], TN)
+        for m in range(1, 4):
+            total = total + dot(os_[m, :, strip], wpack[m, 3 * TILE : 4 * TILE], TN)
+        mine[strip] = total.astype(BF)
+        swap_strip(i).start()
+        return 0
+
+    lax.fori_loop(0, CLIP // BLK, project_out, 0)
+    h_saved.wait()
+    dy_saved.wait()
+
+    def middle_strip(i, _):
+        strip = pl.ds(pl.multiple_of(i * BLK, BLK), BLK)
+        swap_strip(i).wait_recv()
+        mods = mods_ref[pl.ds(i * FBLK, FBLK)]
+        branch = (mine[strip].astype(F32) + peer[strip].astype(F32)).astype(BF)
+        peer[strip] = branch
+        mid = frames_of(xs[strip].astype(F32)) + mods[:, 2:3] * frames_of(branch.astype(F32))
+        dh_acc[strip] = flat(mid)
+        normed, _ = norm_rows(flat(mid))
+        hs[strip] = flat(frames_of(normed) * (1.0 + mods[:, 4:5]) + mods[:, 3:4]).astype(BF)
+        dys[strip] = flat(mods[:, 5:6] * frames_of(dys[strip].astype(F32))).astype(BF)
+        return 0
+
+    lax.fori_loop(0, CLIP // BLK, middle_strip, 0)
+    y_saved = save(dh_acc, y_out)
+    branch_saved = save(peer, branch_out)
+    send_diag(2, 3)
+    send_diag(2, 2)
+    e_acc[...] = jnp.zeros_like(e_acc)
+    y_saved.wait()
+    dh_acc[...] = jnp.zeros_like(dh_acc)
+    homes[1].wait()
+    homes[2].wait()
+
+    def stages(block):
+        buf, p, first = lax.rem(block, 2), block // 2, lax.rem(block, 2) * 2
+        return [
+            pltpu.make_async_copy(stage.at[buf], dst.at[p, pl.ds(first, 2)], stage_sems.at[2 * buf + k])
+            for k, (stage, dst) in enumerate(((up_stage, dup_out), (down_stage, ddown_out)))
+        ]
+
+    def feed_block(block, _):
+        for p in (1, 2, 3):
+
+            @pl.when(block == 2 * p)
+            def _(p=p):
+                late(1, p)
+                late(2, p)
+
+        buf, p, first = lax.rem(block, 2), block // 2, lax.rem(block, 2) * 2
+        up = wfeed[0, p, pl.ds(first, 2)].reshape(2 * TILE, D)
+        down = wfeed[1, p, pl.ds(first, 2)].reshape(2 * TILE, D)
+
+        @pl.when(block >= 2)
+        def _():
+            for copy in stages(block - 2):
+                copy.wait()
+
+        for piece in range(CLIP // ROWS):
+            rows = slice(piece * ROWS, (piece + 1) * ROWS)
+            hidden = hs[rows]
+            grad = dys[rows]
+            pre = dot(hidden, up, NT)
+            square = pre * pre
+            tanh = jnp.tanh(GELU_A * pre * (1.0 + GELU_B * square))
+            act = (0.5 * pre * (1.0 + tanh)).astype(BF)
+            slope = 0.5 * (1.0 + tanh) + 0.5 * pre * (1.0 - tanh * tanh) * (
+                GELU_A * (1.0 + 3.0 * GELU_B * square)
+            )
+            grad_act = dot(grad, down, NT).astype(BF).astype(F32)
+            grad_pre = (grad_act * slope).astype(BF)
+            e_acc[rows] += dot(act, down, NN)
+            dh_acc[rows] += dot(grad_pre, up, NN)
+            if piece == 0:
+                down_acc[...] = dot(act, grad, TN)
+                up_acc[...] = dot(grad_pre, hidden, TN)
+            else:
+                down_stage[buf] = (down_acc[...] + dot(act, grad, TN)).astype(BF).reshape(2, TILE, D)
+                up_stage[buf] = (up_acc[...] + dot(grad_pre, hidden, TN)).astype(BF).reshape(2, TILE, D)
+        for copy in stages(block):
+            copy.start()
+        return 0
+
+    lax.fori_loop(0, 8, feed_block, 0)
+    branch_saved.wait()
+
+    def swap_done(i, _):
+        swap_strip(i).wait_send()
+        return 0
+
+    lax.fori_loop(0, CLIP // BLK, swap_done, 0)
+
+    def cast_strip(i, _):
+        strip = pl.ds(pl.multiple_of(i * BLK, BLK), BLK)
+        mine[strip] = e_acc[strip].astype(BF)
+        peer[strip] = dh_acc[strip].astype(BF)
+        return 0
+
+    lax.fori_loop(0, CLIP // BLK, cast_strip, 0)
+    ends = [save(mine, e_out), save(peer, dh_out), x_saved, pack_saved, qkv_saved, o_saved]
+    for block in (6, 7):
+        for copy in stages(block):
+            copy.wait()
+    for copy in ends:
         copy.wait()
     link.drain()
 
 
-def entry(masters, level_table, levels, bias_pair, activations, cotangent, owner_list):
+def front(masters, level_table, levels, bias_pair, activations, cotangent, owner_list):
     slots = masters.shape[0]
     codes = jnp.stack([levels.reshape(-1) // 32, levels.reshape(-1) % 32], axis=1).astype(BF)
     codes = jnp.pad(jnp.repeat(codes, 64, axis=1), ((0, TILE - codes.shape[0]), (0, 0)))
@@ -507,18 +748,31 @@
     ).astype(jnp.int32)
     vmem = pl.BlockSpec(memory_space=pltpu.VMEM)
     hbm = pl.BlockSpec(memory_space=pl.ANY)
+    clip = jax.ShapeDtypeStruct((CLIP, D), BF)
+    chunks = jax.ShapeDtypeStruct((4, 4, TILE, D), BF)
+    thirds = jax.ShapeDtypeStruct((4, CLIP, 3 * TILE), BF)
     return pl.pallas_call(
-        entry_kernel,
+        front_kernel,
         in_specs=[pl.BlockSpec(memory_space=pltpu.SMEM), hbm, hbm, hbm, hbm],
-        out_specs=[hbm] + [vmem] * 8,
+        out_specs=[hbm] * 14 + [vmem] * 5,
         out_shape=[
-            jax.ShapeDtypeStruct((3, 4, 4, TILE, D), BF),
-            jax.ShapeDtypeStruct((D, 12 * TILE), BF),
-            jax.ShapeDtypeStruct((CLIP, D), BF),
-            jax.ShapeDtypeStruct((CLIP, D), BF),
-            jax.ShapeDtypeStruct((CLIP, D), BF),
+            chunks,
+            thirds,
+            clip,
+            clip,
+            clip,
+            jax.ShapeDtypeStruct((4, 4 * TILE, D), BF),
+            thirds,
+            jax.ShapeDtypeStruct((4, TILE, CLIP), BF),
+            clip,
+            jax.ShapeDtypeStruct((CLIP, D), F32),
+            clip,
+            clip,
+            chunks,
+            chunks,
             jax.ShapeDtypeStruct((FRAMES, 6, D), F32),
             jax.ShapeDtypeStruct((FRAMES, CLIP), F32),
+            jax.ShapeDtypeStruct((4, 2, CLIP), F32),
             jax.ShapeDtypeStruct((256, D), BF),
             jax.ShapeDtypeStruct((256, TILE), BF),
         ],
@@ -532,20 +786,35 @@
             pltpu.VMEM((4, FRAMES, 12 * TILE), F32),
             pltpu.VMEM((4, FRAMES, 12 * TILE), F32),
             pltpu.VMEM((256, LEVELS), BF),
+            pltpu.VMEM((CLIP, D), BF),
+            pltpu.VMEM((4, 4 * TILE, D), BF),
+            pltpu.VMEM((4, CLIP, 3 * TILE), BF),
+            pltpu.VMEM((4, TILE, CLIP), BF),
+            pltpu.VMEM((CLIP, D), BF),
+            pltpu.VMEM((CLIP, D), BF),
+            pltpu.VMEM((CLIP, D), F32),
+            pltpu.VMEM((CLIP, D), F32),
+            pltpu.VMEM((2, 4, 4, TILE, D), BF),
+            pltpu.VMEM((2, 2, TILE, D), BF),
+            pltpu.VMEM((2, 2, TILE, D), BF),
+            pltpu.VMEM((2 * TILE, D), F32),
+            pltpu.VMEM((2 * TILE, D), F32),
             pltpu.SemaphoreType.DMA((ENTRY_COPIES,)),
             pltpu.SemaphoreType.DMA((ENTRY_COPIES,)),
             pltpu.SemaphoreType.DMA((3,)),
             pltpu.SemaphoreType.DMA((3,)),
-            pltpu.SemaphoreType.DMA((7,)),
+            pltpu.SemaphoreType.DMA((4,)),
+            pltpu.SemaphoreType.DMA((4,)),
+            pltpu.SemaphoreType.DMA((24,)),
+            pltpu.SemaphoreType.DMA((64,)),
+            pltpu.SemaphoreType.DMA((4,)),
         ],
-        compiler_params=params(collective_id=0, has_side_effects=True),
-        cost_estimate=cost(1e9, 40e6),
-        name="entry",
+        compiler_params=pltpu.CompilerParams(
+            vmem_limit_bytes=63 * 1024 * 1024, collective_id=0, has_side_effects=True
+        ),
+        cost_estimate=cost(1e11, 60e6),
+        name="front",
     )(index, payload, activations, cotangent, bias_pair)
-
-
-QBLK = 256
-SCALE2 = HD ** (-0.5) * LOG2E
 
 
 def attend_kernel(qkv_ref, bias_ref, o_ref, lse_ref):
@@ -647,7 +916,6 @@
 
 
 UNITS = 256
-ROWS = 512
 
 
 def feed_kernel(h_ref, de_ref, up_ref, down_ref, e_ref, dh_ref, dup_ref, ddown_ref, e_acc, dh_acc, up_acc, down_acc):
@@ -813,8 +1081,7 @@
     h_hbm,
     qkv_hbm,
     o_hbm,
-    win_hbm,
-    wout_hbm,
+    wpack_hbm,
     wmod_hbm,
     up_hbm,
     down_hbm,
@@ -883,8 +1150,10 @@
         pl.semaphore_signal(barrier, inc=1, device_id=(dk, lax.rem(z + s, 4)), device_id_type=MESH)
 
     first_loads = [load(a, b) for a, b in ((g_hbm, gs), (e_hbm, es), (y_hbm, ys), (dy_hbm, dys), (br_hbm, brs))]
-    loads = [load(a, b) for a, b in ((o_hbm, os_), (wout_hbm, wout), (win_hbm, win))]
-    loads += [load(qkv_hbm.at[:, m * 384 : (m + 1) * 384], qs.at[m]) for m in range(4)]
+    loads = [load(a, b) for a, b in ((o_hbm, os_), (qkv_hbm, qs))]
+    for m in range(4):
+        loads.append(load(wpack_hbm.at[m, 3 * TILE : 4 * TILE], wout.at[m]))
+        loads.append(load(wpack_hbm.at[m, 0 : 3 * TILE], win.at[m * 3 * TILE : (m + 1) * 3 * TILE]))
     feed_loads = []
     for g, src in enumerate((up_hbm, down_hbm)):
         feed_loads.append(load(src.at[0], loc.at[g, 0:4]))
@@ -1112,7 +1381,7 @@
 
     lax.fori_loop(0, 4, input_weights, 0)
     plane_first(0, dattn)
-    mod_loads = [load(wmod_hbm.at[:, m * 384 : (m + 1) * 384], qs.at[m]) for m in range(4)]
+    mod_loads = [load(wmod_hbm, qs)]
     plane_final(1)
     plane_final(2)
 
@@ -1204,14 +1473,14 @@
     link.drain()
 
 
-def exit_call(y1, dh2, e, dy, branch, x, h1, qkv, o_rows, w_in, w_out, w_mod, d_up, d_down, mods, bias, lse, emb, hot):
+def exit_call(*args):
     vmem = pl.BlockSpec(memory_space=pltpu.VMEM)
     hbm = pl.BlockSpec(memory_space=pl.ANY)
     chunks = (4, 4, TILE, D)
     heads = (4, TILE, D)
     return pl.pallas_call(
         exit_kernel,
-        in_specs=[hbm] * 14 + [vmem] * 5,
+        in_specs=[hbm] * 13 + [vmem] * 5,
         out_specs=[hbm] * 4 + [vmem],
         out_shape=[
             jax.ShapeDtypeStruct((2 * CLIP, D), BF),
@@ -1261,27 +1530,7 @@
         ),
         cost_estimate=cost(1e11, 60e6),
         name="exit",
-    )(
-        y1,
-        dh2,
-        e,
-        dy,
-        branch,
-        x,
-        h1,
-        qkv,
-        o_rows.reshape(heads),
-        w_in,
-        w_out.reshape(heads),
-        w_mod,
-        d_up.reshape(chunks),
-        d_down.reshape(chunks),
-        mods,
-        bias,
-        lse,
-        emb,
-        hot,
-    )
+    )(*args)
 
 
 def adam_step(grad, left, right, one, two, master, rate):
@@ -1492,9 +1741,12 @@
     rows = TILE // chips
     level_ids = jnp.arange(LEVELS, dtype=jnp.int32)[None, :]
     if fast:
-        with jax.named_scope("entry"):
+        with jax.named_scope("front"):
             flagged = context_flags == 1
-            weights, w_mod, x, dy, h1, mods, bias, all_embedded, own_hot = entry(
+            (
+                _, w_mod, x, dy, h1, w_pack, qkv, o_rows, branch, y1, e_part, dh2_part, d_up, d_down,
+                mods, bias, lse, all_embedded, own_hot,
+            ) = front(
                 masters[0],
                 level_table,
                 level_rows(flagged, group_pattern),
@@ -1503,9 +1755,12 @@
                 cotangent,
                 owner_list,
             )
-            got = weights[0].reshape(chips, groups, 4, rows, D)
-            w_up = weights[1].reshape(-1, D)
-            w_down = weights[2].reshape(-1, D)
+        with jax.named_scope("exit"):
+            block_output, input_grad, everyone, d_w_mod, table_grad = exit_call(
+                y1, dh2_part, e_part, dy, branch, x, h1, qkv, o_rows, w_pack, w_mod,
+                d_up, d_down, mods, bias, lse, all_embedded, own_hot,
+            )
+            input_grad = input_grad.astype(F32)
     else:
         with jax.named_scope("entry"):
             holds = (z // local_clips) == core
@@ -1566,28 +1821,21 @@
             )
             (h1,) = row_call(first_norm_kernel, "first_norm", [x], mods, [BF], [], 4 * CLIP * D)
 
-    w_in = got[:, :, :3].transpose(1, 2, 0, 3, 4).reshape(-1, D)
-    w_out = got[:, :, 3].transpose(1, 0, 2, 3).reshape(-1, D)
-
-    mb = CLIP * D
-    with jax.named_scope("attention"):
-        qkv = dot(h1, w_in, NT).astype(BF)
-        o_rows, lse = attend(qkv, bias)
-        part = dot(o_rows, w_out, TN).astype(BF)
-        y1, branch, h2, de = row_call(
-            middle_kernel, "middle", [x, part, across(part), dy], mods, [F32, BF, BF, BF], [], 18 * mb
-        )
-
-    with jax.named_scope("feed"):
-        e_part, dh2_part, d_up, d_down = feed_both(h2, de, w_up, w_down)
-    if fast:
-        with jax.named_scope("exit"):
-            block_output, input_grad, everyone, d_w_mod, table_grad = exit_call(
-                y1, dh2_part, e_part, dy, branch, x, h1, qkv, o_rows, w_in, w_out, w_mod,
-                d_up, d_down, mods, bias, lse, all_embedded, own_hot,
+        w_in = got[:, :, :3].transpose(1, 2, 0, 3, 4).reshape(-1, D)
+        w_out = got[:, :, 3].transpose(1, 0, 2, 3).reshape(-1, D)
+
+        mb = CLIP * D
+        with jax.named_scope("attention"):
+            qkv = dot(h1, w_in, NT).astype(BF)
+            o_rows, lse = attend(qkv, bias)
+            part = dot(o_rows, w_out, TN).astype(BF)
+            y1, branch, h2, de = row_call(
+                middle_kernel, "middle", [x, part, across(part), dy], mods, [F32, BF, BF, BF], [], 18 * mb
             )
-            input_grad = input_grad.astype(F32)
-    else:
+
+        with jax.named_scope("feed"):
+            e_part, dh2_part, d_up, d_down = feed_both(h2, de, w_up, w_down)
+
         with jax.named_scope("feed_back"):
             out, dy1, da, dm_mid = row_call(
                 back_kernel,

time: 578 us -> 503 us (0.87)
  Pallas kernels: 533 us -> 481 us
  local copies, waits for them, and re-layouts: 18.4 us -> 5.15 us
  matrix products: 7.42 us -> 0 us
    pallas_call x5 -> x2, Pallas kernels: 513 us -> 461 us  [the longest x1 232 us: front(): pl.pallas_call(front_kernel, in_specs=[pl.BlockSpec(memory_space=pltpu.SM...]
    slice x3 -> x0, local copies, waits for them, and re-layouts: 8.33 us -> none  [the longest x1 7.7 us: body(): w_down = weights[2].reshape(-1, D)]
    dot_general x2 -> x0, matrix products: 7.42 us -> none  [dot(): lax.dot_general(left, right, (dims, ((), ())), preferred_element_type=F32)]
  transfers between devices with their start and end apart: 1 -> 0, of which waited for: 1 -> 0; matrix products, arithmetic and copies ran while one was open for 0% -> 0% of each run, Pallas kernels for 0% -> 0%
where the time goes in v4:
time: 503 us
  Pallas kernels  481 us (96%)
  other arithmetic  15.2 us (3%)
  local copies, waits for them, and re-layouts  5.15 us (1%)
    pallas_call x1, Pallas kernels, front(): pl.pallas_call(front_kernel, in_specs=[pl.BlockSpec(memory_space=pltpu.SM...  232 us
    pallas_call x1, Pallas kernels, exit_call(): pl.pallas_call(exit_kernel, in_specs=[hbm] * 13 + [vmem] * 5, out_specs=[...  230 us
    pallas_call x1, Pallas kernels, adam(): pl.pallas_call(functools.partial(adam_kernel, picked=picked, batch=batch)...  20.2 us

profile of v4, /device:TPU:1, one launch (start us, length us, event | category | flops | bytes accessed | tf_op | source)
XLA Modules:
  0.0 502.5 jit_solution(13806961990245345063)
XLA Ops:
  0.6 0.8 fusion.23
  1.5 0.1 broadcast_in_dim.183
  1.7 0.8 reshape.414.bias_ref
  2.5 0.7 compare_convert_fusion
  3.2 0.8 multiply_reduce_fusion
  3.9 0.7 broadcast_select_fusion
  4.6 0.1 reshape.412
  4.7 0.1 copy.38
  4.8 0.1 broadcast_in_dim.178
  5.0 0.1 reshape.413
  5.0 1.9 bitcast_convert_fusion
  6.9 0.2 copy.36
  7.1 0.2 copy.37
  7.4 1.4 maximum_maximum_fusion.pay_ref
  8.8 0.7 select_reduce_fusion.idx_ref
  9.5 231.5 %front.1 = (bf16[4,4,128,1024]{3,2,1,0:T(8,128)(2,1)}, bf16[4,1024,384]{2,1,0:T(8,128)(2,1)}, bf16[1024,1024]{1,0:T(8,128)(2,1)}, bf16[1024,1024]{1,0:T(8,128)(2...) custom-call(s32[288]{0:T(512)} %select_reduce_fusion.idx_ref, ...), custom_call_target="tpu_custom_call" | custom-call | flops 99999997952 | bytes 60000000 | tf_op jit(solution)/shard_map/front/front/pallas_call | solution.py:754
  241.0 229.6 %exit.1 = (bf16[2048,1024]{1,0:T(8,128)(2,1)}, bf16[2048,1024]{1,0:T(8,128)(2,1)}, bf16[8,384,1024]{2,1,0:T(8,128)(2,1)}, bf16[1536,1024]{1,0:T(8,128)(2,1)}, f32[32,1024]{1,0:T(8,128)}) custom-call(f32[1024,1024]{1,0:T(8,128)} %get-tuple-element.34.y_hbm, bf16[1024,1024]{1,0:T(8,128)(2,1)} %get-tuple-element.35.g_hbm, ...), custom_call_target="tpu_custom_call" | custom-call | flops 99999997952 | bytes 60000000 | tf_op jit(solution)/shard_map/exit/exit/pallas_call | solution.py:1481
  470.7 1.3 fusion.14
  472.0 0.1 select_select_fusion
  472.2 0.7 copy.39.tab_ref
  472.9 20.2 %adam.1 = (f32[36,128,128]{2,1,0:T(8,128)}, f32[36,128,128]{2,1,0:T(8,128)}, f32[36,128,128]{2,1,0:T(8,128)}, bf16[36,128,128]{2,1,0:T(8,128)(2,1)}) custom-call(s32[36,12]{1,0:T(8,128)} %copy.39.tab_ref, f32[36]{0:T(128)} %get-tuple-element.61.rate_ref, bf16[8,384,1024]{2,1,0:T(8,128)(2,1)} %get-tuple-element.55.refs_0_, ...), custom_call_target="tpu_custom_call" | custom-call | flops 603979776 | bytes 21233664 | tf_op jit(solution)/shard_map/owners/adam/pallas_call | solution.py:1621
  493.1 6.8 %convert_element_type.18 = f32[2048,1024]{1,0:T(8,128)} convert(bf16[2048,1024]{1,0:T(8,128)(2,1)} %get-tuple-element.53) | non-fusion elementwise | flops 2097152 | bytes 12582912 | tf_op jit(solution)/shard_map/exit/convert_element_type | solution.py:1763
  499.9 2.0 copy.42
  501.9 0.7 copy.43
  (19 shorter events, 0.3 us)
Async XLA Ops:
  0.6 6.3 %copy-start.1 = (bf16[128,1024]{1,0:T(8,128)(2,1)S(1)}, bf16[128,1024]{1,0:T(8,128)(2,1)}, u32[]{:S(2)}) copy-start(bf16[128,1024]{1,0:T(8,128)(2,1)} %param.15) | copy-start | bytes 786436
  6.9 1.8 copy-start.3
  493.1 6.8 %copy-start = (bf16[2048,1024]{1,0:T(8,128)(2,1)S(1)}, bf16[2048,1024]{1,0:T(8,128)(2,1)}, u32[]{:S(2)}) copy-start(bf16[2048,1024]{1,0:T(8,128)(2,1)} %get-tuple-element.92) | copy-start | bytes 12582916
  499.9 2.0 copy-start.2

commit v5 on v4

--- a/solution.py
+++ b/solution.py
@@ -471,12 +471,6 @@
     send_along(0)
     send_plane(0, 0)
     homes[0].start()
-    lax.fori_loop(0, 8, pick_feed, 0)
-    send_along(1)
-    send_along(2)
-    send_plane(1, 0)
-    homes[1].start()
-    homes[2].start()
 
     lax.fori_loop(0, 8, pick_mod, 0)
     mod_saved = save(qs, wmod_out)
@@ -497,11 +491,17 @@
     for s in (1, 3, 2):
         shared[s] = link.send(part.at[lax.rem(z + s, 4)], modbuf.at[z], d, lax.rem(z + s, 4))
 
+    lax.fori_loop(0, 8, pick_feed, 0)
+    send_along(1)
+    send_along(2)
+    homes[1].start()
+    homes[2].start()
     for s in (1, 3, 2):
         send_plane(0, s)
-    send_plane(2, 0)
     for s in (0, 1, 3, 2):
         send_diag(0, s)
+    send_plane(1, 0)
+    send_plane(2, 0)
 
     for s in (1, 3, 2):
         shared[s].wait_recv()
@@ -1071,6 +1071,105 @@
             self.home().wait()
 
 
+class Line:
+    def __init__(self, link, own, held, z, d):
+        self.own, self.held, self.z, self.d = own, held, z, d
+        self.sends, self.recvs, self.base = link.sends, link.recvs, link.used
+        link.used += 2
+
+    def copy(self, way, at):
+        if way == 0:
+            src, count = self.own.at[at + 1 : 4], 3 - at
+        else:
+            src, count = self.own.at[0:at], at
+        return pltpu.make_async_remote_copy(
+            src_ref=src,
+            dst_ref=self.held.at[way, 0:count],
+            send_sem=self.sends.at[self.base + way],
+            recv_sem=self.recvs.at[self.base + way],
+            device_id=(self.d, at + (1 if way == 0 else -1)),
+            device_id_type=MESH,
+        )
+
+    def add(self, chunk, way, slot):
+        def step(i, _):
+            rows = pl.ds(pl.multiple_of(i * 32, 32), 32)
+            total = self.own[chunk, rows].astype(F32) + self.held[way, slot, rows].astype(F32)
+            self.own[chunk, rows] = total.astype(BF)
+            return 0
+
+        lax.fori_loop(0, 4, step, 0)
+
+    def start(self):
+        @pl.when(self.z == 0)
+        def _():
+            self.copy(0, 0).start()
+
+        @pl.when(self.z == 3)
+        def _():
+            self.copy(1, 3).start()
+
+    def turn(self):
+        @pl.when(self.z == 1)
+        def _():
+            self.copy(0, 0).wait_recv()
+            self.add(2, 0, 1)
+            self.add(3, 0, 2)
+            self.copy(0, 1).start()
+
+        @pl.when(self.z == 2)
+        def _():
+            self.copy(1, 3).wait_recv()
+            self.add(0, 1, 0)
+            self.add(1, 1, 1)
+            self.copy(1, 2).start()
+
+    def turn_again(self):
+        @pl.when(self.z == 2)
+        def _():
+            self.copy(0, 1).wait_recv()
+            self.add(3, 0, 1)
+            self.copy(0, 2).start()
+
+        @pl.when(self.z == 1)
+        def _():
+            self.copy(1, 2).wait_recv()
+            self.add(0, 1, 0)
+            self.copy(1, 1).start()
+
+    def total(self, out):
+        for at in range(4):
+
+            @pl.when(self.z == at)
+            def _(at=at):
+                if at == 0:
+                    self.copy(1, 1).wait_recv()
+                if at == 3:
+                    self.copy(0, 2).wait_recv()
+
+                def step(i, _):
+                    rows = pl.ds(pl.multiple_of(i * 32, 32), 32)
+                    total = self.own[at, rows].astype(F32)
+                    if at > 0:
+                        total = total + self.held[0, 0, rows].astype(F32)
+                    if at < 3:
+                        total = total + self.held[1, at, rows].astype(F32)
+                    out[rows] = total.astype(BF)
+                    return 0
+
+                lax.fori_loop(0, 4, step, 0)
+
+    def finish(self):
+        for at in range(4):
+
+            @pl.when(self.z == at)
+            def _(at=at):
+                if at < 3:
+                    self.copy(0, at).wait_send()
+                if at > 0:
+                    self.copy(1, at).wait_send()
+
+
 def exit_kernel(
     y_hbm,
     g_hbm,
@@ -1112,6 +1211,7 @@
     got,
     loc,
     zbuf,
+    held,
     red,
     dm,
     dms,
@@ -1218,7 +1318,7 @@
         add_into(high, high_at, 2, [(g, 1)])
         plane[g, 5] = link.send(high.at[pl.ds(high_at, 2)], got.at[g, 5], dx, z)
 
-    column = {}
+    column, lines = {}, {}
 
     def plane_final(g):
         (own, _), _, _ = places(g)
@@ -1226,27 +1326,34 @@
             plane[g, slot].wait_recv()
         add_into(own, 0, 2, [(g, 2), (g, 4)])
         add_into(own, 2, 2, [(g, 3), (g, 5)])
+        if g:
+            lines[g] = Line(link, own, held.at[g - 1], z, d)
+            lines[g].start()
+            return
         for s in (1, 3, 2):
             to = lax.rem(z + s, 4)
-            column[g, s] = link.send(own.at[to], zbuf.at[g, s - 1], d, to)
+            column[s] = link.send(own.at[to], zbuf.at[s - 1], d, to)
 
     spread = {}
     homes = []
 
     def column_final(g):
         (own, _), _, _ = places(g)
-        for s in (1, 3, 2):
-            column[g, s].wait_recv()
 
         def step(i, _):
             rows = pl.ds(pl.multiple_of(i * 32, 32), 32)
             total = own[z, rows].astype(F32)
             for s in range(3):
-                total = total + zbuf[g, s, rows].astype(F32)
+                total = total + zbuf[s, rows].astype(F32)
             red[g, rows] = total.astype(BF)
             return 0
 
-        lax.fori_loop(0, 4, step, 0)
+        if g:
+            lines[g].total(red.at[g])
+        else:
+            for s in (1, 3, 2):
+                column[s].wait_recv()
+            lax.fori_loop(0, 4, step, 0)
         rows = pl.ds(g * TILE, TILE)
         spread[g, 2] = link.send(red.at[g], everyone.at[2, rows], dx, z)
         spread[g, 4] = link.send(red.at[g], everyone.at[4, rows], dyd, z)
@@ -1354,9 +1461,10 @@
     for copy in feed_loads:
         copy.wait()
     plane_pass(1)
+    output.hop(1)
     lax.fori_loop(2, 4, attend_group, 0)
     plane_pass(2)
-    output.hop(1)
+    plane_final(1)
 
     def hidden_strip(i, _):
         strip = strip_of(i)
@@ -1368,6 +1476,7 @@
 
     lax.fori_loop(0, CLIP // BLK, hidden_strip, 0)
     hidden_swap = link.send(brs, dhp, dk, z)
+    output.hop(2)
     h_load.wait()
     x_load.wait()
 
@@ -1382,8 +1491,8 @@
     lax.fori_loop(0, 4, input_weights, 0)
     plane_first(0, dattn)
     mod_loads = [load(wmod_hbm, qs)]
-    plane_final(1)
     plane_final(2)
+    lines[1].turn()
 
     hidden_swap.wait_recv()
 
@@ -1410,7 +1519,6 @@
     dmall[clip] = dms[z]
     inner = Relay(in_sends, in_recvs, local_sems.at[EXIT_LOCAL - 2], dys, in_all, d, z)
     inner.first()
-    output.hop(2)
 
     for s in (1, 3, 2):
         mod_column[s].wait_recv()
@@ -1421,16 +1529,15 @@
     mod_x = link.send(clips_of(chip), clips_of(chip), dx, z)
     mod_y = link.send(clips_of(chip), clips_of(chip), dyd, z)
     plane_pass(0)
-    column_final(1)
-    column_final(2)
+    lines[2].turn()
+    lines[1].turn_again()
     mod_x.wait_recv()
     over_x = jnp.bitwise_xor(chip, 1)
     mod_xy = link.send(clips_of(over_x), clips_of(over_x), dyd, z)
-    spread_on(1)
-    spread_on(2)
     plane_final(0)
     inner.hop(1)
-    output.hop(3)
+    lines[2].turn_again()
+    column_final(1)
 
     mod_y.wait_recv()
     mod_xy.wait_recv()
@@ -1453,15 +1560,19 @@
             grads[:, part * 256 : (part + 1) * 256], emb_ref[...], TN
         ).astype(BF)
     homes.append(load(win, dwm_out))
+    column_final(2)
+    spread_on(1)
+    inner.hop(2)
+    column_final(0)
+    spread_on(2)
     spread_diag(1)
     spread_diag(2)
-    column_final(0)
-    inner.hop(2)
     spread_on(0)
     for s in (1, 3, 2):
         table[s].wait_recv()
     table_ref[...] = trow[z] + tbuf[0] + tbuf[1] + tbuf[2]
     spread_diag(0)
+    output.hop(3)
     inner.hop(3)
     for g in range(3):
         for slot in (1, 3, 5, 8):
@@ -1470,6 +1581,8 @@
         copy.wait()
     output.finish()
     inner.finish()
+    lines[1].finish()
+    lines[2].finish()
     link.drain()
 
 
@@ -1506,7 +1619,8 @@
             pltpu.VMEM(chunks, BF),
             pltpu.VMEM((3, 6, 2, TILE, D), BF),
             pltpu.VMEM((2, 8, TILE, D), BF),
-            pltpu.VMEM((3, 3, TILE, D), BF),
+            pltpu.VMEM((3, TILE, D), BF),
+            pltpu.VMEM((2, 2, 3, TILE, D), BF),
             pltpu.VMEM((3, TILE, D), BF),
             pltpu.VMEM((FRAMES, 6, D), F32),
             pltpu.VMEM((4, FRAMES, 12 * TILE), BF),
@@ -1547,8 +1661,9 @@
 
 def adam_kernel(tab_ref, rate_ref, *refs, picked, batch):
     if picked:
-        red_ref, mod_ref = refs[:2]
-        refs = refs[2:]
+        red_ref, mod_ref, wide_ref = refs[:3]
+        refs[-1][...] = wide_ref[...].astype(F32)
+        refs = refs[3:-1]
     else:
         grad_ref = refs[0]
         refs = refs[1:]
@@ -1609,12 +1724,19 @@
 def adam(table, rates, sources, master, one, two, left, right):
     slots = master.shape[0]
     batch = max(b for b in (4, 3, 2, 1) if slots % b == 0)
-    picked = len(sources) == 2
+    picked = len(sources) == 3
     tiles = pl.BlockSpec((batch, TILE, TILE), lambda i, *_: (i, 0, 0))
+    extra = []
     if picked:
+        height = 2 * TILE
+        blocks = sources[2].shape[0] // height
+        assert blocks <= slots // batch
+        wide = pl.BlockSpec((height, D), lambda i, *_: (jnp.minimum(i, blocks - 1), 0))
+        extra = [wide]
         source_specs = [
             pl.BlockSpec(sources[0].shape, lambda i, *_: (0, 0, 0)),
             pl.BlockSpec(sources[1].shape, lambda i, *_: (0, 0)),
+            wide,
         ]
     else:
         source_specs = [tiles]
@@ -1624,9 +1746,11 @@
             num_scalar_prefetch=2,
             grid=(slots // batch,),
             in_specs=source_specs + [tiles] * 5,
-            out_specs=[tiles] * 4,
+            out_specs=[tiles] * 4 + extra,
         ),
-        out_shape=[jax.ShapeDtypeStruct(master.shape, F32)] * 3 + [jax.ShapeDtypeStruct(master.shape, BF)],
+        out_shape=[jax.ShapeDtypeStruct(master.shape, F32)] * 3
+        + [jax.ShapeDtypeStruct(master.shape, BF)]
+        + [jax.ShapeDtypeStruct(s.shape, F32) for s in sources[2:]],
         compiler_params=params(),
         cost_estimate=cost(slots * 8 * TILE**3, slots * TILE * TILE * 36),
         name="adam",
@@ -1760,7 +1884,6 @@
                 y1, dh2_part, e_part, dy, branch, x, h1, qkv, o_rows, w_pack, w_mod,
                 d_up, d_down, mods, bias, lse, all_embedded, own_hot,
             )
-            input_grad = input_grad.astype(F32)
     else:
         with jax.named_scope("entry"):
             holds = (z // local_clips) == core
@@ -1927,7 +2050,7 @@
         rates = kind_rates(tile_ids, counts)
         if fast:
             picks = pick_table(tile_ids, device)
-            sources = [everyone, d_w_mod]
+            sources = [everyone, d_w_mod, input_grad]
         else:
             picks = jnp.zeros((slots, 12), jnp.int32)
             absolute = jnp.take(
@@ -1941,12 +2064,12 @@
             g_in = jnp.concatenate([attn[0].T, attn[1].T, attn[2].T], axis=1)
             packed = pack([g_in, attn[3], up.T, down, d_w_mod])
             sources = [jnp.take(packed, tile_ids, axis=0)]
-        new_masters, new_one, new_two, new_weights = adam(
+        new_masters, new_one, new_two, new_weights, *wide = adam(
             picks, rates, sources, masters[0], moment_one[0], moment_two[0], basis_left[0], basis_right[0]
         )
     return (
         block_output,
-        input_grad,
+        wide[0] if fast else input_grad,
         table_grad,
         new_masters[None],
         new_one[None],

time: 503 us -> 450 us (0.89)
  Pallas kernels: 481 us -> 432 us
  other arithmetic: 15.2 us -> 8.46 us
    pallas_call x1, Pallas kernels: 230 us -> 202 us  [exit_call(): pl.pallas_call(exit_kernel, in_specs=[hbm] * 13 + [vmem] * 5, out_specs=[...]
    pallas_call x1, Pallas kernels: 232 us -> 209 us  [front(): pl.pallas_call(front_kernel, in_specs=[pl.BlockSpec(memory_space=pltpu.SM...]
    convert_element_type x1 -> x0, other arithmetic: 6.79 us -> none  [body(): input_grad = input_grad.astype(F32)]
where the time goes in v5:
time: 450 us; the launch traced here: 449 us
  Pallas kernels  432 us (96%)
  other arithmetic  8.46 us (2%)
  local copies, waits for them, and re-layouts  7.81 us (2%)
    pallas_call x1, Pallas kernels, front(): pl.pallas_call(front_kernel, in_specs=[pl.BlockSpec(memory_space=pltpu.SM...  209 us
    pallas_call x1, Pallas kernels, exit_call(): pl.pallas_call(exit_kernel, in_specs=[hbm] * 13 + [vmem] * 5, out_specs=[...  202 us
    pallas_call x1, Pallas kernels, adam(): pl.pallas_call(functools.partial(adam_kernel, picked=picked, batch=batch)...  22 us

profile of v5, /device:TPU:1, one launch (start us, length us, event | category | flops | bytes accessed | tf_op | source)
XLA Modules:
  0.0 449.4 jit_solution(12557546339057406431)
XLA Ops:
  0.6 0.8 fusion.23
  1.5 0.1 and_select_fusion
  1.5 0.1 broadcast_in_dim.183
  1.7 0.8 reshape.414.bias_ref
  2.5 0.7 compare_convert_fusion
  3.2 0.8 multiply_reduce_fusion
  3.9 0.7 broadcast_select_fusion
  4.6 0.1 reshape.412
  4.7 0.1 copy.38
  4.8 0.1 broadcast_in_dim.178
  5.0 0.1 reshape.413
  5.0 1.9 bitcast_convert_fusion
  6.9 0.2 copy.36
  7.1 0.2 copy.37
  7.4 1.4 maximum_maximum_fusion.pay_ref
  8.8 0.7 select_reduce_fusion.idx_ref
  9.5 208.7 %front.1 = (bf16[4,4,128,1024]{3,2,1,0:T(8,128)(2,1)}, bf16[4,1024,384]{2,1,0:T(8,128)(2,1)}, bf16[1024,1024]{1,0:T(8,128)(2,1)}, bf16[1024,1024]{1,0:T(8,128)(2...) custom-call(s32[288]{0:T(512)} %select_reduce_fusion.idx_ref, ...), custom_call_target="tpu_custom_call" | custom-call | flops 99999997952 | bytes 60000000 | tf_op jit(solution)/shard_map/front/front/pallas_call | solution.py:754
  218.2 201.7 %exit.1 = (bf16[2048,1024]{1,0:T(8,128)(2,1)}, bf16[2048,1024]{1,0:T(8,128)(2,1)}, bf16[8,384,1024]{2,1,0:T(8,128)(2,1)}, bf16[1536,1024]{1,0:T(8,128)(2,1)}, f32[32,1024]{1,0:T(8,128)}) custom-call(f32[1024,1024]{1,0:T(8,128)} %get-tuple-element.35.y_hbm, bf16[1024,1024]{1,0:T(8,128)(2,1)} %get-tuple-element.36.g_hbm, ...), custom_call_target="tpu_custom_call" | custom-call | flops 99999997952 | bytes 60000000 | tf_op jit(solution)/shard_map/exit/exit/pallas_call | solution.py:1594
  419.9 1.3 fusion.14
  421.3 0.1 select_select_fusion
  421.4 0.7 copy.39.tab_ref
  422.1 22.0 %adam.1 = (f32[36,128,128]{2,1,0:T(8,128)}, f32[36,128,128]{2,1,0:T(8,128)}, f32[36,128,128]{2,1,0:T(8,128)}, bf16[36,128,128]{2,1,0:T(8,128)(2,1)}, f32[2048,1024]{1,0:T(8,128)}) custom-call(s32[36,12]{1,0:T(8,128)} %copy.39.tab_ref, f32[36]{0:T(128)} %get-tuple-element.63.rate_ref, bf16[8,384,1024]{2,1,0:T(8,128)(2,1)} %get-tuple-element.54.refs_0_, ...), custom_call_target="tpu_custom_call" | custom-call | flops 603979776 | bytes 21233664 | tf_op jit(solution)/shard_map/owners/adam/pallas_call | solution.py:1743
  444.1 4.7 %copy.42 = bf16[2048,1024]{1,0:T(8,128)(2,1)} copy(bf16[2048,1024]{1,0:T(8,128)(2,1)} %get-tuple-element.94) | data formatting | bytes 8388608
  448.8 0.7 copy.43
  (16 shorter events, 0.2 us)
Async XLA Ops:
  0.6 6.3 %copy-start = (bf16[128,1024]{1,0:T(8,128)(2,1)S(1)}, bf16[128,1024]{1,0:T(8,128)(2,1)}, u32[]{:S(2)}) copy-start(bf16[128,1024]{1,0:T(8,128)(2,1)} %param.15) | copy-start | bytes 786436
  6.9 1.8 copy-start.2
  444.1 4.7 %copy-start.1 = (f32[32,1024]{1,0:T(8,128)S(1)}, f32[32,1024]{1,0:T(8,128)}, u32[]{:S(2)}) copy-start(f32[32,1024]{1,0:T(8,128)} %get-tuple-element.96) | copy-start | bytes 393220

commit v6 on v5

--- a/solution.py
+++ b/solution.py
@@ -582,13 +582,12 @@
             send_diag(1, 2)
             send_diag(2, 0)
 
-        for head in range(2):
-            lanes = slice(head * HD, (head + 1) * HD)
-            keys = qs[m, :, TILE + head * HD : TILE + (head + 1) * HD]
-            values = qs[m, :, 2 * TILE + head * HD : 2 * TILE + (head + 1) * HD]
-
-            def step(i, _, lanes=lanes, keys=keys, values=values, head=head):
-                across = pl.ds(pl.multiple_of(i * QBLK, QBLK), QBLK)
+        def step(i, _):
+            across = pl.ds(pl.multiple_of(i * QBLK, QBLK), QBLK)
+            for head in range(2):
+                lanes = slice(head * HD, (head + 1) * HD)
+                keys = qs[m, :, TILE + head * HD : TILE + (head + 1) * HD]
+                values = qs[m, :, 2 * TILE + head * HD : 2 * TILE + (head + 1) * HD]
                 queries = qs[m, across, lanes]
                 scores = dot(keys, queries, NT).reshape(FRAMES, FRAME_TOK, QBLK)
                 scores = scores * SCALE2 + bs[:, across][:, None, :]
@@ -598,9 +597,9 @@
                 mixed = dot(values, weights.reshape(CLIP, QBLK).astype(BF), TN)
                 os_[m, lanes, across] = (mixed / total).astype(BF)
                 lse_ref[m, head : head + 1, across] = peak + jnp.log2(total)
-                return 0
-
-            lax.fori_loop(0, CLIP // QBLK, step, 0)
+            return 0
+
+        lax.fori_loop(0, CLIP // QBLK, step, 0)
         return 0
 
     lax.fori_loop(0, 4, attend_group, 0)
@@ -1264,25 +1263,24 @@
     def strip_of(i):
         return pl.ds(pl.multiple_of(i * BLK, BLK), BLK)
 
-    def swaps(i):
-        return [
-            pltpu.make_async_remote_copy(
-                src_ref=src.at[strip_of(i)],
-                dst_ref=dst.at[strip_of(i)],
-                send_sem=strip_sends.at[2 * i + k],
-                recv_sem=strip_recvs.at[2 * i + k],
-                device_id=(dk, z),
-                device_id_type=MESH,
-            )
-            for k, (src, dst) in enumerate(((g_hbm, gp), (e_hbm, ep)))
-        ]
-
-    def swap_start(i, _):
-        for copy in swaps(i):
-            copy.start()
-        return 0
-
-    lax.fori_loop(0, CLIP // BLK, swap_start, 0)
+    def swap(i, k):
+        src, dst = ((g_hbm, gp), (e_hbm, ep))[k]
+        return pltpu.make_async_remote_copy(
+            src_ref=src.at[strip_of(i)],
+            dst_ref=dst.at[strip_of(i)],
+            send_sem=strip_sends.at[2 * i + k],
+            recv_sem=strip_recvs.at[2 * i + k],
+            device_id=(dk, z),
+            device_id_type=MESH,
+        )
+
+    for k in (1, 0):
+
+        def swap_start(i, _, k=k):
+            swap(i, k).start()
+            return 0
+
+        lax.fori_loop(0, CLIP // BLK, swap_start, 0)
 
     plane = {}
 
@@ -1381,20 +1379,29 @@
     for copy in first_loads:
         copy.wait()
 
+    def out_strip(i, _):
+        strip, frames = strip_of(i), pl.ds(i * FBLK, FBLK)
+        swap(i, 1).wait_recv()
+        mods = mods_ref[frames]
+        feed = es[strip].astype(F32) + ep[strip].astype(F32)
+        dm[frames, 5] = jnp.sum(frames_of(dys[strip].astype(F32) * feed), axis=1)
+        ep[strip] = (ys[strip] + flat(mods[:, 5:6] * frames_of(feed))).astype(BF)
+        return 0
+
+    lax.fori_loop(0, CLIP // BLK, out_strip, 0)
+    output = Relay(out_sends, out_recvs, local_sems.at[EXIT_LOCAL - 1], ep, out_all, d, z)
+    output.first()
+
     def back_strip(i, _):
         strip, frames = strip_of(i), pl.ds(i * FBLK, FBLK)
-        for copy in swaps(i):
-            copy.wait_recv()
+        swap(i, 0).wait_recv()
         mods = mods_ref[frames]
         mid = ys[strip]
-        feed = es[strip].astype(F32) + ep[strip].astype(F32)
         dy = dys[strip].astype(F32)
-        ep[strip] = (mid + flat(mods[:, 5:6] * frames_of(feed))).astype(BF)
         normed, inverse_std = norm_rows(mid)
         grad = gs[strip].astype(F32) + gp[strip].astype(F32)
         dm[frames, 3] = jnp.sum(frames_of(grad), axis=1)
         dm[frames, 4] = jnp.sum(frames_of(grad * normed), axis=1)
-        dm[frames, 5] = jnp.sum(frames_of(dy * feed), axis=1)
         scaled = flat(frames_of(grad) * (1.0 + mods[:, 4:5]))
         dy1 = dy + norm_back(scaled, normed, inverse_std)
         ys[strip] = dy1
@@ -1405,15 +1412,13 @@
     lax.fori_loop(0, CLIP // BLK, back_strip, 0)
 
     def swap_done(i, _):
-        for copy in swaps(i):
-            copy.wait_send()
+        for k in range(2):
+            swap(i, k).wait_send()
         return 0
 
     lax.fori_loop(0, CLIP // BLK, swap_done, 0)
     x_load = load(x_hbm, gs)
     h_load = load(h_hbm, es)
-    output = Relay(out_sends, out_recvs, local_sems.at[EXIT_LOCAL - 1], ep, out_all, d, z)
-    output.first()
     for copy in loads:
         copy.wait()
 
@@ -1647,29 +1652,37 @@
     )(*args)
 
 
-def adam_step(grad, left, right, one, two, master, rate):
-    low_left, low_right = left.astype(BF), right.astype(BF)
-    turned = dot(low_left, grad.astype(BF), TN)
-    rotated = dot(turned.astype(BF), low_right, NN)
-    new_one = BETA_ONE * one + (1.0 - BETA_ONE) * rotated
-    new_two = BETA_TWO * two + (1.0 - BETA_TWO) * rotated * rotated
-    direction = new_one / (jnp.sqrt(new_two) + EPS_ADAM)
-    back = dot(low_left, direction.astype(BF), NN)
-    back = dot(back.astype(BF), low_right, NT)
-    return master - rate * (back + DECAY * master), new_one, new_two
+def adam_steps(grads, lefts, rights, ones, twos, masters, rates):
+    lefts = [left.astype(BF) for left in lefts]
+    rights = [right.astype(BF) for right in rights]
+    turned = [dot(left, grad.astype(BF), TN).astype(BF) for left, grad in zip(lefts, grads)]
+    rotated = [dot(turn, right, NN) for turn, right in zip(turned, rights)]
+    new_ones = [BETA_ONE * one + (1.0 - BETA_ONE) * r for one, r in zip(ones, rotated)]
+    new_twos = [BETA_TWO * two + (1.0 - BETA_TWO) * r * r for two, r in zip(twos, rotated)]
+    ways = [(one / (jnp.sqrt(two) + EPS_ADAM)).astype(BF) for one, two in zip(new_ones, new_twos)]
+    backs = [dot(left, way, NN).astype(BF) for left, way in zip(lefts, ways)]
+    backs = [dot(back, right, NT) for back, right in zip(backs, rights)]
+    return (
+        [m - rate * (back + DECAY * m) for m, back, rate in zip(masters, backs, rates)],
+        new_ones,
+        new_twos,
+    )
 
 
 def adam_kernel(tab_ref, rate_ref, *refs, picked, batch):
     if picked:
-        red_ref, mod_ref, wide_ref = refs[:3]
-        refs[-1][...] = wide_ref[...].astype(F32)
-        refs = refs[3:-1]
+        red_ref, mod_ref, wide_ref, same_ref = refs[:4]
+        refs[-2][...] = wide_ref[...].astype(F32)
+        refs[-1][...] = same_ref[...]
+        refs = refs[4:-2]
     else:
         grad_ref = refs[0]
         refs = refs[1:]
     master_ref, one_ref, two_ref, left_ref, right_ref, nm_ref, n1_ref, n2_ref, nw_ref = refs
+    grads, rates = [], []
     for slot in range(batch):
         tile = pl.program_id(0) * batch + slot
+        rates.append(rate_ref[tile])
         if picked:
             col = pl.multiple_of(tab_ref[tile, 8] * TILE, TILE)
             pieces = [
@@ -1680,21 +1693,29 @@
                 ]
                 for i in range(4)
             ]
-            grad = jnp.concatenate(pieces, axis=0).astype(F32)
+            grad = jnp.concatenate(pieces, axis=0)
             mod_row = pl.multiple_of(tab_ref[tile, 9] * TILE, TILE)
             mod_col = pl.multiple_of(tab_ref[tile, 10] * TILE, TILE)
-            mod_grad = mod_ref[pl.ds(mod_col, TILE), pl.ds(mod_row, TILE)].astype(F32)
+            mod_grad = mod_ref[pl.ds(mod_col, TILE), pl.ds(mod_row, TILE)]
             kind = tab_ref[tile, 11]
-            grad = jnp.where(kind == 0, grad, jnp.where(kind == 2, mod_grad, grad).T)
+            grads.append(jnp.where(kind == 0, grad, jnp.where(kind == 2, mod_grad, grad).T))
         else:
-            grad = grad_ref[slot].astype(F32)
-        master, one, two = adam_step(
-            grad, left_ref[slot], right_ref[slot], one_ref[slot], two_ref[slot], master_ref[slot], rate_ref[tile]
-        )
-        nm_ref[slot] = master
-        n1_ref[slot] = one
-        n2_ref[slot] = two
-        nw_ref[slot] = master.astype(BF)
+            grads.append(grad_ref[slot])
+    slots = range(batch)
+    new_masters, new_ones, new_twos = adam_steps(
+        grads,
+        [left_ref[slot] for slot in slots],
+        [right_ref[slot] for slot in slots],
+        [one_ref[slot] for slot in slots],
+        [two_ref[slot] for slot in slots],
+        [master_ref[slot] for slot in slots],
+        rates,
+    )
+    for slot in slots:
+        nm_ref[slot] = new_masters[slot]
+        n1_ref[slot] = new_ones[slot]
+        n2_ref[slot] = new_twos[slot]
+        nw_ref[slot] = new_masters[slot].astype(BF)
 
 
 def pick_table(tiles, device):
@@ -1723,19 +1744,20 @@
 
 def adam(table, rates, sources, master, one, two, left, right):
     slots = master.shape[0]
-    batch = max(b for b in (4, 3, 2, 1) if slots % b == 0)
-    picked = len(sources) == 3
+    batch = max(b for b in (6, 4, 3, 2, 1) if slots % b == 0)
+    picked = len(sources) == 4
     tiles = pl.BlockSpec((batch, TILE, TILE), lambda i, *_: (i, 0, 0))
     extra = []
     if picked:
-        height = 2 * TILE
+        height = 4 * TILE
         blocks = sources[2].shape[0] // height
         assert blocks <= slots // batch
         wide = pl.BlockSpec((height, D), lambda i, *_: (jnp.minimum(i, blocks - 1), 0))
-        extra = [wide]
+        extra = [wide, wide]
         source_specs = [
             pl.BlockSpec(sources[0].shape, lambda i, *_: (0, 0, 0)),
             pl.BlockSpec(sources[1].shape, lambda i, *_: (0, 0)),
+            wide,
             wide,
         ]
     else:
@@ -1750,7 +1772,7 @@
         ),
         out_shape=[jax.ShapeDtypeStruct(master.shape, F32)] * 3
         + [jax.ShapeDtypeStruct(master.shape, BF)]
-        + [jax.ShapeDtypeStruct(s.shape, F32) for s in sources[2:]],
+        + [jax.ShapeDtypeStruct(s.shape, t) for s, t in zip(sources[2:], (F32, BF))],
         compiler_params=params(),
         cost_estimate=cost(slots * 8 * TILE**3, slots * TILE * TILE * 36),
         name="adam",
@@ -2050,7 +2072,7 @@
         rates = kind_rates(tile_ids, counts)
         if fast:
             picks = pick_table(tile_ids, device)
-            sources = [everyone, d_w_mod, input_grad]
+            sources = [everyone, d_w_mod, input_grad, block_output]
         else:
             picks = jnp.zeros((slots, 12), jnp.int32)
             absolute = jnp.take(
@@ -2068,7 +2090,7 @@
             picks, rates, sources, masters[0], moment_one[0], moment_two[0], basis_left[0], basis_right[0]
         )
     return (
-        block_output,
+        wide[1] if fast else block_output,
         wide[0] if fast else input_grad,
         table_grad,
         new_masters[None],

time: 450 us -> 444 us (0.987)
  local copies, waits for them, and re-layouts: 7.81 us -> 3.14 us
    unnamed x9 -> x8, local copies, waits for them, and re-layouts: 5.51 us -> 0.84 us
where the time goes in v6:
time: 444 us
  Pallas kernels  431 us (97%)
  other arithmetic  8.49 us (2%)
    pallas_call x1, Pallas kernels, front(): pl.pallas_call(front_kernel, in_specs=[pl.BlockSpec(memory_space=pltpu.SM...  209 us
    pallas_call x1, Pallas kernels, exit_call(): pl.pallas_call(exit_kernel, in_specs=[hbm] * 13 + [vmem] * 5, out_specs=[...  202 us
    pallas_call x1, Pallas kernels, adam(): pl.pallas_call(functools.partial(adam_kernel, picked=picked, batch=batch)...  20.8 us

profile of v6, /device:TPU:1, one launch (start us, length us, event | category | flops | bytes accessed | tf_op | source)
XLA Modules:
  0.0 443.6 jit_solution(15059957375537348250)
XLA Ops:
  0.6 0.8 fusion.23
  1.5 0.1 and_select_fusion
  1.5 0.1 broadcast_in_dim.199
  1.7 0.8 reshape.414.bias_ref
  2.5 0.7 compare_convert_fusion
  3.2 0.8 multiply_reduce_fusion
  3.9 0.7 broadcast_select_fusion
  4.6 0.1 reshape.412
  4.7 0.1 copy.38
  4.8 0.1 broadcast_in_dim.194
  5.0 0.1 reshape.413
  5.0 1.9 bitcast_convert_fusion
  6.9 0.2 copy.36
  7.1 0.2 copy.37
  7.3 0.1 pad.8.clone
  7.4 1.4 maximum_maximum_fusion.pay_ref
  8.8 0.7 select_reduce_fusion.idx_ref
  9.5 208.7 %front.1 = (bf16[4,4,128,1024]{3,2,1,0:T(8,128)(2,1)}, bf16[4,1024,384]{2,1,0:T(8,128)(2,1)}, bf16[1024,1024]{1,0:T(8,128)(2,1)}, bf16[1024,1024]{1,0:T(8,128)(2...) custom-call(s32[288]{0:T(512)} %select_reduce_fusion.idx_ref, ...), custom_call_target="tpu_custom_call" | custom-call | flops 99999997952 | bytes 60000000 | tf_op jit(solution)/shard_map/front/front/pallas_call | solution.py:753
  218.2 201.7 %exit.1 = (bf16[2048,1024]{1,0:T(8,128)(2,1)}, bf16[2048,1024]{1,0:T(8,128)(2,1)}, bf16[8,384,1024]{2,1,0:T(8,128)(2,1)}, bf16[1536,1024]{1,0:T(8,128)(2,1)}, f32[32,1024]{1,0:T(8,128)}) custom-call(f32[1024,1024]{1,0:T(8,128)} %get-tuple-element.36.y_hbm, bf16[1024,1024]{1,0:T(8,128)(2,1)} %get-tuple-element.37.g_hbm, ...), custom_call_target="tpu_custom_call" | custom-call | flops 99999997952 | bytes 60000000 | tf_op jit(solution)/shard_map/exit/exit/pallas_call | solution.py:1599
  419.9 1.3 fusion.14
  421.3 0.1 select_select_fusion
  421.4 0.7 copy.39.tab_ref
  422.1 20.8 %adam.1 = (f32[36,128,128]{2,1,0:T(8,128)}, f32[36,128,128]{2,1,0:T(8,128)}, f32[36,128,128]{2,1,0:T(8,128)}, bf16[36,128,128]{2,1,0:T(8,128)(2,1)}, f32[2048,1024]{1,0:T(8,128)}, /*index=5*/bf16[2048,1024]{1,0:T(8,128)(2,1)}) custom-call(s32[36,12]{1,0:T(8,128)} %copy.39.tab_ref, f32[36]{0:T(128)} %get-tuple-element.67.rate_ref, ...), custom_call_target="tpu_custom_call" | custom-call | flops 603979776 | bytes 21233664 | tf_op jit(solution)/shard_map/owners/adam/pallas_call | solution.py:1765
  443.0 0.7 copy.41
  (15 shorter events, 0.2 us)
Async XLA Ops:
  0.6 6.3 %copy-start = (bf16[128,1024]{1,0:T(8,128)(2,1)S(1)}, bf16[128,1024]{1,0:T(8,128)(2,1)}, u32[]{:S(2)}) copy-start(bf16[128,1024]{1,0:T(8,128)(2,1)} %param.15) | copy-start | bytes 786436
  6.9 1.8 copy-start.2
  422.1 20.8 %copy-start.1 = (f32[32,1024]{1,0:T(8,128)S(1)}, f32[32,1024]{1,0:T(8,128)}, u32[]{:S(2)}) copy-start(f32[32,1024]{1,0:T(8,128)} %get-tuple-element.98) | copy-start | bytes 393220

commit v7 on v6

--- a/solution.py
+++ b/solution.py
@@ -518,6 +518,7 @@
 
     lax.fori_loop(0, CLIP // BLK, norm_strip, 0)
     h_saved = save(hs, h_out)
+    e_acc[...] = jnp.zeros_like(e_acc)
 
     def late(g, p):
         for s in (0, 1, 3, 2):
@@ -648,7 +649,6 @@
     branch_saved = save(peer, branch_out)
     send_diag(2, 3)
     send_diag(2, 2)
-    e_acc[...] = jnp.zeros_like(e_acc)
     y_saved.wait()
     dh_acc[...] = jnp.zeros_like(dh_acc)
     homes[1].wait()
@@ -1432,6 +1432,10 @@
     lax.fori_loop(0, 4, project, 0)
 
     def attend_group(m, _):
+        @pl.when(m == 1)
+        def _():
+            output.hop(1)
+
         for head in range(2):
             lanes = slice(head * HD, (head + 1) * HD)
             keys = qs[m, :, TILE + head * HD : TILE + (head + 1) * HD]
@@ -1466,10 +1470,10 @@
     for copy in feed_loads:
         copy.wait()
     plane_pass(1)
-    output.hop(1)
     lax.fori_loop(2, 4, attend_group, 0)
     plane_pass(2)
     plane_final(1)
+    output.hop(2)
 
     def hidden_strip(i, _):
         strip = strip_of(i)
@@ -1481,7 +1485,6 @@
 
     lax.fori_loop(0, CLIP // BLK, hidden_strip, 0)
     hidden_swap = link.send(brs, dhp, dk, z)
-    output.hop(2)
     h_load.wait()
     x_load.wait()
 
@@ -1744,7 +1747,7 @@
 
 def adam(table, rates, sources, master, one, two, left, right):
     slots = master.shape[0]
-    batch = max(b for b in (6, 4, 3, 2, 1) if slots % b == 0)
+    batch = max(b for b in (9, 6, 4, 3, 2, 1) if slots % b == 0)
     picked = len(sources) == 4
     tiles = pl.BlockSpec((batch, TILE, TILE), lambda i, *_: (i, 0, 0))
     extra = []

time: 444 us -> 442 us (level)
  no operation moved by 1% of the time
where the time goes in v7:
time: 442 us
  Pallas kernels  429 us (97%)
  other arithmetic  8.49 us (2%)
    pallas_call x1, Pallas kernels, front(): pl.pallas_call(front_kernel, in_specs=[pl.BlockSpec(memory_space=pltpu.SM...  208 us
    pallas_call x1, Pallas kernels, exit_call(): pl.pallas_call(exit_kernel, in_specs=[hbm] * 13 + [vmem] * 5, out_specs=[...  202 us
    pallas_call x1, Pallas kernels, adam(): pl.pallas_call(functools.partial(adam_kernel, picked=picked, batch=batch)...  19 us

profile of v7, /device:TPU:1, one launch (start us, length us, event | category | flops | bytes accessed | tf_op | source)
XLA Modules:
  0.0 441.6 jit_solution(1257060145552174480)
XLA Ops:
  0.6 0.8 fusion.23
  1.5 0.1 and_select_fusion
  1.5 0.1 broadcast_in_dim.199
  1.7 0.8 reshape.414.bias_ref
  2.5 0.7 compare_convert_fusion
  3.2 0.8 multiply_reduce_fusion
  3.9 0.7 broadcast_select_fusion
  4.6 0.1 reshape.412
  4.7 0.1 copy.38
  4.8 0.1 broadcast_in_dim.194
  5.0 0.1 reshape.413
  5.0 1.9 bitcast_convert_fusion
  6.9 0.2 copy.36
  7.1 0.2 copy.37
  7.3 0.1 pad.8.clone
  7.4 1.4 maximum_maximum_fusion.pay_ref
  8.8 0.7 select_reduce_fusion.idx_ref
  9.5 208.4 %front.1 = (bf16[4,4,128,1024]{3,2,1,0:T(8,128)(2,1)}, bf16[4,1024,384]{2,1,0:T(8,128)(2,1)}, bf16[1024,1024]{1,0:T(8,128)(2,1)}, bf16[1024,1024]{1,0:T(8,128)(2...) custom-call(s32[288]{0:T(512)} %select_reduce_fusion.idx_ref, ...), custom_call_target="tpu_custom_call" | custom-call | flops 99999997952 | bytes 60000000 | tf_op jit(solution)/shard_map/front/front/pallas_call | solution.py:753
  217.9 201.7 %exit.1 = (bf16[2048,1024]{1,0:T(8,128)(2,1)}, bf16[2048,1024]{1,0:T(8,128)(2,1)}, bf16[8,384,1024]{2,1,0:T(8,128)(2,1)}, bf16[1536,1024]{1,0:T(8,128)(2,1)}, f32[32,1024]{1,0:T(8,128)}) custom-call(f32[1024,1024]{1,0:T(8,128)} %get-tuple-element.36.y_hbm, bf16[1024,1024]{1,0:T(8,128)(2,1)} %get-tuple-element.37.g_hbm, ...), custom_call_target="tpu_custom_call" | custom-call | flops 99999997952 | bytes 60000000 | tf_op jit(solution)/shard_map/exit/exit/pallas_call | solution.py:1602
  419.6 1.3 fusion.14
  421.0 0.1 select_select_fusion
  421.1 0.7 copy.39.tab_ref
  421.9 19.0 %adam.1 = (f32[36,128,128]{2,1,0:T(8,128)}, f32[36,128,128]{2,1,0:T(8,128)}, f32[36,128,128]{2,1,0:T(8,128)}, bf16[36,128,128]{2,1,0:T(8,128)(2,1)}, f32[2048,1024]{1,0:T(8,128)}, /*index=5*/bf16[2048,1024]{1,0:T(8,128)(2,1)}) custom-call(s32[36,12]{1,0:T(8,128)} %copy.39.tab_ref, f32[36]{0:T(128)} %get-tuple-element.67.rate_ref, ...), custom_call_target="tpu_custom_call" | custom-call | flops 603979776 | bytes 21233664 | tf_op jit(solution)/shard_map/owners/adam/pallas_call | solution.py:1768
  440.9 0.7 copy.41
  (15 shorter events, 0.2 us)
Async XLA Ops:
  0.6 6.3 %copy-start = (bf16[128,1024]{1,0:T(8,128)(2,1)S(1)}, bf16[128,1024]{1,0:T(8,128)(2,1)}, u32[]{:S(2)}) copy-start(bf16[128,1024]{1,0:T(8,128)(2,1)} %param.15) | copy-start | bytes 786436
  6.9 1.8 copy-start.2
  421.8 19.1 %copy-start.1 = (f32[32,1024]{1,0:T(8,128)S(1)}, f32[32,1024]{1,0:T(8,128)}, u32[]{:S(2)}) copy-start(f32[32,1024]{1,0:T(8,128)} %get-tuple-element.98) | copy-start | bytes 393220
